TPU v7x, 32 devices: a whole 2x2x4 slice. The times are simulated.
32 devices in a mesh: side: 4 (over y, core), batch: 8 (over z, x).
Axes of the slice: x: 2, y: 2, z: 4, core: 2. Of those that a mesh axis runs over, the one named last changes fastest.
Arguments:
- hidden_in: bfloat16 [4, 8, 1024, 512], P('side', 'batch'), may hold values from -6 to 6
- segments: int32 [4, 8, 1024], P('side', 'batch'), may hold values from -1 to 31, as said below
- query_cls: int32 [8, 32], P('batch'), may hold values from 0 to 930, as said below
- passage_cls: int32 [4, 8, 5], P('side', 'batch'), may hold values from 0 to 800, as said below
- pair_passage: int32 [256], P('batch'), may hold values from 0 to 119
- passage_cluster: int32 [120], replicated, may hold values from 0 to 31
- teacher: float32 [256, 120], P('batch'), may hold values from -6 to 6
- query_weight: bfloat16 [512, 512], replicated, may hold values from -0.25 to 0.25
- query_bias: float32 [512], replicated, may hold values from -3 to 3
- key_weight: bfloat16 [512, 512], replicated, may hold values from -0.25 to 0.25
- value_weight: bfloat16 [512, 512], replicated, may hold values from -0.25 to 0.25
- value_bias: float32 [512], replicated, may hold values from -1.75 to 1.75
- out_weight: bfloat16 [512, 512], replicated, may hold values from -1 to 1
- out_bias: float32 [512], replicated, may hold values from -1.75 to 1.75
- first_gain: float32 [512], replicated, may hold values from 0.5 to 1.5
- first_shift: float32 [512], replicated, may hold values from -1.75 to 1.75
- inner_weight: bfloat16 [512, 2048], replicated, may hold values from -0.25 to 0.25
- inner_bias: float32 [2048], replicated, may hold values from -3 to 3
- outer_weight: bfloat16 [2048, 512], replicated, may hold values from -0.125 to 0.125
- outer_bias: float32 [512], replicated, may hold values from -1.75 to 1.75
- second_gain: float32 [512], replicated, may hold values from 0.5 to 1.5
- second_shift: float32 [512], replicated, may hold values from -1.75 to 1.75
Outputs:
- loss: float32 [], replicated
- rows_out: bfloat16 [4, 8, 1024, 512], P('side', 'batch')
- input_grad: bfloat16 [4, 8, 1024, 512], P('side', 'batch')
- grad_query_weight: float32 [512, 512], replicated
- grad_query_bias: float32 [512], replicated
- grad_key_weight: float32 [512, 512], replicated
- grad_value_weight: float32 [512, 512], replicated
- grad_value_bias: float32 [512], replicated
- grad_out_weight: float32 [512, 512], replicated
- grad_out_bias: float32 [512], replicated
- grad_first_gain: float32 [512], replicated
- grad_first_shift: float32 [512], replicated
- grad_inner_weight: float32 [512, 2048], replicated
- grad_inner_bias: float32 [2048], replicated
- grad_outer_weight: float32 [2048, 512], replicated
- grad_outer_bias: float32 [512], replicated
- grad_second_gain: float32 [512], replicated
- grad_second_shift: float32 [512], replicated
Inputs may be any that keep to these rules, and one draw needn't show every extreme that they name: `segments`: in every row segment numbers start at 0 and never fall; the tokens after the last segment carry -1. A row of the first group holds 32 queries of 8 to 30 tokens, one of exactly 30; a row of another group holds 5 passages of 50 to 200 tokens, one of exactly 200. `query_cls`: the first token of each segment of the first group's row, in order. `passage_cls`: the first token of each passage of the row, in order; in the first group it holds the first 5 query starts, which nothing uses.
All inputs are finite; a program needn't handle non-finite values.
Results may differ from a plain program's by a relative error of at most 0.02.
Values may be sent and summed in bfloat16 or wider, within the bound.
No kernel may reach another device: no remote copies, remote signals or barrier semaphores. Data moves between devices by JAX's collectives and lax.ppermute only.
A program may use at most 192 MiB of HBM per device.

v0:
```python
import functools

import jax
import jax.numpy as jnp
import numpy as np
from jax import lax
from jax.experimental import pallas as pl
from jax.experimental.pallas import tpu as pltpu
from jax.sharding import PartitionSpec as P

HEADS = 8
HD = 64
EPSILON = 1e-05
NEG_FILL = -1e30
BF = jnp.bfloat16
F32 = jnp.float32
CORE_SWAP = [(0, 1), (1, 0), (2, 3), (3, 2)]
CHIP_SWAP = [(0, 2), (2, 0), (1, 3), (3, 1)]
MIB = 1 << 20
VM = pl.BlockSpec(memory_space=pltpu.VMEM)


def dot(left, right, precision=None):
    return jnp.dot(left, right, preferred_element_type=F32, precision=precision)


def dot_t(left, right):
    return lax.dot_general(left, right, (((1,), (1,)), ((), ())), preferred_element_type=F32)


def t_dot(left, right):
    return lax.dot_general(left, right, (((0,), (0,)), ((), ())), preferred_element_type=F32)


def iota(shape, axis):
    return lax.broadcasted_iota(jnp.int32, shape, axis)


def one_hot(rows, cols, row_of_col):
    return jnp.where(iota((rows, cols), 0) == row_of_col, 1.0, 0.0).astype(BF)


def norm_stats(summed):
    centre = jnp.mean(summed, axis=1, keepdims=True)
    deviation = summed - centre
    inverse = lax.rsqrt(jnp.mean(deviation * deviation, axis=1, keepdims=True) + EPSILON)
    return deviation * inverse, inverse


def norm_back(upstream, normed, inverse, gain):
    scaled = upstream * gain
    inner = jnp.mean(scaled, axis=1, keepdims=True)
    cross = jnp.mean(scaled * normed, axis=1, keepdims=True)
    return inverse * (scaled - inner - normed * cross)


def gelu(pre):
    return (0.5 * pre) * (1.0 + lax.erf(pre * (0.5**0.5)))


def gelu_parts(pre):
    phi = 0.5 + 0.5 * lax.erf(pre * (0.5**0.5))
    density = jnp.exp(-0.5 * (pre * pre)) * 0.3989422804014327
    return pre * phi, phi + pre * density


def spread_heads(rows):
    head = iota((1, rows.shape[1]), 1) // HD
    return jnp.concatenate(
        [jnp.where(head == h, rows, jnp.zeros_like(rows)) for h in range(HEADS)], axis=0
    )


def fold_heads(wide):
    count = wide.shape[0] // HEADS
    head = iota((1, wide.shape[1]), 1) // HD
    total = jnp.zeros((count, wide.shape[1]), wide.dtype)
    for h in range(HEADS):
        total = jnp.where(head == h, wide[h * count : (h + 1) * count], total)
    return total


class Fetched:
    def __init__(self, source, buffer, semaphores, axis=0, parts=1):
        self.buffer, self.shape = buffer, buffer.shape
        self.axis, self.size = axis, buffer.shape[axis] // parts
        self.waiting = {}
        for i in range(parts):
            at = self.place(i) if parts > 1 else (Ellipsis,)
            copy = pltpu.make_async_copy(source.at[at], buffer.at[at], semaphores.at[i])
            copy.start()
            self.waiting[i] = copy

    def place(self, i):
        return (slice(None),) * self.axis + (pl.ds(i * self.size, self.size),)

    def part(self, i):
        if i in self.waiting:
            self.waiting.pop(i).wait()
        return self.buffer[self.place(i)]

    def ref(self):
        for i in sorted(self.waiting):
            self.waiting.pop(i).wait()
        return self.buffer

    def __getitem__(self, index):
        return self.ref()[index]


class Result:
    def __init__(self, buffer, target, semaphores):
        self.buffer, self.target, self.semaphores = buffer, target, semaphores
        self.shape, self.dtype, self.copies = buffer.shape, buffer.dtype, []

    def __setitem__(self, index, value):
        self.buffer[index] = value

    def __getitem__(self, index):
        return self.buffer[index]

    def flush(self, first=None, size=None):
        source, target = self.buffer, self.target
        if first is not None:
            source, target = source.at[pl.ds(first, size)], target.at[pl.ds(first, size)]
        copy = pltpu.make_async_copy(source, target, self.semaphores.at[len(self.copies)])
        copy.start()
        self.copies.append(copy)


PARTS = 4
TOKEN = ((8, 128), F32, False)


def call(kernel, outs, ins, flops=0, scratch=(), limit=8, far=(), smem=(), split=None, after=(), name=None):
    n_in, n_out, n_after = len(ins), len(outs), len(after)
    split = split or {}
    far_in = list(smem) + [i for i in far if i not in smem]
    far_out = [i for i in range(n_out) if not outs[i][2]]
    shapes = [(pltpu.VMEM if near else pltpu.HBM)(s, d) for s, d, near in list(outs) + [TOKEN]]
    moved = sum(x.size * x.dtype.itemsize for x in ins)
    moved += sum(int(np.prod(s)) * jnp.dtype(d).itemsize for s, d, _ in outs)
    ins = [pltpu.with_memory_space_constraint(x, pltpu.HBM) if i in far_in else x for i, x in enumerate(ins)]
    after = [pltpu.with_memory_space_constraint(x, pltpu.HBM) for x in after]

    def wrapped(*refs):
        refs = list(refs)
        in_refs, refs = refs[:n_in], refs[n_in + n_after :]
        out_refs, refs = refs[:n_out], refs[n_out + 1 :]
        in_bufs, refs = refs[: len(far_in)], refs[len(far_in) :]
        out_bufs, refs = refs[: len(far_out)], refs[len(far_out) :]
        if far_in:
            semaphores, refs = refs[0], refs[1:]
            for k, i in enumerate(far_in):
                in_refs[i] = Fetched(in_refs[i], in_bufs[k], semaphores.at[k], *split.get(i, ()))
        if far_out:
            semaphores, refs = refs[0], refs[1:]
            for k, i in enumerate(far_out):
                out_refs[i] = Result(out_bufs[k], out_refs[i], semaphores.at[k])
        kernel(*in_refs, *out_refs, *refs)
        for i in far_in:
            in_refs[i].ref()
        for i in far_out:
            if not out_refs[i].copies:
                out_refs[i].flush()
        for i in far_out:
            for copy in out_refs[i].copies:
                copy.wait()

    hbm = pl.BlockSpec(memory_space=pltpu.HBM)
    spaces = [hbm if i in far_in else VM for i in range(n_in)] + [hbm] * n_after
    out_spaces = [hbm if i in far_out else VM for i in range(n_out)] + [hbm]
    buffers = [(pltpu.SMEM if i in smem else pltpu.VMEM)(ins[i].shape, ins[i].dtype) for i in far_in]
    buffers += [pltpu.VMEM(outs[i][0], outs[i][1]) for i in far_out]
    if far_in:
        buffers.append(pltpu.SemaphoreType.DMA((len(far_in), PARTS)))
    if far_out:
        buffers.append(pltpu.SemaphoreType.DMA((len(far_out), PARTS)))
    return pl.pallas_call(
        wrapped,
        out_shape=shapes,
        in_specs=spaces,
        out_specs=out_spaces,
        scratch_shapes=buffers + list(scratch),
        compiler_params=pltpu.CompilerParams(vmem_limit_bytes=limit * MIB),
        cost_estimate=pl.CostEstimate(
            flops=int(flops), bytes_accessed=int(moved), transcendentals=0
        ),
        name=name,
    )(*ins, *after)


def behind(value, *tokens):
    tokens = [pltpu.with_memory_space_constraint(x, pltpu.HBM) for x in tokens]
    return pl.pallas_call(
        lambda *refs: None,
        out_shape=pltpu.VMEM(value.shape, value.dtype),
        in_specs=[VM] + [pl.BlockSpec(memory_space=pltpu.HBM)] * len(tokens),
        out_specs=VM,
        input_output_aliases={0: 0},
        name="hand_on",
    )(value, *tokens)


class Rows:
    def __init__(self, batch_n, n_query, n_pass, pass_count):
        block = n_query + 3 * n_pass
        block += -block % 16
        self.batch_n, self.n_query, self.n_pass, self.block = batch_n, n_query, n_pass, block
        self.half = block // 2
        self.columns = pass_count + 1 + -(pass_count + 1) % 128
        self.count = batch_n * block
        self.quarter = block // 4
        self.slot = self.quarter + -self.quarter % 16
        core, batch, rest = np.meshgrid(
            np.arange(2), np.arange(batch_n), np.arange(self.half), indexing="ij"
        )
        place = (core * self.half + rest).reshape(-1)
        batch = batch.reshape(-1)
        self.code = (batch * block + place).astype(np.int32)
        y, peer, spot = np.meshgrid(
            np.arange(2), np.arange(batch_n), np.arange(self.slot), indexing="ij"
        )
        spot = np.where(spot < self.quarter, peer * self.half + y * self.quarter + spot, -1).reshape(-1)
        self.slots = np.concatenate([spot, np.where(spot < 0, -1, spot + batch_n * self.half)])
        self.slots = self.slots.astype(np.int32)
        self.query = np.where(place < n_query, batch * n_query + place, -1).astype(np.int32)
        group, slot = (place - n_query) // n_pass, (place - n_query) % n_pass
        is_pass = (place >= n_query) & (group < 3)
        self.passage = np.where(is_pass, (group * batch_n + batch) * n_pass + slot, -1).astype(np.int32)


def core_chip():
    side = lax.axis_index("side")
    return side % 2, side // 2


def block_source(rows, at):
    core, chip = core_chip()
    n, p = rows.n_query, rows.n_pass
    begin = lambda c, y: jnp.where(y == chip, 0, 2 * n) + jnp.where(c == core, 0, n)
    source = jnp.where(at < n + 3 * p, begin(1, 1) + at - (n + 2 * p), -1)
    source = jnp.where(at < n + 2 * p, begin(0, 1) + at - (n + p), source)
    source = jnp.where(at < n + p, begin(1, 0) + at - n, source)
    return jnp.where(at < n, begin(0, 0) + at, source)


def take_rows(source, parts):
    total = sum(p.shape[0] for p in parts)
    pick = jnp.where(iota((source.shape[0], total), 1) == source, 1.0, 0.0).astype(BF)
    return dot(pick, jnp.concatenate([p[...] for p in parts], axis=0)).astype(BF)


def half_kernel(rows, own_ref, other_ref, far_ref, far_other_ref, *refs):
    core, chip = core_chip()
    n = rows.n_query
    at = iota((rows.half, 1), 0) + core * rows.half
    half = take_rows(block_source(rows, at), (own_ref, other_ref, far_ref, far_other_ref))
    out_ref = refs[-1]
    if len(refs) == 1:
        out_ref[...] = half
        return
    teacher_ref, pair_ref = refs[:2]
    count, told = n // 2, teacher_ref.shape[1]
    mine = jnp.where(core == 0, teacher_ref[:count, :], teacher_ref[count:, :])
    line = iota((count, 1), 0)
    pair = jnp.zeros((count, 1), jnp.int32)
    for i in range(count):
        pair = jnp.where(line == i, pair_ref.ref()[core * count + i], pair)
    pair = jnp.broadcast_to(pair.astype(F32), (count, rows.columns - told))
    mine = jnp.concatenate([mine, pair], axis=1)
    high = mine.astype(BF)
    mid = (mine - high.astype(F32)).astype(BF)
    low = (mine - high.astype(F32) - mid.astype(F32)).astype(BF)
    terms = jnp.concatenate([high, mid, low], axis=1)
    side = out_ref.shape[2] // 2
    terms = jnp.concatenate([terms, jnp.zeros((count, side - terms.shape[1]), BF)], axis=1)
    terms = jnp.concatenate([terms[: count // 2], terms[count // 2 :]], axis=1)
    full = jnp.concatenate([half, terms], axis=0)
    for b in range(rows.batch_n):
        out_ref[b] = full


def near_rows(own, *tokens):
    other = lax.ppermute(own, "side", CORE_SWAP)
    far = lax.ppermute(own, "side", CHIP_SWAP)
    if tokens:
        far = behind(far, *tokens)
    return own, other, far, lax.ppermute(far, "side", CORE_SWAP)


def join_halves(core, mine, theirs):
    return jnp.concatenate(
        [jnp.where(core == 0, mine, theirs), jnp.where(core == 0, theirs, mine)], axis=0
    )


def cls_forward_kernel(
    n_pass, x_ref, seg_ref, query_cls_ref, pass_cls_ref, wq_ref, bq_ref, wk_ref, wv_ref, bv_ref,
    rows_ref, query_ref, pick_ref, key_ref, value_ref, probs_ref,
):
    side = lax.axis_index("side")
    n_query, width = query_ref.shape
    slot = iota((n_query, 1), 0)
    cls = jnp.full((n_query, 1), -1, jnp.int32)
    for i in range(n_query):
        place = jnp.where(side == 0, query_cls_ref.ref()[0, i], pass_cls_ref.ref()[0, 0, i] if i < n_pass else -1)
        cls = jnp.where(slot == i, place, cls)
    pick = iota((n_query, x_ref.shape[0]), 1) == cls
    pick_low = jnp.where(pick, 1.0, 0.0).astype(BF)
    pick_ref[...] = pick_low
    x = x_ref.ref()
    key_ref[...] = dot(x[...], wk_ref[...]).astype(BF)
    key_ref.flush()
    value_ref[...] = (dot(x[...], wv_ref[...]) + bv_ref[...]).astype(BF)
    value_ref.flush()
    seg = seg_ref[0].astype(F32)
    cls_seg = jnp.sum(jnp.where(pick, seg, 0.0), axis=1, keepdims=True)
    tokens = dot(pick_low, x[...]).astype(BF)
    query = (dot(tokens, wq_ref[...]) + bq_ref[...]).astype(BF)
    query_ref[...] = query
    bias = jnp.where(cls_seg == seg, 0.0, NEG_FILL)
    scores = dot_t(spread_heads(query) * BF(HD**-0.5), key_ref[...])
    scores = scores + jnp.concatenate([bias] * HEADS, axis=0)
    expo = jnp.exp(scores - jnp.max(scores, axis=1, keepdims=True))
    probs = expo / jnp.sum(expo, axis=1, keepdims=True)
    probs_ref[...] = probs
    probs_ref.flush()
    rows_ref[:, :width] = fold_heads(dot(probs.astype(BF), value_ref[...])).astype(BF)
    rows_ref[:, width:] = tokens


def middle_kernel(
    rows, pass_count,
    mine_ref, theirs_ref, wo_ref, bo_ref, g1_ref, s1_ref, wi_ref, bi_ref, wu_ref, bu_ref, g2_ref, s2_ref,
    at_ref, value_ref, probs_ref, x_ref, key_ref, query_ref, cluster_ref,
    keep_ref, give_ref, low_ref, context_ref, gown_ref, scores_ref,
    loss_ref, small_ref, inner_bias_ref,
    both_ref, first_ref, active_ref, pre_ref, second_ref, attended_ref, slope_ref, told_ref,
):
    width = wo_ref.shape[0]
    n_queries, n_columns = told_ref.shape
    chunk = wi_ref.size
    side, batch = lax.axis_index("side"), lax.axis_index("batch")
    core = side % 2
    code_at, query_at, pass_at = at_ref[0:1, :], at_ref[1:2, :], at_ref[2:3, :]
    count = rows.n_query // 2
    for half in range(2):
        for b in range(rows.batch_n):
            one = jnp.where(core == half, mine_ref[b], theirs_ref[b])
            first_row = (half * rows.batch_n + b) * rows.half
            both_ref[first_row : first_row + rows.half, :] = one[: rows.half]
            terms = one[rows.half :].astype(F32)
            for part in range(2):
                begin = part * one.shape[1] // 2
                cut = [terms[:, begin + k * n_columns : begin + (k + 1) * n_columns] for k in range(3)]
                row = b * rows.n_query + half * count + part * count // 2
                told_ref[row : row + count // 2, :] = cut[0] + cut[1] + cut[2]
    attended = both_ref[:, width:].astype(F32) + (dot(both_ref[:, :width], wo_ref[...]) + bo_ref[...])
    first_hat, first_inv = norm_stats(attended)
    first = first_hat * g1_ref[...] + s1_ref[...]
    first_low = first.astype(BF)
    first_ref[...] = first_low
    second = first + bu_ref[...]
    for i in range(PARTS):
        c = i * chunk
        pre = dot(first_low, wi_ref.part(i)) + bi_ref[:, c : c + chunk]
        active, slope = gelu_parts(pre)
        active = active.astype(BF)
        active_ref[:, c : c + chunk] = active
        slope_ref[:, c : c + chunk] = slope
        second += dot(active, wu_ref.part(i))
    both_ref.flush()
    first_ref.flush()
    active_ref.flush()
    second_hat, second_inv = norm_stats(second)
    final = (second_hat * g2_ref[...] + s2_ref[...]).astype(BF)

    scale = width ** (-0.5)
    query_pick = one_hot(n_queries, rows.count, query_at)
    pass_pick = one_hot(n_columns, rows.count, pass_at)
    query_vec = dot(query_pick, final).astype(BF)
    pass_vec = dot(pass_pick, final).astype(BF)
    score = dot_t(query_vec, pass_vec) * scale
    column = iota((n_queries, n_columns), 1)
    is_pair = column == told_ref[:, n_columns - 1 :].astype(jnp.int32)
    cluster = jnp.full((1, n_columns), -1.0, F32)
    for j in range(pass_count):
        cluster = jnp.where(column[:1] == j, cluster_ref.ref()[j].astype(F32), cluster)
    query_cluster = jnp.sum(jnp.where(is_pair, cluster, 0.0), axis=1, keepdims=True)
    counted = (cluster == query_cluster) & jnp.logical_not(is_pair) & (column < pass_count)
    pair_score = jnp.sum(jnp.where(is_pair, score, 0.0), axis=1, keepdims=True)
    resid = jnp.where(counted, pair_score - score - told_ref[...], 0.0)
    squares = jnp.sum(jnp.sum(resid * resid, axis=1, keepdims=True), axis=0, keepdims=True)
    pairs = jnp.where(counted, 1.0, 0.0)
    pairs = jnp.sum(jnp.sum(pairs, axis=1, keepdims=True), axis=0, keepdims=True)
    loss_ref[...] = squares / jnp.maximum(pairs, 1.0)
    grad_score = jnp.where(is_pair, jnp.sum(resid, axis=1, keepdims=True), 0.0) - resid
    grad_low = (grad_score * scale).astype(BF)
    grad_rows = dot(t_dot(query_pick, grad_low).astype(BF), pass_pick).astype(BF)
    grad_final = dot(grad_rows, final) + t_dot(grad_rows, final)

    def note(at, value):
        small_ref[at : at + 1, :] = jnp.sum(value, axis=0, keepdims=True)

    grad_second = norm_back(grad_final, second_hat, second_inv, g2_ref[...])
    second_low = grad_second.astype(BF)
    second_ref[...] = second_low
    grad_first = grad_second
    for i in range(PARTS):
        c = i * chunk
        grad_pre = dot_t(second_low, wu_ref.part(i)) * slope_ref[:, c : c + chunk]
        inner_bias_ref[:, c : c + chunk] = jnp.sum(grad_pre, axis=0, keepdims=True)
        pre_low = grad_pre.astype(BF)
        pre_ref[:, c : c + chunk] = pre_low
        grad_first += dot_t(pre_low, wi_ref.part(i))
    pre_ref.flush()
    second_ref.flush()
    grad_attended = norm_back(grad_first, first_hat, first_inv, g1_ref[...])
    attended_low = grad_attended.astype(BF)
    attended_ref[...] = attended_low
    attended_ref.flush()
    grad_context = dot_t(attended_low, wo_ref[...]).astype(BF)
    note(0, grad_final * second_hat)
    note(1, grad_final)
    note(2, grad_second)
    note(3, grad_first * first_hat)
    note(4, grad_first)
    note(5, grad_attended)
    note(6, grad_context.astype(F32))
    small_ref[7:8, :] = jnp.zeros((1, width), F32)


    slot = iota((rows.n_query, 1), 0)
    base = batch * rows.block + jnp.where(side == 0, 0, rows.n_query + rows.n_pass * (side - 1))
    live = slot < jnp.where(side == 0, rows.n_query, rows.n_pass)
    own = (code_at == base + slot) & live
    high = grad_attended.astype(BF)
    rest = (grad_attended - high.astype(F32)).astype(BF)
    own = jnp.where(own, 1.0, 0.0).astype(BF)
    gown_ref[...] = dot(own, high) + dot(own, rest)
    context = dot(own, grad_context).astype(BF)
    context_ref[...] = context
    wide = spread_heads(context)
    probs = probs_ref[...]
    grad_probs = dot_t(wide, value_ref[...])
    row_dot = jnp.sum(probs * grad_probs, axis=1, keepdims=True)
    grad_scores = (probs * (grad_probs - row_dot)).astype(BF)
    scores_ref[...] = grad_scores
    scores_ref.flush()
    query_wide = spread_heads(query_ref[...]) * BF(HD**-0.5)
    x = x_ref.ref()
    key_side = dot(grad_scores, x[...]).astype(BF)
    value_side = dot(probs.astype(BF), x[...]).astype(BF)
    key_part = t_dot(key_side, query_wide)
    value_part = t_dot(value_side, wide)
    keep_ref[...] = jnp.where(core == 0, key_part, value_part)
    give_ref[...] = jnp.where(core == 0, value_part, key_part).astype(BF)
    low_ref[...] = (fold_heads(dot(grad_scores, key_ref[...])) * HD**-0.5).astype(BF)


def input_grad_kernel(
    pick_ref, scores_ref, probs_ref, context_ref, query_ref, low_ref, gown_ref,
    wq_ref, wk_ref, wv_ref, out_ref,
):
    query_wide = spread_heads(query_ref[...]) * BF(HD**-0.5)
    key_low = t_dot(scores_ref[...], query_wide).astype(BF)
    value_low = t_dot(probs_ref[...].astype(BF), spread_heads(context_ref[...])).astype(BF)
    sparse = gown_ref[...] + dot_t(low_ref[...], wq_ref[...])
    high = sparse.astype(BF)
    rest = (sparse - high.astype(F32)).astype(BF)
    pick = pick_ref[...]
    total = dot_t(key_low, wk_ref[...]) + dot_t(value_low, wv_ref[...])
    total += t_dot(jnp.concatenate([pick, pick], axis=0), jnp.concatenate([high, rest], axis=0))
    out_ref[...] = total.astype(BF)


def chip_sum_kernel(keep_ref, got_ref, out_ref):
    out_ref[...] = (keep_ref[...] + got_ref[...].astype(F32)).astype(BF)


def add_parts_kernel(rows, parts_ref, own_ref, other_ref, far_ref, far_other_ref, out_ref):
    core, chip = core_chip()
    peers, size = parts_ref.shape[:2]
    total = parts_ref[0].astype(F32)
    for i in range(1, peers):
        total += parts_ref[i].astype(F32)
    at = iota((rows.slot, 1), 0)
    source = block_source(rows, core * rows.half + chip * rows.quarter + at)
    source = jnp.where(at < rows.quarter, source, -1)
    low = take_rows(source, (own_ref, other_ref, far_ref, far_other_ref))
    total = jnp.concatenate([total.astype(BF), low], axis=0)
    for i in range(peers):
        out_ref[i] = total


def last_kernel(size, mine_ref, theirs_ref, x_ref, key_ref, value_ref, query_ref, bias_ref):
    core, _ = core_chip()
    peers = mine_ref.shape[0]
    step = peers // PARTS
    for i in range(PARTS):
        for j in range(i * step, i * step + step):
            mine, theirs = mine_ref[j, :size].astype(F32), theirs_ref[j, :size].astype(F32)
            key_ref[j * size : j * size + size, :] = jnp.where(core == 0, mine, theirs)
            value_ref[j * size : j * size + size, :] = jnp.where(core == 0, theirs, mine)
        key_ref.flush(i * step * size, step * size)
        value_ref.flush(i * step * size, step * size)
    mine = jnp.concatenate([mine_ref[j, size:] for j in range(peers)], axis=0)
    theirs = jnp.concatenate([theirs_ref[j, size:] for j in range(peers)], axis=0)
    low = join_halves(core, mine, theirs)
    bias_ref[...] = jnp.sum(low.astype(F32), axis=0, keepdims=True)
    part_rows(query_ref, x_ref, low)


def core_groups(batch_n):
    return [[(y * 2 + c) * batch_n + b for y in range(2) for b in range(batch_n)] for c in range(2)]


def exchange(sent, batch_n):
    return lax.all_to_all(
        sent, ("side", "batch"), split_axis=0, concat_axis=0, axis_index_groups=core_groups(batch_n)
    )


def scatter_sum(keep, give, batch_n):
    got = lax.ppermute(give, "side", CORE_SWAP)
    total, token = call(chip_sum_kernel, [(keep.shape, BF, True)], (keep, got), name="chip_sum")
    return exchange(total.reshape(2 * batch_n, keep.shape[0] // (2 * batch_n), keep.shape[1]), batch_n), token


def part_rows(result, left, right):
    size = result.shape[0] // PARTS
    for i in range(PARTS):
        result[i * size : i * size + size, :] = t_dot(left[:, i * size : i * size + size], right)
        result.flush(i * size, size)


def weight_grads_kernel(
    active_ref, second_ref, first_ref, pre_ref, both_ref, attended_ref, slots_ref,
    outer_ref, inner_ref, out_ref, x_ref,
):
    part_rows(outer_ref, active_ref, second_ref[...])
    part_rows(inner_ref, first_ref, pre_ref[...])
    part_rows(out_ref, both_ref, attended_ref[...])
    width = out_ref.shape[0]
    count = both_ref.shape[0]
    pick = one_hot(count, slots_ref.shape[1], slots_ref[...])
    x_ref[...] = t_dot(pick, both_ref[:, width:]).astype(BF)


def column_of(row):
    return jnp.transpose(jnp.broadcast_to(row, (128, row.shape[1])))[:, :1]


def attention_kernel(
    tile, sizes, x_ref, wq_ref, bq_ref, key_ref, value_ref, seg_ref, out_ref, q_scr, bias_scr
):
    count = x_ref.shape[0]
    x, wq, bq, seg = x_ref.ref(), wq_ref.ref(), bq_ref[...], seg_ref[0]
    places = iota((1, count), 1)
    keys, values = key_ref.ref(), value_ref.ref()

    @pl.loop(0, count // tile)
    def _(i):
        row = pl.multiple_of(i * tile, tile)
        q = (dot(x[pl.ds(row, tile), :], wq[...]) + bq).astype(BF)
        q_scr[...] = q * BF(HD**-0.5)
        first = jnp.max(jnp.where(places == row, seg, -2))
        last = jnp.max(jnp.where(places == row + (tile - 1), seg, -2))
        low = jnp.min(jnp.where(seg == first, places, count)) // 128 * 128
        high = jnp.max(jnp.where(seg == last, places, -1)) + 1
        own = seg_ref.ref()[0, :, pl.ds(row, tile)].astype(F32)
        own = column_of(own)
        before = jnp.int32(0)
        for size in sizes:
            start = jnp.minimum(low, count - size)
            fits = (high - start <= size) if size < count else jnp.bool_(True)

            @pl.when(jnp.logical_and(before == 0, fits))
            def _(size=size, start=start):
                at = pl.multiple_of(start, 128)
                near = seg_ref.ref()[0, :, pl.ds(at, size)].astype(F32)
                bias_scr[:, :size] = jnp.where(own == near, 0.0, NEG_FILL)
                half = iota((1, 2 * HD), 1) // HD
                slabs = [slice(h // 2 * 2 * HD, h // 2 * 2 * HD + 2 * HD) for h in range(HEADS)]
                scores = [
                    dot_t(
                        jnp.where(half == h % 2, q_scr[:, slabs[h]], BF(0)),
                        keys[pl.ds(at, size), slabs[h]],
                    )
                    + bias_scr[:, :size]
                    for h in range(HEADS)
                ]
                expos = [jnp.exp(s - jnp.max(s, axis=1, keepdims=True)).astype(BF) for s in scores]
                outs = []
                for h in range(HEADS):
                    ones = jnp.where(half == h % 2, values[pl.ds(at, size), slabs[h]], BF(1))
                    mixed = dot(expos[h], ones)
                    outs.append(mixed / pltpu.roll(mixed, HD, 1))
                for h in range(0, HEADS, 2):
                    out_ref.buffer[pl.ds(row, tile), slabs[h]] = jnp.where(
                        half == 0, outs[h], outs[h + 1]
                    ).astype(BF)

            before = jnp.where(fits, 1, before)


def attention(x, wq, bq, keys, values, seg, after, tile=256):
    t, d = x.shape
    sizes = [s for s in (384, 512, 768) if s < t] + [t]
    return call(
        functools.partial(attention_kernel, tile, sizes),
        [((t, d), BF, False)],
        (x, wq, bq, keys, values, seg),
        flops=8 * 10**9,
        far=range(6),
        limit=20,
        scratch=[pltpu.VMEM((tile, d), BF), pltpu.VMEM((tile, t), F32)],
        after=after,
        name="attention",
    )


def ffn_kernel(
    tile, x_ref, c_ref, wo_ref, bo_ref, g1_ref, s1_ref, wi_ref, bi_ref, wu_ref, bu_ref, g2_ref,
    s2_ref, out_ref,
):
    chunk = wi_ref.size
    for t in range(0, x_ref.shape[0], tile):
        part = slice(t, t + tile)
        attended = x_ref[part, :].astype(F32) + (dot(c_ref[part, :], wo_ref[...]) + bo_ref[...])
        first = norm_stats(attended)[0] * g1_ref[...] + s1_ref[...]
        first_low = first.astype(BF)
        second = first + bu_ref[...]
        for c in range(PARTS):
            pre = dot(first_low, wi_ref.part(c)) + bi_ref[:, c * chunk : c * chunk + chunk]
            second += dot(gelu(pre).astype(BF), wu_ref.part(c))
        out_ref[part, :] = (norm_stats(second)[0] * g2_ref[...] + s2_ref[...]).astype(BF)
        out_ref.flush(t, tile)


def ffn(x, context, weights, after, tile=512):
    return call(
        functools.partial(ffn_kernel, tile),
        [(x.shape, BF, False)],
        (x, context) + weights,
        flops=6 * 10**9,
        far=range(12),
        limit=20,
        split={6: (1, PARTS), 8: (0, PARTS)},
        after=after,
        name="feed_forward",
    )


def middle_large(
    rows, pass_count, core, mine, theirs, told, cluster, wo, bo, g1, s1, wi, bi, wu, bu, g2, s2
):
    width = wo.shape[0]
    both = join_halves(core, mine, theirs)
    attended = both[:, width:].astype(F32) + (dot(both[:, :width], wo) + bo)
    first_hat, first_inv = norm_stats(attended)
    first = first_hat * g1 + s1
    first_low = first.astype(BF)
    active, slope = gelu_parts(dot(first_low, wi) + bi)
    active_low = active.astype(BF)
    second = first + (dot(active_low, wu) + bu)
    second_hat, second_inv = norm_stats(second)
    final = (second_hat * g2 + s2).astype(BF)
    order_q = np.argsort(rows.query, kind="stable")[-rows.batch_n * rows.n_query :]
    order_p = np.argsort(rows.passage, kind="stable")[-pass_count:]
    query_vec, pass_vec = final[order_q], final[order_p]
    scale = width ** (-0.5)
    score = dot_t(query_vec, pass_vec) * scale
    is_pair = iota(score.shape, 1) == told[:, pass_count:].astype(jnp.int32)
    query_cluster = jnp.sum(jnp.where(is_pair, cluster, 0.0), axis=1, keepdims=True)
    counted = (cluster == query_cluster) & jnp.logical_not(is_pair)
    pair_score = jnp.sum(jnp.where(is_pair, score, 0.0), axis=1, keepdims=True)
    resid = jnp.where(counted, pair_score - score - told[:, :pass_count], 0.0)
    loss = jnp.sum(resid * resid) / jnp.maximum(jnp.sum(counted.astype(F32)), 1.0)
    grad_score = jnp.where(is_pair, jnp.sum(resid, axis=1, keepdims=True), 0.0) - resid
    grad_low = (grad_score * scale).astype(BF)
    grad_final = jnp.zeros((rows.count, width), F32)
    grad_final = grad_final.at[order_q].set(dot(grad_low, pass_vec))
    grad_final = grad_final.at[order_p].set(t_dot(grad_low, query_vec))
    grad_second = norm_back(grad_final, second_hat, second_inv, g2)
    second_low = grad_second.astype(BF)
    grad_pre = dot_t(second_low, wu) * slope
    pre_low = grad_pre.astype(BF)
    grad_first = dot_t(pre_low, wi) + grad_second
    grad_attended = norm_back(grad_first, first_hat, first_inv, g1)
    attended_low = grad_attended.astype(BF)
    grad_context = dot_t(attended_low, wo).astype(BF)
    small = jnp.stack(
        [
            jnp.sum(v, axis=0)
            for v in (
                grad_final * second_hat, grad_final, grad_second, grad_first * first_hat,
                grad_first, grad_attended, grad_context.astype(F32),
            )
        ]
    )
    inner_bias = jnp.sum(grad_pre, axis=0, keepdims=True)
    return (
        loss.reshape(1, 1), grad_attended, grad_context, small, inner_bias,
        both, first_low, active_low, pre_low, second_low, attended_low,
    )


def own_large(rows, side, batch, grad_attended, grad_context, tokens, keys, values, cls_query, probs):
    core = side % 2
    slot = jnp.arange(rows.n_query)[:, None]
    base = batch * rows.block + jnp.where(side == 0, 0, rows.n_query + rows.n_pass * (side - 1))
    live = slot < jnp.where(side == 0, rows.n_query, rows.n_pass)
    own = ((rows.code[None, :] == base + slot) & live).astype(F32)
    own_attended = dot(own, grad_attended, lax.Precision.HIGHEST)
    context = dot(own.astype(BF), grad_context).astype(BF)
    wide = spread_heads(context)
    grad_probs = dot_t(wide, values)
    row_dot = jnp.sum(probs * grad_probs, axis=1, keepdims=True)
    grad_scores = (probs * (grad_probs - row_dot)).astype(BF)
    query_wide = spread_heads(cls_query) * BF(HD**-0.5)
    key_part = t_dot(dot(grad_scores, tokens).astype(BF), query_wide)
    value_part = t_dot(dot(probs.astype(BF), tokens).astype(BF), wide)
    keep = jnp.where(core == 0, key_part, value_part)
    give = jnp.where(core == 0, value_part, key_part).astype(BF)
    low = (fold_heads(dot(grad_scores, keys)) * HD**-0.5).astype(BF)
    return keep, give, low, context, own_attended, grad_scores


def middle(rows, pass_count, mine, theirs, kept, weights, cluster, hidden, after):
    width, ff = weights[4].shape
    count = rows.count
    keys, values, cls_query, probs = kept
    at = np.stack([rows.code, rows.query, rows.passage])
    ins = (mine, theirs) + weights + (at, values, probs, hidden, keys, cls_query, cluster)
    outs = [
        ((width, width), F32, True), ((width, width), BF, True), ((rows.n_query, width), BF, True),
        ((rows.n_query, width), BF, False), ((rows.n_query, width), F32, False), (probs.shape, BF, False),
        ((1, 1), F32, False), ((8, width), F32, False), ((1, ff), F32, False),
        ((count, 2 * width), BF, False), ((count, width), BF, False), ((count, ff), BF, False),
        ((count, ff), BF, False), ((count, width), BF, False), ((count, width), BF, False),
    ]
    return call(
        functools.partial(middle_kernel, rows, pass_count),
        outs,
        ins,
        flops=12 * count * width * ff,
        scratch=[
            pltpu.VMEM((count, ff), F32),
            pltpu.VMEM((rows.batch_n * rows.n_query, rows.columns), F32),
        ],
        far=range(2, len(ins)),
        split={6: (1, PARTS), 8: (0, PARTS)},
        smem=(len(ins) - 1,),
        limit=40,
        after=after,
        name="cls_middle",
    )


def body(
    hidden_in,
    segments,
    query_cls,
    passage_cls,
    pair_passage,
    passage_cluster,
    teacher,
    query_weight,
    query_bias,
    key_weight,
    value_weight,
    value_bias,
    out_weight,
    out_bias,
    first_gain,
    first_shift,
    inner_weight,
    inner_bias,
    outer_weight,
    outer_bias,
    second_gain,
    second_shift,
):
    count_tok = hidden_in.shape[2]
    width = hidden_in.shape[3]
    n_query = query_cls.shape[1]
    n_pass = passage_cls.shape[2]
    batch_n = lax.axis_size("batch")
    side = lax.axis_index("side")
    pass_count = teacher.shape[1]
    rows = Rows(batch_n, n_query, n_pass, pass_count)

    hidden = hidden_in.reshape(count_tok, width)

    def vec(v):
        return v.reshape(1, -1)

    weights = (
        out_weight, vec(out_bias), vec(first_gain), vec(first_shift), inner_weight, vec(inner_bias),
        outer_weight, vec(outer_bias), vec(second_gain), vec(second_shift),
    )
    small_case = rows.count <= 512 and 3 * rows.columns <= width and n_query % 32 == 0

    token = ((count_tok, width), BF, False)
    own, cls_query, pick, keys, values, probs, _ = call(
        functools.partial(cls_forward_kernel, n_pass),
        [
            ((n_query, 2 * width), BF, True),
            ((n_query, width), BF, False),
            ((n_query, count_tok), BF, False),
            token,
            token,
            ((HEADS * n_query, count_tok), F32, False),
        ],
        (
            hidden, segments, query_cls, passage_cls, query_weight, vec(query_bias), key_weight,
            value_weight, vec(value_bias),
        ),
        flops=4 * count_tok * width * width,
        far=(0, 6, 1, 4, 5, 7, 8),
        smem=(2, 3),
        limit=20,
        name="cls_forward",
    )

    extra = n_query // 4 if small_case else 0
    near = near_rows(own)
    if small_case:
        sent, half_done = call(
            functools.partial(half_kernel, rows),
            [((batch_n, rows.half + extra, 2 * width), BF, True)],
            near + (teacher, pair_passage),
            far=(4,),
            smem=(5,),
            name="half_rows",
        )
    else:
        half, half_done = call(
            functools.partial(half_kernel, rows),
            [((rows.half, 2 * width), BF, True)],
            near,
            name="half_rows",
        )
        sent = jnp.broadcast_to(half[None], (batch_n,) + half.shape)
    mine = lax.all_to_all(sent, "batch", split_axis=0, concat_axis=0)
    context, attention_done = attention(
        hidden, query_weight, vec(query_bias), keys, values, segments, (half_done,)
    )
    if small_case:
        mine = behind(mine, attention_done)
    theirs = lax.ppermute(mine, "side", CORE_SWAP)

    if small_case:
        kept = (keys, values, cls_query, probs)
        (
            keep, give, query_low, own_context, own_attended, grad_scores, loss, small, grad_inner_bias,
            both, first_low, active_low, pre_low, second_low, attended_low, _,
        ) = middle(
            rows, pass_count, mine, theirs, kept, weights, passage_cluster, hidden, (attention_done,)
        )
    else:
        told = jnp.concatenate([teacher, pair_passage[:, None].astype(F32)], axis=1)
        told = lax.all_to_all(
            jnp.broadcast_to(told[None], (batch_n,) + told.shape), "batch", split_axis=0, concat_axis=0
        ).reshape(batch_n * n_query, pass_count + 1)
        flat = (batch_n * rows.half, 2 * width)
        (
            loss, grad_attended, grad_context, small, grad_inner_bias,
            both, first_low, active_low, pre_low, second_low, attended_low,
        ) = middle_large(
            rows, pass_count, side % 2, mine.reshape(flat), theirs.reshape(flat), told,
            passage_cluster.astype(F32)[None, :], *weights,
        )
        keep, give, query_low, own_context, own_attended, grad_scores = own_large(
            rows, side, lax.axis_index("batch"), grad_attended, grad_context,
            hidden, keys, values, cls_query, probs,
        )

    parts, sum_done = scatter_sum(keep, give, batch_n)
    input_grad, input_done = call(
        input_grad_kernel,
        [(hidden.shape, BF, False)],
        (
            pick, grad_scores, probs, own_context, cls_query, query_low, own_attended, query_weight,
            key_weight, value_weight,
        ),
        flops=6 * count_tok * width * width,
        far=(1, 4, 2, 3, 0, 6, 8, 9, 7),
        limit=20,
        after=(sum_done,),
        name="input_grad",
    )
    peers, size = parts.shape[:2]
    if small_case and size % 16 == 0:
        saved = (active_low, second_low, first_low, pre_low, both, attended_low, rows.slots[None, :])
        grad_outer_weight, grad_inner_weight, grad_out_weight, all_tokens, weight_done = call(
            weight_grads_kernel,
            [
                (outer_weight.shape, F32, False),
                (inner_weight.shape, F32, False),
                (out_weight.shape, F32, False),
                ((rows.slots.shape[0], width), BF, False),
            ],
            saved,
            flops=2 * rows.count * width * (4 * width + width),
            far=range(7),
            limit=32,
            after=(sum_done,),
            name="weight_grads",
        )
        low = near_rows(query_low, weight_done)
        sent, add_done = call(
            functools.partial(add_parts_kernel, rows),
            [((peers, size + rows.slot, width), BF, True)],
            (parts,) + low,
            after=(input_done, weight_done),
            name="add_parts",
        )
        whole = exchange(sent, batch_n)
        rows_out, ffn_done = ffn(hidden, context, weights, (add_done,))
        whole = behind(whole, ffn_done)
        other = lax.ppermute(whole, "side", CORE_SWAP)
        grad_key_weight, grad_value_weight, grad_query_weight, grad_query_bias, _ = call(
            functools.partial(last_kernel, size),
            [((width, width), F32, False)] * 3 + [((1, width), F32, False)],
            (whole, other, all_tokens),
            far=(2,),
            limit=12,
            name="last_grads",
        )
    else:
        rows_out, _ = ffn(hidden, context, weights, (sum_done,))
        part = jnp.sum(parts.astype(F32), axis=0).astype(BF)
        whole = exchange(jnp.broadcast_to(part[None], parts.shape), batch_n).reshape(width, width)
        grad_outer_weight = t_dot(active_low, second_low)
        grad_inner_weight = t_dot(first_low, pre_low)
        grad_out_weight = t_dot(both[:, :width], attended_low)
        half, _ = call(
            functools.partial(half_kernel, rows),
            [((rows.half, width), BF, True)],
            near_rows(query_low),
            name="low_rows",
        )
        flat = (batch_n * rows.half, width)
        half = jnp.broadcast_to(half[None], (batch_n,) + half.shape)
        low_mine = lax.all_to_all(half, "batch", split_axis=0, concat_axis=0).reshape(flat)
        low_theirs = lax.ppermute(low_mine, "side", CORE_SWAP)
        all_low = join_halves(side % 2, low_mine, low_theirs)
        grad_query_weight = t_dot(both[:, width:], all_low)
        grad_query_bias = jnp.sum(all_low.astype(F32), axis=0)
        other = lax.ppermute(whole, "side", CORE_SWAP)
        first_core = side % 2 == 0
        grad_key_weight = jnp.where(first_core, whole, other).astype(F32)
        grad_value_weight = jnp.where(first_core, other, whole).astype(F32)

    return (
        loss.reshape(()),
        rows_out.reshape(hidden_in.shape),
        input_grad.reshape(hidden_in.shape),
        grad_query_weight,
        grad_query_bias.reshape(-1),
        grad_key_weight,
        grad_value_weight,
        small[6],
        grad_out_weight,
        small[5],
        small[3],
        small[4],
        grad_inner_weight,
        grad_inner_bias.reshape(-1),
        grad_outer_weight,
        small[2],
        small[0],
        small[1],
    )


def solution(mesh):
    rows = P("side", "batch", None, None)
    in_specs = (
        rows,
        P("side", "batch", None),
        P("batch", None),
        P("side", "batch", None),
        P("batch"),
        P(),
        P("batch", None),
    ) + (P(),) * 15
    out_specs = (P(), rows, rows) + (P(),) * 15
    return jax.shard_map(body, mesh=mesh, in_specs=in_specs, out_specs=out_specs, check_vma=False)
```

profile of v0, /device:TPU:0, one launch (start us, length us, event | category | flops | bytes accessed | tf_op | source)
XLA Modules:
  0.0 107.6 jit_solution(846004827023681056)
XLA Ops:
  0.7 5.6 %cls_forward.1 = (bf16[32,1024]{1,0:T(8,128)(2,1)S(1)}, bf16[32,512]{1,0:T(8,128)(2,1)}, bf16[32,1024]{1,0:T(8,128)(2,1)}, bf16[1024,512]{1,0:T(8,128)(2,1)}, bf...) custom-call(bf16[1024,512]{1,0:T(8,128)(2,1)} %bitcast.30, s32[1,1,1024]{2,1,0:T(1,128)} %refs_5_.3, ...), custom_call_target="tpu_custom_call" | custom-call | flops 1073741824 | bytes 5939348 | tf_op jit(solution)/shard_map/cls_forward/pallas_call | solution.py:179
  6.2 3.0 %collective-permute-start.1 = (bf16[32,1024]{1,0:T(8,128)(2,1)S(1)}, bf16[32,1024]{1,0:T(8,128)(2,1)S(1)}, u32[]{:S(2)}, u32[]{:S(2)}) collective-permute-start(bf16[32,1024]{1,0:T(8,128)(2,1)S(1)} %get-tuple-element.60.refs_0_), channel_id=1, source_target_pairs={{0,16},{16,0},{8,24},{24,8},{1,17},{17,1},{9,25},{25,9},{2,18},{18... | collective-permute-start | bytes 196616 | tf_op jit(solution)/shard_map/ppermute | solution.py:286
  9.3 2.2 %collective-permute-done.1.refs_2_ = bf16[32,1024]{1,0:T(8,128)(2,1)S(1)} collective-permute-done((bf16[32,1024]{1,0:T(8,128)(2,1)S(1)}, bf16[32,1024]{1,0:T(8,128)(2,1)S(1)}, u32[]{:S(2)}, u32[]{:S(2)}) %collective-permute-start.1) | collective-permute-done | bytes 65568 | tf_op jit(solution)/shard_map/ppermute | solution.py:286
  11.5 1.2 %collective-permute-done.2.refs_3_ = bf16[32,1024]{1,0:T(8,128)(2,1)S(1)} collective-permute-done((bf16[32,1024]{1,0:T(8,128)(2,1)S(1)}, bf16[32,1024]{1,0:T(8,128)(2,1)S(1)}, u32[]{:S(2)}, u32[]{:S(2)}) %collective-permute-start.2) | collective-permute-done | bytes 65568 | tf_op jit(solution)/shard_map/ppermute | solution.py:289
  12.8 1.7 %half_rows.1 = (bf16[8,32,1024]{2,1,0:T(8,128)(2,1)}, f32[8,128]{1,0:T(8,128)}) custom-call(bf16[32,1024]{1,0:T(8,128)(2,1)S(1)} %get-tuple-element.60.refs_0_, bf16[32,1024]{1,0:T(8,128)(2,1)S(1)} %collective-permute-done.refs_1_, bf16[32,1024]{1,0:T(8,128)(2,1)S(1)} %collective-permute-done.1.refs_2_, bf16[32,1024]{1,0:T(8,128)(2,1)S(1)} %collective-permute-done.2.refs_3_, ...), custom_call_target="tpu_custom_call" | custom-call | bytes 801920 | tf_op jit(solution)/shard_map/half_rows/pallas_call | solution.py:179
  14.5 6.3 %all-to-all-start = ((bf16[8,32,1024]{2,1,0:T(8,128)(2,1)}), bf16[8,32,1024]{2,1,0:T(8,128)(2,1)S(1)}, u32[]{:S(2)}, u32[]{:S(2)}) async-start(bf16[8,32,1024]{2,1,0:T(8,128)(2,1)} %get-tuple-element.61), calls=%async_computation | async-start | bytes 1048576 | tf_op jit(solution)/shard_map/all_to_all | solution.py:847
  20.8 12.7 %attention.1 = (bf16[1024,512]{1,0:T(8,128)(2,1)}, f32[8,128]{1,0:T(8,128)}) custom-call(bf16[1024,512]{1,0:T(8,128)(2,1)} %bitcast.31, bf16[512,512]{1,0:T(8,128)(2,1)} %refs_7_.3, f32[1,512]{1,0:T(1,128)} %bitcast.38, bf16[1024,512]{1,0:T(8,128)(2,1)} %get-tuple-element.62.refs_3_.refs_16_, bf16[1024,512]{1,0:T(8,128)(2,1)} %get-tuple-element.63.refs_4_.refs_13_, ...), custom_call_target="tpu_custom_call" | custom-call | flops 8000000000 | bytes 4724736 | tf_op jit(solution)/shard_map/attention/pallas_call | solution.py:179
  33.5 2.1 %all-to-all-done.refs_0_ = bf16[8,32,1024]{2,1,0:T(8,128)(2,1)S(1)} async-done(((bf16[8,32,1024]{2,1,0:T(8,128)(2,1)}), bf16[8,32,1024]{2,1,0:T(8,128)(2,1)S(1)}, u32[]{:S(2)}, u32[]{:S(2)}) %all-to-all-start) | async-done | bytes 524320 | tf_op jit(solution)/shard_map/all_to_all | solution.py:847
  35.6 1.9 %collective-permute-done.3.refs_1_ = bf16[8,32,1024]{2,1,0:T(8,128)(2,1)S(1)} collective-permute-done((bf16[8,32,1024]{2,1,0:T(8,128)(2,1)S(1)}, bf16[8,32,1024]{2,1,0:T(8,128)(2,1)S(1)}, u32[]{:S(2)}, u32[]{:S(2)}) %collective-permute-start.3) | collective-permute-done | bytes 524320 | tf_op jit(solution)/shard_map/ppermute | solution.py:853
  37.5 15.1 %cls_middle.1 = (f32[512,512]{1,0:T(8,128)S(1)}, bf16[512,512]{1,0:T(8,128)(2,1)S(1)}, bf16[32,512]{1,0:T(8,128)(2,1)S(1)}, bf16[32,512]{1,0:T(8,128)(2,1)}, f32...) custom-call(bf16[8,32,1024]{2,1,0:T(8,128)(2,1)S(1)} %hand_on.3.refs, ...), custom_call_target="tpu_custom_call" | custom-call | flops 4831838208 | bytes 17384420 | tf_op jit(solution)/shard_map/cls_middle/pallas_call | solution.py:179
  52.8 1.8 %collective-permute-done.4.refs_1_ = bf16[512,512]{1,0:T(8,128)(2,1)S(1)} collective-permute-done((bf16[512,512]{1,0:T(8,128)(2,1)S(1)}, bf16[512,512]{1,0:T(8,128)(2,1)S(1)}, u32[]{:S(2)}, u32[]{:S(2)}) %collective-permute-start.4) | collective-permute-done | bytes 524320 | tf_op jit(solution)/shard_map/ppermute | solution.py:526
  54.6 0.9 chip_sum.1
  55.5 5.6 %all-to-all-start.1 = ((bf16[16,32,512]{2,1,0:T(8,128)(2,1)}), bf16[16,32,512]{2,1,0:T(8,128)(2,1)S(1)}, u32[]{:S(2)}, u32[]{:S(2)}) async-start(bf16[16,32,512]{2,1,0:T(8,128)(2,1)} %bitcast.11), calls=%async_computation.1 | async-start | bytes 1048576 | tf_op jit(solution)/shard_map/all_to_all | solution.py:520
  61.1 2.0 %collective-permute-start.6 = (bf16[32,512]{1,0:T(8,128)(2,1)S(1)}, bf16[32,512]{1,0:T(8,128)(2,1)S(1)}, u32[]{:S(2)}, u32[]{:S(2)}) collective-permute-start(bf16[32,512]{1,0:T(8,128)(2,1)S(1)} %get-tuple-element.73.refs_5_.refs_1_), channel_id=1, source_target_pairs={{0,16},{16,0},{8,24},{24,8},{1,17},{17,1},{9,25},{25,9},{2,18},{18... | collective-permute-start | bytes 98312 | tf_op jit(solution)/shard_map/ppermute | solution.py:286
  63.0 6.3 %weight_grads.1 = (f32[2048,512]{1,0:T(8,128)}, f32[512,2048]{1,0:T(8,128)}, f32[512,512]{1,0:T(8,128)}, bf16[512,512]{1,0:T(8,128)(2,1)}, f32[8,128]{1,0:T(8,128)}) custom-call(bf16[384,2048]{1,0:T(8,128)(2,1)} %get-tuple-element.74.refs_0_, bf16[384,512]{1,0:T(8,128)(2,1)} %get-tuple-element.75.refs_1_, bf16[384,512]{1,0:T(8,128)(2,1)} %get-tuple-element.76.refs_2_, ...), custom_call_target="tpu_custom_call" | custom-call | flops 1006632960 | bytes 15075328 | tf_op jit(solution)/shard_map/weight_grads/pallas_call | solution.py:179
  70.0 5.2 %input_grad.1 = (bf16[1024,512]{1,0:T(8,128)(2,1)}, f32[8,128]{1,0:T(8,128)}) custom-call(bf16[32,1024]{1,0:T(8,128)(2,1)} %get-tuple-element.82.refs_0_, bf16[256,1024]{1,0:T(8,128)(2,1)} %get-tuple-element.83.refs_1_, f32[256,1024]{1,0:T(8,128)} %get-tuple-element.66.refs_14_.refs_2_, bf16[32,512]{1,0:T(8,128)(2,1)} %get-tuple-element.84.refs_3_, ...), custom_call_target="tpu_custom_call" | custom-call | flops 1610612736 | bytes 4423680 | tf_op jit(solution)/shard_map/input_grad/pallas_call | solution.py:179
  75.2 1.2 %all-to-all-done.1.refs_0_ = bf16[16,32,512]{2,1,0:T(8,128)(2,1)S(1)} async-done(((bf16[16,32,512]{2,1,0:T(8,128)(2,1)}), bf16[16,32,512]{2,1,0:T(8,128)(2,1)S(1)}, u32[]{:S(2)}, u32[]{:S(2)}) %all-to-all-start.1) | async-done | bytes 524320 | tf_op jit(solution)/shard_map/all_to_all | solution.py:520
  76.4 1.0 add_parts.1
  77.5 4.3 %all-to-all-start.2 = ((bf16[16,48,512]{2,1,0:T(8,128)(2,1)}), bf16[16,48,512]{2,1,0:T(8,128)(2,1)S(1)}, u32[]{:S(2)}, u32[]{:S(2)}) async-start(bf16[16,48,512]{2,1,0:T(8,128)(2,1)} %get-tuple-element.90), calls=%async_computation.2 | async-start | bytes 1572864 | tf_op jit(solution)/shard_map/all_to_all | solution.py:520
  81.8 11.7 %feed_forward.1 = (bf16[1024,512]{1,0:T(8,128)(2,1)}, f32[8,128]{1,0:T(8,128)}) custom-call(bf16[1024,512]{1,0:T(8,128)(2,1)} %bitcast.33, bf16[1024,512]{1,0:T(8,128)(2,1)} %get-tuple-element.69.refs_1_, bf16[512,512]{1,0:T(8,128)(2,1)} %refs_2_.5, f32[1,512]{1,0:T(1,128)} %bitcast.40, f32[1,512]{1,0:T(1,128)} %bitcast.42, f32[1,512]{1,0:T(1,128)} %bitcast.44, ...), custom_call_target="tpu_custom_call" | custom-call | flops 6000000000 | bytes 7884800 | tf_op jit(solution)/shard_map/feed_forward/pallas_call | solution.py:179
  93.5 8.9 %all-to-all-done.2.refs_0_ = bf16[16,48,512]{2,1,0:T(8,128)(2,1)S(1)} async-done(((bf16[16,48,512]{2,1,0:T(8,128)(2,1)}), bf16[16,48,512]{2,1,0:T(8,128)(2,1)S(1)}, u32[]{:S(2)}, u32[]{:S(2)}) %all-to-all-start.2) | async-done | bytes 786464 | tf_op jit(solution)/shard_map/all_to_all | solution.py:520
  102.4 0.6 fusion
  103.0 1.7 %collective-permute-done.8.refs_1_ = bf16[16,48,512]{2,1,0:T(8,128)(2,1)S(1)} collective-permute-done((bf16[16,48,512]{2,1,0:T(8,128)(2,1)S(1)}, bf16[16,48,512]{2,1,0:T(8,128)(2,1)S(1)}, u32[]{:S(2)}, u32[]{:S(2)}) %collective-permute-start.8) | collective-permute-done | bytes 786464 | tf_op jit(solution)/shard_map/ppermute | solution.py:924
  104.7 2.7 %last_grads.1 = (f32[512,512]{1,0:T(8,128)}, f32[512,512]{1,0:T(8,128)}, f32[512,512]{1,0:T(8,128)}, f32[1,512]{1,0:T(1,128)}, f32[8,128]{1,0:T(8,128)}) custom-call(bf16[16,48,512]{2,1,0:T(8,128)(2,1)S(1)} %hand_on.5.refs_0_, bf16[16,48,512]{2,1,0:T(8,128)(2,1)S(1)} %collective-permute-done.8.refs_1_, bf16[512,512]{1,0:T(8,128)(2,1)} %get-tuple-element.92.refs_2_), custom_call_target="tpu_custom_call" | custom-call | bytes 5244928 | tf_op jit(solution)/shard_map/last_grads/pallas_call | solution.py:179
  (16 shorter events, 0.8 us)
Async XLA Ops:
  6.2 5.3 %collective-permute-start.1 = (bf16[32,1024]{1,0:T(8,128)(2,1)S(1)}, bf16[32,1024]{1,0:T(8,128)(2,1)S(1)}, u32[]{:S(2)}, u32[]{:S(2)}) collective-permute-start(bf16[32,1024]{1,0:T(8,128)(2,1)S(1)} %get-tuple-element.60.refs_0_), channel_id=1, source_target_pairs={{0,16},{16,0},{8,24},{24,8},{1,17},{17,1},{9,25},{25,9},{2,18},{18... | collective-permute-start | bytes 196616 | tf_op jit(solution)/shard_map/ppermute | solution.py:286
  9.3 2.3 %collective-permute-start = (bf16[32,1024]{1,0:T(8,128)(2,1)S(1)}, bf16[32,1024]{1,0:T(8,128)(2,1)S(1)}, u32[]{:S(2)}, u32[]{:S(2)}) collective-permute-start(bf16[32,1024]{1,0:T(8,128)(2,1)S(1)} %get-tuple-element.60.refs_0_), channel_id=1, source_target_pairs={{0,8},{8,0},{16,24},{24,16},{1,9},{9,1},{17,25},{25,17},{2,10},{10... | collective-permute-start | bytes 196616 | tf_op jit(solution)/shard_map/ppermute | solution.py:285
  11.5 1.3 %collective-permute-start.2 = (bf16[32,1024]{1,0:T(8,128)(2,1)S(1)}, bf16[32,1024]{1,0:T(8,128)(2,1)S(1)}, u32[]{:S(2)}, u32[]{:S(2)}) collective-permute-start(bf16[32,1024]{1,0:T(8,128)(2,1)S(1)} %collective-permute-done.1.refs_2_), channel_id=1, source_target_pairs={{0,8},{8,0},{16,24},{24,16},{1,9},{9,1},{17,25},{25,17},{2,10},{10... | collective-permute-start | bytes 196616 | tf_op jit(solution)/shard_map/ppermute | solution.py:289
  14.5 21.1 %all-to-all-start = ((bf16[8,32,1024]{2,1,0:T(8,128)(2,1)}), bf16[8,32,1024]{2,1,0:T(8,128)(2,1)S(1)}, u32[]{:S(2)}, u32[]{:S(2)}) async-start(bf16[8,32,1024]{2,1,0:T(8,128)(2,1)} %get-tuple-element.61), calls=%async_computation | async-start | bytes 1048576 | tf_op jit(solution)/shard_map/all_to_all | solution.py:847
  35.6 1.9 %collective-permute-start.3 = (bf16[8,32,1024]{2,1,0:T(8,128)(2,1)S(1)}, bf16[8,32,1024]{2,1,0:T(8,128)(2,1)S(1)}, u32[]{:S(2)}, u32[]{:S(2)}) collective-permute-start(bf16[8,32,1024]{2,1,0:T(8,128)(2,1)S(1)} %hand_on.3.refs_0_), channel_id=1, source_target_pairs={{0,8},{8,0},{16,24},{24,16},{1,9},{9,1},{17,25},{25,17},{2,10},{10... | collective-permute-start | bytes 1572872 | tf_op jit(solution)/shard_map/ppermute | solution.py:853
  52.6 2.0 %collective-permute-start.4 = (bf16[512,512]{1,0:T(8,128)(2,1)S(1)}, bf16[512,512]{1,0:T(8,128)(2,1)S(1)}, u32[]{:S(2)}, u32[]{:S(2)}) collective-permute-start(bf16[512,512]{1,0:T(8,128)(2,1)S(1)} %get-tuple-element.71), channel_id=1, source_target_pairs={{0,8},{8,0},{16,24},{24,16},{1,9},{9,1},{17,25},{25,17},{2,10},{10... | collective-permute-start | bytes 1572872 | tf_op jit(solution)/shard_map/ppermute | solution.py:526
  55.5 21.0 %all-to-all-start.1 = ((bf16[16,32,512]{2,1,0:T(8,128)(2,1)}), bf16[16,32,512]{2,1,0:T(8,128)(2,1)S(1)}, u32[]{:S(2)}, u32[]{:S(2)}) async-start(bf16[16,32,512]{2,1,0:T(8,128)(2,1)} %bitcast.11), calls=%async_computation.1 | async-start | bytes 1048576 | tf_op jit(solution)/shard_map/all_to_all | solution.py:520
  61.1 8.3 %collective-permute-start.6 = (bf16[32,512]{1,0:T(8,128)(2,1)S(1)}, bf16[32,512]{1,0:T(8,128)(2,1)S(1)}, u32[]{:S(2)}, u32[]{:S(2)}) collective-permute-start(bf16[32,512]{1,0:T(8,128)(2,1)S(1)} %get-tuple-element.73.refs_5_.refs_1_), channel_id=1, source_target_pairs={{0,16},{16,0},{8,24},{24,8},{1,17},{17,1},{9,25},{25,9},{2,18},{18... | collective-permute-start | bytes 98312 | tf_op jit(solution)/shard_map/ppermute | solution.py:286
  63.0 12.2 %collective-permute-start.5 = (bf16[32,512]{1,0:T(8,128)(2,1)S(1)}, bf16[32,512]{1,0:T(8,128)(2,1)S(1)}, u32[]{:S(2)}, u32[]{:S(2)}) collective-permute-start(bf16[32,512]{1,0:T(8,128)(2,1)S(1)} %get-tuple-element.73.refs_5_.refs_1_), channel_id=1, source_target_pairs={{0,8},{8,0},{16,24},{24,16},{1,9},{9,1},{17,25},{25,17},{2,10},{10... | collective-permute-start | bytes 98312 | tf_op jit(solution)/shard_map/ppermute | solution.py:285
  69.4 5.8 %collective-permute-start.7 = (bf16[32,512]{1,0:T(8,128)(2,1)S(1)}, bf16[32,512]{1,0:T(8,128)(2,1)S(1)}, u32[]{:S(2)}, u32[]{:S(2)}) collective-permute-start(bf16[32,512]{1,0:T(8,128)(2,1)S(1)} %hand_on.4.refs_3_), channel_id=1, source_target_pairs={{0,8},{8,0},{16,24},{24,16},{1,9},{9,1},{17,25},{25,17},{2,10},{10... | collective-permute-start | bytes 98312 | tf_op jit(solution)/shard_map/ppermute | solution.py:289
  77.5 24.9 %all-to-all-start.2 = ((bf16[16,48,512]{2,1,0:T(8,128)(2,1)}), bf16[16,48,512]{2,1,0:T(8,128)(2,1)S(1)}, u32[]{:S(2)}, u32[]{:S(2)}) async-start(bf16[16,48,512]{2,1,0:T(8,128)(2,1)} %get-tuple-element.90), calls=%async_computation.2 | async-start | bytes 1572864 | tf_op jit(solution)/shard_map/all_to_all | solution.py:520
  81.8 20.6 %copy-start = (f32[8,512]{1,0:T(8,128)S(1)}, f32[8,512]{1,0:T(8,128)}, u32[]{:S(2)}) copy-start(f32[8,512]{1,0:T(8,128)} %get-tuple-element.97) | copy-start | bytes 49156
  102.4 2.3 %collective-permute-start.8 = (bf16[16,48,512]{2,1,0:T(8,128)(2,1)S(1)}, bf16[16,48,512]{2,1,0:T(8,128)(2,1)S(1)}, u32[]{:S(2)}, u32[]{:S(2)}) collective-permute-start(bf16[16,48,512]{2,1,0:T(8,128)(2,1)S(1)} %hand_on.5.refs_0_), channel_id=1, source_target_pairs={{0,8},{8,0},{16,24},{24,16},{1,9},{9,1},{17,25},{25,17},{2,10},{10... | collective-permute-start | bytes 2359304 | tf_op jit(solution)/shard_map/ppermute | solution.py:924
where the time goes:
time: 108 us
  Pallas kernels  63 us (58%)
  starting transfers between devices  22 us (20%)
  waiting for transfers between devices  21 us (19%)
    pallas_call x10, Pallas kernels, call(): pl.pallas_call(wrapped, out_shape=shapes, in_specs=spaces, out_specs=out_...  63 us
    all_to_all x2, waiting for transfers between devices, exchange(): lax.all_to_all(sent, ('side', 'batch'), split_axis=0, concat_axis=0, axis...  10.1 us
    all_to_all x2, starting transfers between devices, exchange(): lax.all_to_all(sent, ('side', 'batch'), split_axis=0, concat_axis=0, axis...  9.92 us
    all_to_all x1, starting transfers between devices, body(): mine = lax.all_to_all(sent, 'batch', split_axis=0, concat_axis=0)  6.32 us
    ppermute x2, starting transfers between devices, near_rows(): far = lax.ppermute(own, 'side', CHIP_SWAP)  5.01 us
    ppermute x2, waiting for transfers between devices, near_rows(): far = lax.ppermute(own, 'side', CHIP_SWAP)  2.24 us
  transfers between devices with their start and end apart: 12, of which 8 were waited for; matrix products, arithmetic and copies ran while one was open for 1% of the time, Pallas kernels for 33%

commit v1 on v0

--- a/solution.py
+++ b/solution.py
@@ -84,22 +84,29 @@
     def __init__(self, source, buffer, semaphores, axis=0, parts=1):
         self.buffer, self.shape = buffer, buffer.shape
         self.axis, self.size = axis, buffer.shape[axis] // parts
-        self.waiting = {}
+        self.waiting, self.copies = {}, []
         for i in range(parts):
             at = self.place(i) if parts > 1 else (Ellipsis,)
-            copy = pltpu.make_async_copy(source.at[at], buffer.at[at], semaphores.at[i])
-            copy.start()
-            self.waiting[i] = copy
+            self.copies.append(pltpu.make_async_copy(source.at[at], buffer.at[at], semaphores.at[i]))
+
+    def start(self):
+        if not self.waiting and self.copies:
+            self.waiting = dict(enumerate(self.copies))
+            self.copies = []
+            for copy in self.waiting.values():
+                copy.start()
 
     def place(self, i):
         return (slice(None),) * self.axis + (pl.ds(i * self.size, self.size),)
 
     def part(self, i):
+        self.start()
         if i in self.waiting:
             self.waiting.pop(i).wait()
         return self.buffer[self.place(i)]
 
     def ref(self):
+        self.start()
         for i in sorted(self.waiting):
             self.waiting.pop(i).wait()
         return self.buffer
@@ -132,7 +139,7 @@
 TOKEN = ((8, 128), F32, False)
 
 
-def call(kernel, outs, ins, flops=0, scratch=(), limit=8, far=(), smem=(), split=None, after=(), name=None):
+def call(kernel, outs, ins, flops=0, scratch=(), limit=8, far=(), smem=(), split=None, late=(), after=(), name=None):
     n_in, n_out, n_after = len(ins), len(outs), len(after)
     split = split or {}
     far_in = list(smem) + [i for i in far if i not in smem]
@@ -153,6 +160,8 @@
             semaphores, refs = refs[0], refs[1:]
             for k, i in enumerate(far_in):
                 in_refs[i] = Fetched(in_refs[i], in_bufs[k], semaphores.at[k], *split.get(i, ()))
+                if i not in late:
+                    in_refs[i].start()
         if far_out:
             semaphores, refs = refs[0], refs[1:]
             for k, i in enumerate(far_out):
@@ -198,6 +207,7 @@
         in_specs=[VM] + [pl.BlockSpec(memory_space=pltpu.HBM)] * len(tokens),
         out_specs=VM,
         input_output_aliases={0: 0},
+        compiler_params=pltpu.CompilerParams(vmem_limit_bytes=MIB),
         name="hand_on",
     )(value, *tokens)
 
@@ -260,25 +270,28 @@
     if len(refs) == 1:
         out_ref[...] = half
         return
-    teacher_ref, pair_ref = refs[:2]
-    count, told = n // 2, teacher_ref.shape[1]
-    mine = jnp.where(core == 0, teacher_ref[:count, :], teacher_ref[count:, :])
+    full = jnp.concatenate([half, refs[0][...]], axis=0)
+    for b in range(rows.batch_n):
+        out_ref[b] = full
+
+
+def teacher_terms(rows, teacher_ref, pair_ref, out_ref):
+    core, _ = core_chip()
+    count, told = rows.n_query // 2, teacher_ref.shape[1]
     line = iota((count, 1), 0)
     pair = jnp.zeros((count, 1), jnp.int32)
     for i in range(count):
         pair = jnp.where(line == i, pair_ref.ref()[core * count + i], pair)
     pair = jnp.broadcast_to(pair.astype(F32), (count, rows.columns - told))
+    mine = jnp.where(core == 0, teacher_ref[:count, :], teacher_ref[count:, :])
     mine = jnp.concatenate([mine, pair], axis=1)
     high = mine.astype(BF)
     mid = (mine - high.astype(F32)).astype(BF)
     low = (mine - high.astype(F32) - mid.astype(F32)).astype(BF)
     terms = jnp.concatenate([high, mid, low], axis=1)
-    side = out_ref.shape[2] // 2
+    side = out_ref.shape[1] // 2
     terms = jnp.concatenate([terms, jnp.zeros((count, side - terms.shape[1]), BF)], axis=1)
-    terms = jnp.concatenate([terms[: count // 2], terms[count // 2 :]], axis=1)
-    full = jnp.concatenate([half, terms], axis=0)
-    for b in range(rows.batch_n):
-        out_ref[b] = full
+    out_ref[...] = jnp.concatenate([terms[: count // 2], terms[count // 2 :]], axis=1)
 
 
 def near_rows(own, *tokens):
@@ -295,10 +308,21 @@
     )
 
 
+def cls_probs(pick, query, key_ref, seg_ref):
+    seg = seg_ref[0].astype(F32)
+    cls_seg = jnp.sum(jnp.where(pick, seg, 0.0), axis=1, keepdims=True)
+    bias = jnp.where(cls_seg == seg, 0.0, NEG_FILL)
+    scores = dot_t(spread_heads(query) * BF(HD**-0.5), key_ref[...])
+    scores = scores + jnp.concatenate([bias] * HEADS, axis=0)
+    expo = jnp.exp(scores - jnp.max(scores, axis=1, keepdims=True))
+    return expo / jnp.sum(expo, axis=1, keepdims=True)
+
+
 def cls_forward_kernel(
-    n_pass, x_ref, seg_ref, query_cls_ref, pass_cls_ref, wq_ref, bq_ref, wk_ref, wv_ref, bv_ref,
-    rows_ref, query_ref, pick_ref, key_ref, value_ref, probs_ref,
+    rows, with_terms, x_ref, seg_ref, query_cls_ref, pass_cls_ref, wq_ref, bq_ref, wk_ref, wv_ref, bv_ref,
+    teacher_ref, pair_ref, rows_ref, query_ref, pick_ref, key_ref, value_ref, terms_ref,
 ):
+    n_pass = rows.n_pass
     side = lax.axis_index("side")
     n_query, width = query_ref.shape
     slot = iota((n_query, 1), 0)
@@ -309,38 +333,36 @@
     pick = iota((n_query, x_ref.shape[0]), 1) == cls
     pick_low = jnp.where(pick, 1.0, 0.0).astype(BF)
     pick_ref[...] = pick_low
+    pick_ref.flush()
+    if with_terms:
+        teacher_terms(rows, teacher_ref, pair_ref, terms_ref)
+    for i in range(PARTS):
+        part = slice(i * x_ref.size, i * x_ref.size + x_ref.size)
+        key_ref[part, :] = dot(x_ref.part(i), wk_ref[...]).astype(BF)
+    key_ref.flush()
     x = x_ref.ref()
-    key_ref[...] = dot(x[...], wk_ref[...]).astype(BF)
-    key_ref.flush()
     value_ref[...] = (dot(x[...], wv_ref[...]) + bv_ref[...]).astype(BF)
     value_ref.flush()
-    seg = seg_ref[0].astype(F32)
-    cls_seg = jnp.sum(jnp.where(pick, seg, 0.0), axis=1, keepdims=True)
     tokens = dot(pick_low, x[...]).astype(BF)
     query = (dot(tokens, wq_ref[...]) + bq_ref[...]).astype(BF)
     query_ref[...] = query
-    bias = jnp.where(cls_seg == seg, 0.0, NEG_FILL)
-    scores = dot_t(spread_heads(query) * BF(HD**-0.5), key_ref[...])
-    scores = scores + jnp.concatenate([bias] * HEADS, axis=0)
-    expo = jnp.exp(scores - jnp.max(scores, axis=1, keepdims=True))
-    probs = expo / jnp.sum(expo, axis=1, keepdims=True)
-    probs_ref[...] = probs
-    probs_ref.flush()
+    query_ref.flush()
+    probs = cls_probs(pick, query, key_ref, seg_ref)
     rows_ref[:, :width] = fold_heads(dot(probs.astype(BF), value_ref[...])).astype(BF)
     rows_ref[:, width:] = tokens
 
 
 def middle_kernel(
     rows, pass_count,
-    mine_ref, theirs_ref, wo_ref, bo_ref, g1_ref, s1_ref, wi_ref, bi_ref, wu_ref, bu_ref, g2_ref, s2_ref,
-    at_ref, value_ref, probs_ref, x_ref, key_ref, query_ref, cluster_ref,
+    mine_ref, theirs_ref, wo_ref, vector_ref, wi_ref, wu_ref, at_ref, value_ref, probs_ref, x_ref, key_ref, query_ref, cluster_ref,
     keep_ref, give_ref, low_ref, context_ref, gown_ref, scores_ref,
     loss_ref, small_ref, inner_bias_ref,
     both_ref, first_ref, active_ref, pre_ref, second_ref, attended_ref, slope_ref, told_ref,
 ):
     width = wo_ref.shape[0]
+    bo_ref, g1_ref, s1_ref, bu_ref, g2_ref, s2_ref, bi_ref = vectors_of(vector_ref, width)
     n_queries, n_columns = told_ref.shape
-    chunk = wi_ref.size
+    chunk = wi_ref.shape[1] // PARTS
     side, batch = lax.axis_index("side"), lax.axis_index("batch")
     core = side % 2
     code_at, query_at, pass_at = at_ref[0:1, :], at_ref[1:2, :], at_ref[2:3, :]
@@ -358,18 +380,20 @@
                 told_ref[row : row + count // 2, :] = cut[0] + cut[1] + cut[2]
     attended = both_ref[:, width:].astype(F32) + (dot(both_ref[:, :width], wo_ref[...]) + bo_ref[...])
     first_hat, first_inv = norm_stats(attended)
+    for ref in (value_ref, probs_ref, x_ref, key_ref, query_ref):
+        ref.start()
     first = first_hat * g1_ref[...] + s1_ref[...]
     first_low = first.astype(BF)
     first_ref[...] = first_low
     second = first + bu_ref[...]
     for i in range(PARTS):
         c = i * chunk
-        pre = dot(first_low, wi_ref.part(i)) + bi_ref[:, c : c + chunk]
+        pre = dot(first_low, wi_ref[:, c : c + chunk]) + bi_ref[:, c : c + chunk]
         active, slope = gelu_parts(pre)
         active = active.astype(BF)
         active_ref[:, c : c + chunk] = active
         slope_ref[:, c : c + chunk] = slope
-        second += dot(active, wu_ref.part(i))
+        second += dot(active, wu_ref[c : c + chunk, :])
     both_ref.flush()
     first_ref.flush()
     active_ref.flush()
@@ -395,6 +419,7 @@
     pairs = jnp.where(counted, 1.0, 0.0)
     pairs = jnp.sum(jnp.sum(pairs, axis=1, keepdims=True), axis=0, keepdims=True)
     loss_ref[...] = squares / jnp.maximum(pairs, 1.0)
+    loss_ref.flush()
     grad_score = jnp.where(is_pair, jnp.sum(resid, axis=1, keepdims=True), 0.0) - resid
     grad_low = (grad_score * scale).astype(BF)
     grad_rows = dot(t_dot(query_pick, grad_low).astype(BF), pass_pick).astype(BF)
@@ -409,11 +434,12 @@
     grad_first = grad_second
     for i in range(PARTS):
         c = i * chunk
-        grad_pre = dot_t(second_low, wu_ref.part(i)) * slope_ref[:, c : c + chunk]
+        grad_pre = dot_t(second_low, wu_ref[c : c + chunk, :]) * slope_ref[:, c : c + chunk]
         inner_bias_ref[:, c : c + chunk] = jnp.sum(grad_pre, axis=0, keepdims=True)
         pre_low = grad_pre.astype(BF)
         pre_ref[:, c : c + chunk] = pre_low
-        grad_first += dot_t(pre_low, wi_ref.part(i))
+        grad_first += dot_t(pre_low, wi_ref[:, c : c + chunk])
+    inner_bias_ref.flush()
     pre_ref.flush()
     second_ref.flush()
     grad_attended = norm_back(grad_first, first_hat, first_inv, g1_ref[...])
@@ -429,6 +455,7 @@
     note(5, grad_attended)
     note(6, grad_context.astype(F32))
     small_ref[7:8, :] = jnp.zeros((1, width), F32)
+    small_ref.flush()
 
 
     slot = iota((rows.n_query, 1), 0)
@@ -439,8 +466,10 @@
     rest = (grad_attended - high.astype(F32)).astype(BF)
     own = jnp.where(own, 1.0, 0.0).astype(BF)
     gown_ref[...] = dot(own, high) + dot(own, rest)
+    gown_ref.flush()
     context = dot(own, grad_context).astype(BF)
     context_ref[...] = context
+    context_ref.flush()
     wide = spread_heads(context)
     probs = probs_ref[...]
     grad_probs = dot_t(wide, value_ref[...])
@@ -548,17 +577,40 @@
     x_ref[...] = t_dot(pick, both_ref[:, width:]).astype(BF)
 
 
+class Row:
+    def __init__(self, source, at, width):
+        self.source, self.at, self.width = source, at, width
+
+    def __getitem__(self, index):
+        first, last = 0, self.width
+        if index is not Ellipsis:
+            first, last = index[1].start, index[1].stop
+        return self.source[self.at : self.at + 1, first:last]
+
+
+def vectors_of(source, width):
+    return [Row(source, i, width) for i in range(6)] + [Row(source, 6, source.shape[1])]
+
+
 def column_of(row):
     return jnp.transpose(jnp.broadcast_to(row, (128, row.shape[1])))[:, :1]
 
 
 def attention_kernel(
-    tile, sizes, x_ref, wq_ref, bq_ref, key_ref, value_ref, seg_ref, out_ref, q_scr, bias_scr
+    tile, sizes, x_ref, wq_ref, bq_ref, key_ref, value_ref, seg_ref, *refs
 ):
+    pick_ref, query_ref = refs[:2]
+    out_ref, vector_ref, probs_ref, q_scr, bias_scr = refs[-5:]
     count = x_ref.shape[0]
     x, wq, bq, seg = x_ref.ref(), wq_ref.ref(), bq_ref[...], seg_ref[0]
     places = iota((1, count), 1)
     keys, values = key_ref.ref(), value_ref.ref()
+
+    for i, ref in enumerate(refs[2:-5]):
+        vector_ref[i : i + 1, : ref.shape[1]] = ref[...]
+    vector_ref.flush()
+    probs_ref[...] = cls_probs(pick_ref[...].astype(F32) > 0.5, query_ref[...], key_ref, seg_ref)
+    probs_ref.flush()
 
     @pl.loop(0, count // tile)
     def _(i):
@@ -605,26 +657,30 @@
             before = jnp.where(fits, 1, before)
 
 
-def attention(x, wq, bq, keys, values, seg, after, tile=256):
+def attention(x, wq, bq, keys, values, seg, pick, query, vectors, after, tile=256):
     t, d = x.shape
     sizes = [s for s in (384, 512, 768) if s < t] + [t]
     return call(
         functools.partial(attention_kernel, tile, sizes),
-        [((t, d), BF, False)],
-        (x, wq, bq, keys, values, seg),
+        [
+            ((t, d), BF, False),
+            ((8, vectors[-1].shape[1]), F32, False),
+            ((HEADS * query.shape[0], t), F32, False),
+        ],
+        (x, wq, bq, keys, values, seg, pick, query) + vectors,
         flops=8 * 10**9,
-        far=range(6),
+        far=range(8 + len(vectors)),
+        scratch=[pltpu.VMEM((tile, d), BF), pltpu.VMEM((tile, t), F32)],
         limit=20,
-        scratch=[pltpu.VMEM((tile, d), BF), pltpu.VMEM((tile, t), F32)],
         after=after,
         name="attention",
     )
 
 
 def ffn_kernel(
-    tile, x_ref, c_ref, wo_ref, bo_ref, g1_ref, s1_ref, wi_ref, bi_ref, wu_ref, bu_ref, g2_ref,
-    s2_ref, out_ref,
+    tile, x_ref, c_ref, wo_ref, vector_ref, wi_ref, wu_ref, out_ref,
 ):
+    bo_ref, g1_ref, s1_ref, bu_ref, g2_ref, s2_ref, bi_ref = vectors_of(vector_ref, x_ref.shape[1])
     chunk = wi_ref.size
     for t in range(0, x_ref.shape[0], tile):
         part = slice(t, t + tile)
@@ -645,9 +701,9 @@
         [(x.shape, BF, False)],
         (x, context) + weights,
         flops=6 * 10**9,
-        far=range(12),
+        far=range(6),
         limit=20,
-        split={6: (1, PARTS), 8: (0, PARTS)},
+        split={4: (1, PARTS), 5: (0, PARTS)},
         after=after,
         name="feed_forward",
     )
@@ -728,8 +784,33 @@
     return keep, give, low, context, own_attended, grad_scores
 
 
+def fetch(arrays, behind_this):
+    hbm = pl.BlockSpec(memory_space=pltpu.HBM)
+    count = len(arrays)
+
+    def kernel(*refs):
+        semaphores = refs[-1]
+        copies = [
+            pltpu.make_async_copy(refs[i], refs[count + 1 + i], semaphores.at[i]) for i in range(count)
+        ]
+        for copy in copies:
+            copy.start()
+        for copy in copies:
+            copy.wait()
+
+    return pl.pallas_call(
+        kernel,
+        out_shape=[pltpu.VMEM(x.shape, x.dtype) for x in arrays],
+        in_specs=[hbm] * count + [VM],
+        out_specs=[VM] * count,
+        scratch_shapes=[pltpu.SemaphoreType.DMA((count,))],
+        compiler_params=pltpu.CompilerParams(vmem_limit_bytes=4 * MIB),
+        name="fetch",
+    )(*[pltpu.with_memory_space_constraint(x, pltpu.HBM) for x in arrays], behind_this)
+
+
 def middle(rows, pass_count, mine, theirs, kept, weights, cluster, hidden, after):
-    width, ff = weights[4].shape
+    width, ff = weights[2].shape
     count = rows.count
     keys, values, cls_query, probs = kept
     at = np.stack([rows.code, rows.query, rows.passage])
@@ -750,10 +831,10 @@
             pltpu.VMEM((count, ff), F32),
             pltpu.VMEM((rows.batch_n * rows.n_query, rows.columns), F32),
         ],
-        far=range(2, len(ins)),
-        split={6: (1, PARTS), 8: (0, PARTS)},
+        far=range(6, len(ins)),
         smem=(len(ins) - 1,),
-        limit=40,
+        late=range(7, len(ins) - 1),
+        limit=32,
         after=after,
         name="cls_middle",
     )
@@ -804,36 +885,35 @@
     small_case = rows.count <= 512 and 3 * rows.columns <= width and n_query % 32 == 0
 
     token = ((count_tok, width), BF, False)
-    own, cls_query, pick, keys, values, probs, _ = call(
-        functools.partial(cls_forward_kernel, n_pass),
+    extra = n_query // 4 if small_case else 8
+    own, cls_query, pick, keys, values, terms, _ = call(
+        functools.partial(cls_forward_kernel, rows, small_case),
         [
             ((n_query, 2 * width), BF, True),
             ((n_query, width), BF, False),
             ((n_query, count_tok), BF, False),
             token,
             token,
-            ((HEADS * n_query, count_tok), F32, False),
+            ((extra, 2 * width), BF, True),
         ],
         (
             hidden, segments, query_cls, passage_cls, query_weight, vec(query_bias), key_weight,
-            value_weight, vec(value_bias),
+            value_weight, vec(value_bias), teacher, pair_passage,
         ),
         flops=4 * count_tok * width * width,
-        far=(0, 6, 1, 4, 5, 7, 8),
-        smem=(2, 3),
-        limit=20,
+        far=(6, 0, 9, 7, 1, 4, 5, 8),
+        smem=(2, 3, 10),
+        split={0: (0, PARTS)},
+        limit=24,
         name="cls_forward",
     )
 
-    extra = n_query // 4 if small_case else 0
     near = near_rows(own)
     if small_case:
         sent, half_done = call(
             functools.partial(half_kernel, rows),
             [((batch_n, rows.half + extra, 2 * width), BF, True)],
-            near + (teacher, pair_passage),
-            far=(4,),
-            smem=(5,),
+            near + (terms,),
             name="half_rows",
         )
     else:
@@ -845,9 +925,11 @@
         )
         sent = jnp.broadcast_to(half[None], (batch_n,) + half.shape)
     mine = lax.all_to_all(sent, "batch", split_axis=0, concat_axis=0)
-    context, attention_done = attention(
-        hidden, query_weight, vec(query_bias), keys, values, segments, (half_done,)
-    )
+    vectors = (weights[1], weights[2], weights[3], weights[7], weights[8], weights[9], weights[5])
+    context, vectors, probs, attention_done = attention(
+        hidden, query_weight, vec(query_bias), keys, values, segments, pick, cls_query, vectors, (half_done,)
+    )
+    matrices = (out_weight, vectors, inner_weight, outer_weight)
     if small_case:
         mine = behind(mine, attention_done)
     theirs = lax.ppermute(mine, "side", CORE_SWAP)
@@ -858,7 +940,7 @@
             keep, give, query_low, own_context, own_attended, grad_scores, loss, small, grad_inner_bias,
             both, first_low, active_low, pre_low, second_low, attended_low, _,
         ) = middle(
-            rows, pass_count, mine, theirs, kept, weights, passage_cluster, hidden, (attention_done,)
+            rows, pass_count, mine, theirs, kept, tuple(fetch(matrices, mine)), passage_cluster, hidden, ()
         )
     else:
         told = jnp.concatenate([teacher, pair_passage[:, None].astype(F32)], axis=1)
@@ -919,7 +1001,7 @@
             name="add_parts",
         )
         whole = exchange(sent, batch_n)
-        rows_out, ffn_done = ffn(hidden, context, weights, (add_done,))
+        rows_out, ffn_done = ffn(hidden, context, matrices, (add_done,))
         whole = behind(whole, ffn_done)
         other = lax.ppermute(whole, "side", CORE_SWAP)
         grad_key_weight, grad_value_weight, grad_query_weight, grad_query_bias, _ = call(
@@ -931,7 +1013,7 @@
             name="last_grads",
         )
     else:
-        rows_out, _ = ffn(hidden, context, weights, (sum_done,))
+        rows_out, _ = ffn(hidden, context, matrices, (sum_done,))
         part = jnp.sum(parts.astype(F32), axis=0).astype(BF)
         whole = exchange(jnp.broadcast_to(part[None], parts.shape), batch_n).reshape(width, width)
         grad_outer_weight = t_dot(active_low, second_low)

time: 108 us -> 105 us (0.972)
  waiting for transfers between devices: 21 us -> 18.7 us
  Pallas kernels: 63 us -> 61.1 us
  starting transfers between devices: 22 us -> 23.1 us
    pallas_call x10, Pallas kernels: 63 us -> 58.6 us  [call(): pl.pallas_call(wrapped, out_shape=shapes, in_specs=spaces, out_specs=out_...]
    pallas_call x0 -> x1, Pallas kernels: none -> 2.45 us  [fetch(): pl.pallas_call(kernel, out_shape=[pltpu.VMEM(x.shape, x.dtype) for x in a...]
    ppermute x1, waiting for transfers between devices: 1.91 us -> 0.01 us  [body(): theirs = lax.ppermute(mine, 'side', CORE_SWAP)]
    all_to_all x1, waiting for transfers between devices: 2.06 us -> 0.83 us  [body(): mine = lax.all_to_all(sent, 'batch', split_axis=0, concat_axis=0)]
  transfers between devices with their start and end apart: 12 -> 12, of which waited for: 8 -> 7; matrix products, arithmetic and copies ran while one was open for 1% -> 1% of each run, Pallas kernels for 33% -> 37%
where the time goes in v1:
time: 105 us
  Pallas kernels  61.1 us (58%)
  starting transfers between devices  23.1 us (22%)
  waiting for transfers between devices  18.7 us (18%)
    pallas_call x10, Pallas kernels, call(): pl.pallas_call(wrapped, out_shape=shapes, in_specs=spaces, out_specs=out_...  58.6 us
    all_to_all x2, waiting for transfers between devices, exchange(): lax.all_to_all(sent, ('side', 'batch'), split_axis=0, concat_axis=0, axis...  11.2 us
    all_to_all x2, starting transfers between devices, exchange(): lax.all_to_all(sent, ('side', 'batch'), split_axis=0, concat_axis=0, axis...  10.6 us
    all_to_all x1, starting transfers between devices, body(): mine = lax.all_to_all(sent, 'batch', split_axis=0, concat_axis=0)  6.31 us
    ppermute x2, starting transfers between devices, near_rows(): far = lax.ppermute(own, 'side', CHIP_SWAP)  5.01 us
    pallas_call x1, Pallas kernels, fetch(): pl.pallas_call(kernel, out_shape=[pltpu.VMEM(x.shape, x.dtype) for x in a...  2.45 us
    ppermute x2, waiting for transfers between devices, near_rows(): far = lax.ppermute(own, 'side', CHIP_SWAP)  2.24 us
  transfers between devices with their start and end apart: 12, of which 7 were waited for; matrix products, arithmetic and copies ran while one was open for 1% of the time, Pallas kernels for 37%

profile of v1, /device:TPU:0, one launch (start us, length us, event | category | flops | bytes accessed | tf_op | source)
XLA Modules:
  0.0 104.5 jit_solution(6164773605175557134)
XLA Ops:
  0.7 5.2 %cls_forward.1 = (bf16[32,1024]{1,0:T(8,128)(2,1)S(1)}, bf16[32,512]{1,0:T(8,128)(2,1)}, bf16[32,1024]{1,0:T(8,128)(2,1)}, bf16[1024,512]{1,0:T(8,128)(2,1)}, bf...) custom-call(bf16[1024,512]{1,0:T(8,128)(2,1)} %bitcast.30, s32[1,1,1024]{2,1,0:T(1,128)} %refs_5_.2, ...), custom_call_target="tpu_custom_call" | custom-call | flops 1073741824 | bytes 4922644 | tf_op jit(solution)/shard_map/cls_forward/pallas_call | solution.py:188
  5.9 3.0 %collective-permute-start.1 = (bf16[32,1024]{1,0:T(8,128)(2,1)S(1)}, bf16[32,1024]{1,0:T(8,128)(2,1)S(1)}, u32[]{:S(2)}, u32[]{:S(2)}) collective-permute-start(bf16[32,1024]{1,0:T(8,128)(2,1)S(1)} %get-tuple-element.66.refs_0_), channel_id=1, source_target_pairs={{0,16},{16,0},{8,24},{24,8},{1,17},{17,1},{9,25},{25,9},{2,18},{18... | collective-permute-start | bytes 196616 | tf_op jit(solution)/shard_map/ppermute | solution.py:299
  8.9 2.2 %collective-permute-done.1.refs_2_ = bf16[32,1024]{1,0:T(8,128)(2,1)S(1)} collective-permute-done((bf16[32,1024]{1,0:T(8,128)(2,1)S(1)}, bf16[32,1024]{1,0:T(8,128)(2,1)S(1)}, u32[]{:S(2)}, u32[]{:S(2)}) %collective-permute-start.1) | collective-permute-done | bytes 65568 | tf_op jit(solution)/shard_map/ppermute | solution.py:299
  11.2 1.2 %collective-permute-done.2.refs_3_ = bf16[32,1024]{1,0:T(8,128)(2,1)S(1)} collective-permute-done((bf16[32,1024]{1,0:T(8,128)(2,1)S(1)}, bf16[32,1024]{1,0:T(8,128)(2,1)S(1)}, u32[]{:S(2)}, u32[]{:S(2)}) %collective-permute-start.2) | collective-permute-done | bytes 65568 | tf_op jit(solution)/shard_map/ppermute | solution.py:302
  12.4 1.0 half_rows.1
  13.4 6.3 %all-to-all-start = ((bf16[8,32,1024]{2,1,0:T(8,128)(2,1)}), bf16[8,32,1024]{2,1,0:T(8,128)(2,1)S(1)}, u32[]{:S(2)}, u32[]{:S(2)}) async-start(bf16[8,32,1024]{2,1,0:T(8,128)(2,1)} %get-tuple-element.68), calls=%async_computation | async-start | bytes 1048576 | tf_op jit(solution)/shard_map/all_to_all | solution.py:927
  19.7 14.0 %attention.1 = (bf16[1024,512]{1,0:T(8,128)(2,1)}, f32[8,2048]{1,0:T(8,128)}, f32[256,1024]{1,0:T(8,128)}, f32[8,128]{1,0:T(8,128)}) custom-call(bf16[1024,512]{1,0:T(8,128)(2,1)} %bitcast.31, bf16[512,512]{1,0:T(8,128)(2,1)} %refs_7_.3, f32[1,512]{1,0:T(1,128)} %bitcast.37, bf16[1024,512]{1,0:T(8,128)(2,1)} %get-tuple-element.69.refs_3_.refs_10_, ...), custom_call_target="tpu_custom_call" | custom-call | flops 8000000000 | bytes 5957632 | tf_op jit(solution)/shard_map/attention/pallas_call | solution.py:188
  33.7 0.8 all-to-all-done.refs_0_
  34.5 2.5 %fetch.1 = (bf16[512,512]{1,0:T(8,128)(2,1)S(1)}, f32[8,2048]{1,0:T(8,128)S(1)}, bf16[512,2048]{1,0:T(8,128)(2,1)S(1)}, bf16[2048,512]{1,0:T(8,128)(2,1)S(1)}) custom-call(bf16[512,512]{1,0:T(8,128)(2,1)} %refs_2_.5, f32[8,2048]{1,0:T(8,128)} %get-tuple-element.75.refs_1_.refs_3_, bf16[512,2048]{1,0:T(8,128)(2,1)} %refs_4_.3, bf16[2048,512]{1,0:T(8,128)(2,1)} %refs_5_.3, ...), custom_call_target="tpu_custom_call" | custom-call | tf_op jit(solution)/shard_map/fetch/pallas_call | solution.py:801
  37.0 11.6 %cls_middle.1 = (f32[512,512]{1,0:T(8,128)S(1)}, bf16[512,512]{1,0:T(8,128)(2,1)S(1)}, bf16[32,512]{1,0:T(8,128)(2,1)S(1)}, bf16[32,512]{1,0:T(8,128)(2,1)}, f32...) custom-call(bf16[8,32,1024]{2,1,0:T(8,128)(2,1)S(1)} %hand_on.3.refs, ...), custom_call_target="tpu_custom_call" | custom-call | flops 4831838208 | bytes 17429476 | tf_op jit(solution)/shard_map/cls_middle/pallas_call | solution.py:188
  49.1 1.5 %collective-permute-done.4.refs_1_ = bf16[512,512]{1,0:T(8,128)(2,1)S(1)} collective-permute-done((bf16[512,512]{1,0:T(8,128)(2,1)S(1)}, bf16[512,512]{1,0:T(8,128)(2,1)S(1)}, u32[]{:S(2)}, u32[]{:S(2)}) %collective-permute-start.4) | collective-permute-done | bytes 524320 | tf_op jit(solution)/shard_map/ppermute | solution.py:555
  50.7 0.9 chip_sum.1
  51.6 6.4 %all-to-all-start.1 = ((bf16[16,32,512]{2,1,0:T(8,128)(2,1)}), bf16[16,32,512]{2,1,0:T(8,128)(2,1)S(1)}, u32[]{:S(2)}, u32[]{:S(2)}) async-start(bf16[16,32,512]{2,1,0:T(8,128)(2,1)} %bitcast.11), calls=%async_computation.1 | async-start | bytes 1048576 | tf_op jit(solution)/shard_map/all_to_all | solution.py:549
  57.9 2.0 %collective-permute-start.6 = (bf16[32,512]{1,0:T(8,128)(2,1)S(1)}, bf16[32,512]{1,0:T(8,128)(2,1)S(1)}, u32[]{:S(2)}, u32[]{:S(2)}) collective-permute-start(bf16[32,512]{1,0:T(8,128)(2,1)S(1)} %get-tuple-element.86.refs_5_.refs_1_), channel_id=1, source_target_pairs={{0,16},{16,0},{8,24},{24,8},{1,17},{17,1},{9,25},{25,9},{2,18},{18... | collective-permute-start | bytes 98312 | tf_op jit(solution)/shard_map/ppermute | solution.py:299
  59.9 6.3 %weight_grads.1 = (f32[2048,512]{1,0:T(8,128)}, f32[512,2048]{1,0:T(8,128)}, f32[512,512]{1,0:T(8,128)}, bf16[512,512]{1,0:T(8,128)(2,1)}, f32[8,128]{1,0:T(8,128)}) custom-call(bf16[384,2048]{1,0:T(8,128)(2,1)} %get-tuple-element.87.refs_0_, bf16[384,512]{1,0:T(8,128)(2,1)} %get-tuple-element.88.refs_1_, bf16[384,512]{1,0:T(8,128)(2,1)} %get-tuple-element.89.refs_2_, ...), custom_call_target="tpu_custom_call" | custom-call | flops 1006632960 | bytes 15075328 | tf_op jit(solution)/shard_map/weight_grads/pallas_call | solution.py:188
  66.8 5.2 %input_grad.1 = (bf16[1024,512]{1,0:T(8,128)(2,1)}, f32[8,128]{1,0:T(8,128)}) custom-call(bf16[32,1024]{1,0:T(8,128)(2,1)} %get-tuple-element.71.refs_6_.refs_0_, bf16[256,1024]{1,0:T(8,128)(2,1)} %get-tuple-element.95.refs_1_, f32[256,1024]{1,0:T(8,128)} %get-tuple-element.80.refs_8_.refs_2_, bf16[32,512]{1,0:T(8,128)(2,1)} %get-tuple-element.96.refs_3_, ...), custom_call_target="tpu_custom_call" | custom-call | flops 1610612736 | bytes 4423680 | tf_op jit(solution)/shard_map/input_grad/pallas_call | solution.py:188
  72.1 1.3 %all-to-all-done.1.refs_0_ = bf16[16,32,512]{2,1,0:T(8,128)(2,1)S(1)} async-done(((bf16[16,32,512]{2,1,0:T(8,128)(2,1)}), bf16[16,32,512]{2,1,0:T(8,128)(2,1)S(1)}, u32[]{:S(2)}, u32[]{:S(2)}) %all-to-all-start.1) | async-done | bytes 524320 | tf_op jit(solution)/shard_map/all_to_all | solution.py:549
  73.4 1.0 add_parts.1
  74.5 4.3 %all-to-all-start.2 = ((bf16[16,48,512]{2,1,0:T(8,128)(2,1)}), bf16[16,48,512]{2,1,0:T(8,128)(2,1)S(1)}, u32[]{:S(2)}, u32[]{:S(2)}) async-start(bf16[16,48,512]{2,1,0:T(8,128)(2,1)} %get-tuple-element.102), calls=%async_computation.2 | async-start | bytes 1572864 | tf_op jit(solution)/shard_map/all_to_all | solution.py:549
  78.7 10.7 %feed_forward.1 = (bf16[1024,512]{1,0:T(8,128)(2,1)}, f32[8,128]{1,0:T(8,128)}) custom-call(bf16[1024,512]{1,0:T(8,128)(2,1)} %bitcast.33, bf16[1024,512]{1,0:T(8,128)(2,1)} %get-tuple-element.82.refs_1_, bf16[512,512]{1,0:T(8,128)(2,1)} %refs_2_.5, f32[8,2048]{1,0:T(8,128)} %get-tuple-element.75.refs_1_.refs_3_, bf16[512,2048]{1,0:T(8,128)(2,1)} %refs_4_.3, ...), custom_call_target="tpu_custom_call" | custom-call | flops 6000000000 | bytes 7929856 | tf_op jit(solution)/shard_map/feed_forward/pallas_call | solution.py:188
  89.4 9.8 %all-to-all-done.2.refs_0_ = bf16[16,48,512]{2,1,0:T(8,128)(2,1)S(1)} async-done(((bf16[16,48,512]{2,1,0:T(8,128)(2,1)}), bf16[16,48,512]{2,1,0:T(8,128)(2,1)S(1)}, u32[]{:S(2)}, u32[]{:S(2)}) %all-to-all-start.2) | async-done | bytes 786464 | tf_op jit(solution)/shard_map/all_to_all | solution.py:549
  99.3 0.6 fusion
  99.9 1.7 %collective-permute-done.8.refs_1_ = bf16[16,48,512]{2,1,0:T(8,128)(2,1)S(1)} collective-permute-done((bf16[16,48,512]{2,1,0:T(8,128)(2,1)S(1)}, bf16[16,48,512]{2,1,0:T(8,128)(2,1)S(1)}, u32[]{:S(2)}, u32[]{:S(2)}) %collective-permute-start.8) | collective-permute-done | bytes 786464 | tf_op jit(solution)/shard_map/ppermute | solution.py:1006
  101.6 2.7 %last_grads.1 = (f32[512,512]{1,0:T(8,128)}, f32[512,512]{1,0:T(8,128)}, f32[512,512]{1,0:T(8,128)}, f32[1,512]{1,0:T(1,128)}, f32[8,128]{1,0:T(8,128)}) custom-call(bf16[16,48,512]{2,1,0:T(8,128)(2,1)S(1)} %hand_on.5.refs_0_, bf16[16,48,512]{2,1,0:T(8,128)(2,1)S(1)} %collective-permute-done.8.refs_1_, bf16[512,512]{1,0:T(8,128)(2,1)} %get-tuple-element.104.refs_2_), custom_call_target="tpu_custom_call" | custom-call | bytes 5244928 | tf_op jit(solution)/shard_map/last_grads/pallas_call | solution.py:188
  (17 shorter events, 1.2 us)
Async XLA Ops:
  5.9 5.3 %collective-permute-start.1 = (bf16[32,1024]{1,0:T(8,128)(2,1)S(1)}, bf16[32,1024]{1,0:T(8,128)(2,1)S(1)}, u32[]{:S(2)}, u32[]{:S(2)}) collective-permute-start(bf16[32,1024]{1,0:T(8,128)(2,1)S(1)} %get-tuple-element.66.refs_0_), channel_id=1, source_target_pairs={{0,16},{16,0},{8,24},{24,8},{1,17},{17,1},{9,25},{25,9},{2,18},{18... | collective-permute-start | bytes 196616 | tf_op jit(solution)/shard_map/ppermute | solution.py:299
  8.9 2.3 %collective-permute-start = (bf16[32,1024]{1,0:T(8,128)(2,1)S(1)}, bf16[32,1024]{1,0:T(8,128)(2,1)S(1)}, u32[]{:S(2)}, u32[]{:S(2)}) collective-permute-start(bf16[32,1024]{1,0:T(8,128)(2,1)S(1)} %get-tuple-element.66.refs_0_), channel_id=1, source_target_pairs={{0,8},{8,0},{16,24},{24,16},{1,9},{9,1},{17,25},{25,17},{2,10},{10... | collective-permute-start | bytes 196616 | tf_op jit(solution)/shard_map/ppermute | solution.py:298
  11.2 1.3 %collective-permute-start.2 = (bf16[32,1024]{1,0:T(8,128)(2,1)S(1)}, bf16[32,1024]{1,0:T(8,128)(2,1)S(1)}, u32[]{:S(2)}, u32[]{:S(2)}) collective-permute-start(bf16[32,1024]{1,0:T(8,128)(2,1)S(1)} %collective-permute-done.1.refs_2_), channel_id=1, source_target_pairs={{0,8},{8,0},{16,24},{24,16},{1,9},{9,1},{17,25},{25,17},{2,10},{10... | collective-permute-start | bytes 196616 | tf_op jit(solution)/shard_map/ppermute | solution.py:302
  13.4 21.1 %all-to-all-start = ((bf16[8,32,1024]{2,1,0:T(8,128)(2,1)}), bf16[8,32,1024]{2,1,0:T(8,128)(2,1)S(1)}, u32[]{:S(2)}, u32[]{:S(2)}) async-start(bf16[8,32,1024]{2,1,0:T(8,128)(2,1)} %get-tuple-element.68), calls=%async_computation | async-start | bytes 1048576 | tf_op jit(solution)/shard_map/all_to_all | solution.py:927
  34.5 2.5 %collective-permute-start.3 = (bf16[8,32,1024]{2,1,0:T(8,128)(2,1)S(1)}, bf16[8,32,1024]{2,1,0:T(8,128)(2,1)S(1)}, u32[]{:S(2)}, u32[]{:S(2)}) collective-permute-start(bf16[8,32,1024]{2,1,0:T(8,128)(2,1)S(1)} %hand_on.3.refs_4_.refs_0_), channel_id=1, source_target_pairs={{0,8},{8,0},{16,24},{24,16},{1,9},{9,1},{17,25},{25,17},{2,10},{10... | collective-permute-start | bytes 1572872 | tf_op jit(solution)/shard_map/ppermute | solution.py:935
  48.6 2.1 %collective-permute-start.4 = (bf16[512,512]{1,0:T(8,128)(2,1)S(1)}, bf16[512,512]{1,0:T(8,128)(2,1)S(1)}, u32[]{:S(2)}, u32[]{:S(2)}) collective-permute-start(bf16[512,512]{1,0:T(8,128)(2,1)S(1)} %get-tuple-element.84), channel_id=1, source_target_pairs={{0,8},{8,0},{16,24},{24,16},{1,9},{9,1},{17,25},{25,17},{2,10},{10... | collective-permute-start | bytes 1572872 | tf_op jit(solution)/shard_map/ppermute | solution.py:555
  51.6 21.8 %all-to-all-start.1 = ((bf16[16,32,512]{2,1,0:T(8,128)(2,1)}), bf16[16,32,512]{2,1,0:T(8,128)(2,1)S(1)}, u32[]{:S(2)}, u32[]{:S(2)}) async-start(bf16[16,32,512]{2,1,0:T(8,128)(2,1)} %bitcast.11), calls=%async_computation.1 | async-start | bytes 1048576 | tf_op jit(solution)/shard_map/all_to_all | solution.py:549
  57.9 8.3 %collective-permute-start.6 = (bf16[32,512]{1,0:T(8,128)(2,1)S(1)}, bf16[32,512]{1,0:T(8,128)(2,1)S(1)}, u32[]{:S(2)}, u32[]{:S(2)}) collective-permute-start(bf16[32,512]{1,0:T(8,128)(2,1)S(1)} %get-tuple-element.86.refs_5_.refs_1_), channel_id=1, source_target_pairs={{0,16},{16,0},{8,24},{24,8},{1,17},{17,1},{9,25},{25,9},{2,18},{18... | collective-permute-start | bytes 98312 | tf_op jit(solution)/shard_map/ppermute | solution.py:299
  59.9 12.1 %collective-permute-start.5 = (bf16[32,512]{1,0:T(8,128)(2,1)S(1)}, bf16[32,512]{1,0:T(8,128)(2,1)S(1)}, u32[]{:S(2)}, u32[]{:S(2)}) collective-permute-start(bf16[32,512]{1,0:T(8,128)(2,1)S(1)} %get-tuple-element.86.refs_5_.refs_1_), channel_id=1, source_target_pairs={{0,8},{8,0},{16,24},{24,16},{1,9},{9,1},{17,25},{25,17},{2,10},{10... | collective-permute-start | bytes 98312 | tf_op jit(solution)/shard_map/ppermute | solution.py:298
  66.3 5.8 %collective-permute-start.7 = (bf16[32,512]{1,0:T(8,128)(2,1)S(1)}, bf16[32,512]{1,0:T(8,128)(2,1)S(1)}, u32[]{:S(2)}, u32[]{:S(2)}) collective-permute-start(bf16[32,512]{1,0:T(8,128)(2,1)S(1)} %hand_on.4.refs_3_), channel_id=1, source_target_pairs={{0,8},{8,0},{16,24},{24,16},{1,9},{9,1},{17,25},{25,17},{2,10},{10... | collective-permute-start | bytes 98312 | tf_op jit(solution)/shard_map/ppermute | solution.py:302
  74.5 24.8 %all-to-all-start.2 = ((bf16[16,48,512]{2,1,0:T(8,128)(2,1)}), bf16[16,48,512]{2,1,0:T(8,128)(2,1)S(1)}, u32[]{:S(2)}, u32[]{:S(2)}) async-start(bf16[16,48,512]{2,1,0:T(8,128)(2,1)} %get-tuple-element.102), calls=%async_computation.2 | async-start | bytes 1572864 | tf_op jit(solution)/shard_map/all_to_all | solution.py:549
  78.7 20.6 %copy-start = (f32[8,512]{1,0:T(8,128)S(1)}, f32[8,512]{1,0:T(8,128)}, u32[]{:S(2)}) copy-start(f32[8,512]{1,0:T(8,128)} %get-tuple-element.109) | copy-start | bytes 49156
  99.3 2.3 %collective-permute-start.8 = (bf16[16,48,512]{2,1,0:T(8,128)(2,1)S(1)}, bf16[16,48,512]{2,1,0:T(8,128)(2,1)S(1)}, u32[]{:S(2)}, u32[]{:S(2)}) collective-permute-start(bf16[16,48,512]{2,1,0:T(8,128)(2,1)S(1)} %hand_on.5.refs_0_), channel_id=1, source_target_pairs={{0,8},{8,0},{16,24},{24,16},{1,9},{9,1},{17,25},{25,17},{2,10},{10... | collective-permute-start | bytes 2359304 | tf_op jit(solution)/shard_map/ppermute | solution.py:1006

commit v2 on v1

--- a/solution.py
+++ b/solution.py
@@ -115,6 +115,10 @@
         return self.ref()[index]
 
 
+def ref_of(x):
+    return x.ref() if isinstance(x, Fetched) else x.buffer if isinstance(x, Result) else x
+
+
 class Result:
     def __init__(self, buffer, target, semaphores):
         self.buffer, self.target, self.semaphores = buffer, target, semaphores
@@ -136,6 +140,7 @@
 
 
 PARTS = 4
+SLABS_AT_ONCE = {384: 2, 512: 2, 768: 2}
 TOKEN = ((8, 128), F32, False)
 
 
@@ -220,24 +225,26 @@
         self.half = block // 2
         self.columns = pass_count + 1 + -(pass_count + 1) % 128
         self.count = batch_n * block
+        self.queries = batch_n * n_query
         self.quarter = block // 4
         self.slot = self.quarter + -self.quarter % 16
-        core, batch, rest = np.meshgrid(
-            np.arange(2), np.arange(batch_n), np.arange(self.half), indexing="ij"
-        )
-        place = (core * self.half + rest).reshape(-1)
-        batch = batch.reshape(-1)
-        self.code = (batch * block + place).astype(np.int32)
-        y, peer, spot = np.meshgrid(
-            np.arange(2), np.arange(batch_n), np.arange(self.slot), indexing="ij"
-        )
-        spot = np.where(spot < self.quarter, peer * self.half + y * self.quarter + spot, -1).reshape(-1)
-        self.slots = np.concatenate([spot, np.where(spot < 0, -1, spot + batch_n * self.half)])
-        self.slots = self.slots.astype(np.int32)
-        self.query = np.where(place < n_query, batch * n_query + place, -1).astype(np.int32)
+        batch, place = np.meshgrid(np.arange(batch_n), np.arange(block), indexing="ij")
         group, slot = (place - n_query) // n_pass, (place - n_query) % n_pass
-        is_pass = (place >= n_query) & (group < 3)
-        self.passage = np.where(is_pass, (group * batch_n + batch) * n_pass + slot, -1).astype(np.int32)
+        order = self.queries + (group * batch_n + batch) * n_pass + slot
+        order = np.where(place < n_query, batch * n_query + place, order)
+        order = np.where(group < 3, order, self.queries + pass_count + batch)
+        self.order = order
+        self.code = np.empty(self.count, np.int32)
+        self.code[order.reshape(-1)] = np.arange(self.count)
+
+    def landed(self):
+        halves = self.order.reshape(self.batch_n, 2, self.half).transpose(1, 0, 2)
+        return halves.reshape(-1).astype(np.int32)
+
+    def slots(self):
+        quarters = self.order.reshape(self.batch_n, 2, 2, self.quarter).transpose(1, 2, 0, 3)
+        none = np.full((2, 2, self.batch_n, self.slot - self.quarter), -1)
+        return np.concatenate([quarters, none], axis=3).reshape(-1).astype(np.int32)
 
 
 def core_chip():
@@ -270,28 +277,22 @@
     if len(refs) == 1:
         out_ref[...] = half
         return
-    full = jnp.concatenate([half, refs[0][...]], axis=0)
+    full = jnp.concatenate([half, refs[0][...]], axis=1)
     for b in range(rows.batch_n):
         out_ref[b] = full
 
 
-def teacher_terms(rows, teacher_ref, pair_ref, out_ref):
+def teacher_rows(rows, teacher_ref, pair_ref, out_ref):
     core, _ = core_chip()
-    count, told = rows.n_query // 2, teacher_ref.shape[1]
+    count, told = teacher_ref.shape
     line = iota((count, 1), 0)
     pair = jnp.zeros((count, 1), jnp.int32)
     for i in range(count):
-        pair = jnp.where(line == i, pair_ref.ref()[core * count + i], pair)
+        pair = jnp.where(line == i, pair_ref.ref()[i], pair)
     pair = jnp.broadcast_to(pair.astype(F32), (count, rows.columns - told))
-    mine = jnp.where(core == 0, teacher_ref[:count, :], teacher_ref[count:, :])
-    mine = jnp.concatenate([mine, pair], axis=1)
-    high = mine.astype(BF)
-    mid = (mine - high.astype(F32)).astype(BF)
-    low = (mine - high.astype(F32) - mid.astype(F32)).astype(BF)
-    terms = jnp.concatenate([high, mid, low], axis=1)
-    side = out_ref.shape[1] // 2
-    terms = jnp.concatenate([terms, jnp.zeros((count, side - terms.shape[1]), BF)], axis=1)
-    out_ref[...] = jnp.concatenate([terms[: count // 2], terms[count // 2 :]], axis=1)
+    whole = jnp.concatenate([teacher_ref[...], pair], axis=1).astype(BF)
+    place = iota((rows.half, 1), 0) + core * rows.half
+    out_ref[...] = take_rows(jnp.where(place < count, place, -1), (whole,))
 
 
 def near_rows(own, *tokens):
@@ -308,19 +309,18 @@
     )
 
 
-def cls_probs(pick, query, key_ref, seg_ref):
+def softmax_of(scores, pick, seg_ref):
     seg = seg_ref[0].astype(F32)
     cls_seg = jnp.sum(jnp.where(pick, seg, 0.0), axis=1, keepdims=True)
     bias = jnp.where(cls_seg == seg, 0.0, NEG_FILL)
-    scores = dot_t(spread_heads(query) * BF(HD**-0.5), key_ref[...])
     scores = scores + jnp.concatenate([bias] * HEADS, axis=0)
     expo = jnp.exp(scores - jnp.max(scores, axis=1, keepdims=True))
     return expo / jnp.sum(expo, axis=1, keepdims=True)
 
 
 def cls_forward_kernel(
-    rows, with_terms, x_ref, seg_ref, query_cls_ref, pass_cls_ref, wq_ref, bq_ref, wk_ref, wv_ref, bv_ref,
-    teacher_ref, pair_ref, rows_ref, query_ref, pick_ref, key_ref, value_ref, terms_ref,
+    rows, with_teacher, x_ref, seg_ref, query_cls_ref, pass_cls_ref, wq_ref, bq_ref, wk_ref, wv_ref, bv_ref,
+    teacher_ref, pair_ref, rows_ref, query_ref, pick_ref, told_ref, key_ref,
 ):
     n_pass = rows.n_pass
     side = lax.axis_index("side")
@@ -328,56 +328,47 @@
     slot = iota((n_query, 1), 0)
     cls = jnp.full((n_query, 1), -1, jnp.int32)
     for i in range(n_query):
-        place = jnp.where(side == 0, query_cls_ref.ref()[0, i], pass_cls_ref.ref()[0, 0, i] if i < n_pass else -1)
+        first = query_cls_ref.ref()[0, i]
+        place = jnp.where(side == 0, first, pass_cls_ref.ref()[0, 0, i] if i < n_pass else -1)
         cls = jnp.where(slot == i, place, cls)
     pick = iota((n_query, x_ref.shape[0]), 1) == cls
     pick_low = jnp.where(pick, 1.0, 0.0).astype(BF)
     pick_ref[...] = pick_low
     pick_ref.flush()
-    if with_terms:
-        teacher_terms(rows, teacher_ref, pair_ref, terms_ref)
-    for i in range(PARTS):
-        part = slice(i * x_ref.size, i * x_ref.size + x_ref.size)
-        key_ref[part, :] = dot(x_ref.part(i), wk_ref[...]).astype(BF)
+    if with_teacher:
+        teacher_rows(rows, teacher_ref, pair_ref, told_ref)
+    key_ref[...] = dot(x_ref[...], wk_ref[...]).astype(BF)
     key_ref.flush()
-    x = x_ref.ref()
-    value_ref[...] = (dot(x[...], wv_ref[...]) + bv_ref[...]).astype(BF)
-    value_ref.flush()
-    tokens = dot(pick_low, x[...]).astype(BF)
+    tokens = dot(pick_low, x_ref[...]).astype(BF)
     query = (dot(tokens, wq_ref[...]) + bq_ref[...]).astype(BF)
     query_ref[...] = query
     query_ref.flush()
-    probs = cls_probs(pick, query, key_ref, seg_ref)
-    rows_ref[:, :width] = fold_heads(dot(probs.astype(BF), value_ref[...])).astype(BF)
     rows_ref[:, width:] = tokens
+    probs = softmax_of(dot_t(spread_heads(query) * BF(HD**-0.5), key_ref[...]), pick, seg_ref)
+    mixed = dot(probs.astype(BF), x_ref[...])
+    high = mixed.astype(BF)
+    rest = (mixed - high.astype(F32)).astype(BF)
+    context = fold_heads(dot(high, wv_ref[...]) + dot(rest, wv_ref[...])) + bv_ref[...]
+    rows_ref[:, :width] = context.astype(BF)
 
 
 def middle_kernel(
     rows, pass_count,
-    mine_ref, theirs_ref, wo_ref, vector_ref, wi_ref, wu_ref, at_ref, value_ref, probs_ref, x_ref, key_ref, query_ref, cluster_ref,
+    mine_ref, theirs_ref, wo_ref, vector_ref, wi_ref, wu_ref, code_ref, landed_ref, value_ref, probs_ref, x_ref, key_ref, query_ref, cluster_ref,
     keep_ref, give_ref, low_ref, context_ref, gown_ref, scores_ref,
     loss_ref, small_ref, inner_bias_ref,
-    both_ref, first_ref, active_ref, pre_ref, second_ref, attended_ref, slope_ref, told_ref,
+    both_ref, first_ref, active_ref, pre_ref, second_ref, attended_ref, slope_ref,
 ):
     width = wo_ref.shape[0]
     bo_ref, g1_ref, s1_ref, bu_ref, g2_ref, s2_ref, bi_ref = vectors_of(vector_ref, width)
-    n_queries, n_columns = told_ref.shape
+    n_queries, n_columns = rows.queries, rows.columns
     chunk = wi_ref.shape[1] // PARTS
     side, batch = lax.axis_index("side"), lax.axis_index("batch")
     core = side % 2
-    code_at, query_at, pass_at = at_ref[0:1, :], at_ref[1:2, :], at_ref[2:3, :]
-    count = rows.n_query // 2
-    for half in range(2):
-        for b in range(rows.batch_n):
-            one = jnp.where(core == half, mine_ref[b], theirs_ref[b])
-            first_row = (half * rows.batch_n + b) * rows.half
-            both_ref[first_row : first_row + rows.half, :] = one[: rows.half]
-            terms = one[rows.half :].astype(F32)
-            for part in range(2):
-                begin = part * one.shape[1] // 2
-                cut = [terms[:, begin + k * n_columns : begin + (k + 1) * n_columns] for k in range(3)]
-                row = b * rows.n_query + half * count + part * count // 2
-                told_ref[row : row + count // 2, :] = cut[0] + cut[1] + cut[2]
+    order = one_hot(rows.count, rows.count, landed_ref[...])
+    placed = dot(order, join_halves(core, mine_ref[...], theirs_ref[...]))
+    both_ref[...] = placed[:, : 2 * width].astype(BF)
+    told = placed[: rows.queries, 2 * width :]
     attended = both_ref[:, width:].astype(F32) + (dot(both_ref[:, :width], wo_ref[...]) + bo_ref[...])
     first_hat, first_inv = norm_stats(attended)
     for ref in (value_ref, probs_ref, x_ref, key_ref, query_ref):
@@ -401,20 +392,16 @@
     final = (second_hat * g2_ref[...] + s2_ref[...]).astype(BF)
 
     scale = width ** (-0.5)
-    query_pick = one_hot(n_queries, rows.count, query_at)
-    pass_pick = one_hot(n_columns, rows.count, pass_at)
-    query_vec = dot(query_pick, final).astype(BF)
-    pass_vec = dot(pass_pick, final).astype(BF)
+    query_vec, pass_vec = final[:n_queries], final[n_queries:]
     score = dot_t(query_vec, pass_vec) * scale
     column = iota((n_queries, n_columns), 1)
-    is_pair = column == told_ref[:, n_columns - 1 :].astype(jnp.int32)
-    cluster = jnp.full((1, n_columns), -1.0, F32)
-    for j in range(pass_count):
-        cluster = jnp.where(column[:1] == j, cluster_ref.ref()[j].astype(F32), cluster)
+    is_pair = column == told[:, n_columns - 1 :].astype(jnp.int32)
+    none = jnp.full((1, n_columns - pass_count), -1.0, F32)
+    cluster = jnp.concatenate([cluster_ref[...].astype(F32), none], axis=1)
     query_cluster = jnp.sum(jnp.where(is_pair, cluster, 0.0), axis=1, keepdims=True)
     counted = (cluster == query_cluster) & jnp.logical_not(is_pair) & (column < pass_count)
     pair_score = jnp.sum(jnp.where(is_pair, score, 0.0), axis=1, keepdims=True)
-    resid = jnp.where(counted, pair_score - score - told_ref[...], 0.0)
+    resid = jnp.where(counted, pair_score - score - told, 0.0)
     squares = jnp.sum(jnp.sum(resid * resid, axis=1, keepdims=True), axis=0, keepdims=True)
     pairs = jnp.where(counted, 1.0, 0.0)
     pairs = jnp.sum(jnp.sum(pairs, axis=1, keepdims=True), axis=0, keepdims=True)
@@ -422,8 +409,7 @@
     loss_ref.flush()
     grad_score = jnp.where(is_pair, jnp.sum(resid, axis=1, keepdims=True), 0.0) - resid
     grad_low = (grad_score * scale).astype(BF)
-    grad_rows = dot(t_dot(query_pick, grad_low).astype(BF), pass_pick).astype(BF)
-    grad_final = dot(grad_rows, final) + t_dot(grad_rows, final)
+    grad_final = jnp.concatenate([dot(grad_low, pass_vec), t_dot(grad_low, query_vec)], axis=0)
 
     def note(at, value):
         small_ref[at : at + 1, :] = jnp.sum(value, axis=0, keepdims=True)
@@ -461,7 +447,7 @@
     slot = iota((rows.n_query, 1), 0)
     base = batch * rows.block + jnp.where(side == 0, 0, rows.n_query + rows.n_pass * (side - 1))
     live = slot < jnp.where(side == 0, rows.n_query, rows.n_pass)
-    own = (code_at == base + slot) & live
+    own = (code_ref[...] == base + slot) & live
     high = grad_attended.astype(BF)
     rest = (grad_attended - high.astype(F32)).astype(BF)
     own = jnp.where(own, 1.0, 0.0).astype(BF)
@@ -597,22 +583,14 @@
 
 
 def attention_kernel(
-    tile, sizes, x_ref, wq_ref, bq_ref, key_ref, value_ref, seg_ref, *refs
+    tile, tiles, sizes, x_ref, wq_ref, bq_ref, key_ref, value_ref, seg_ref, out_ref, q_scr, bias_scr
 ):
-    pick_ref, query_ref = refs[:2]
-    out_ref, vector_ref, probs_ref, q_scr, bias_scr = refs[-5:]
     count = x_ref.shape[0]
-    x, wq, bq, seg = x_ref.ref(), wq_ref.ref(), bq_ref[...], seg_ref[0]
+    x, wq, bq, seg = ref_of(x_ref), ref_of(wq_ref), bq_ref[...], seg_ref[0]
     places = iota((1, count), 1)
-    keys, values = key_ref.ref(), value_ref.ref()
-
-    for i, ref in enumerate(refs[2:-5]):
-        vector_ref[i : i + 1, : ref.shape[1]] = ref[...]
-    vector_ref.flush()
-    probs_ref[...] = cls_probs(pick_ref[...].astype(F32) > 0.5, query_ref[...], key_ref, seg_ref)
-    probs_ref.flush()
-
-    @pl.loop(0, count // tile)
+    keys, values, seg_whole = ref_of(key_ref), ref_of(value_ref), ref_of(seg_ref)
+
+    @pl.loop(*tiles)
     def _(i):
         row = pl.multiple_of(i * tile, tile)
         q = (dot(x[pl.ds(row, tile), :], wq[...]) + bq).astype(BF)
@@ -621,7 +599,7 @@
         last = jnp.max(jnp.where(places == row + (tile - 1), seg, -2))
         low = jnp.min(jnp.where(seg == first, places, count)) // 128 * 128
         high = jnp.max(jnp.where(seg == last, places, -1)) + 1
-        own = seg_ref.ref()[0, :, pl.ds(row, tile)].astype(F32)
+        own = seg_whole[0, :, pl.ds(row, tile)].astype(F32)
         own = column_of(own)
         before = jnp.int32(0)
         for size in sizes:
@@ -631,60 +609,107 @@
             @pl.when(jnp.logical_and(before == 0, fits))
             def _(size=size, start=start):
                 at = pl.multiple_of(start, 128)
-                near = seg_ref.ref()[0, :, pl.ds(at, size)].astype(F32)
+                near = seg_whole[0, :, pl.ds(at, size)].astype(F32)
                 bias_scr[:, :size] = jnp.where(own == near, 0.0, NEG_FILL)
                 half = iota((1, 2 * HD), 1) // HD
-                slabs = [slice(h // 2 * 2 * HD, h // 2 * 2 * HD + 2 * HD) for h in range(HEADS)]
-                scores = [
-                    dot_t(
-                        jnp.where(half == h % 2, q_scr[:, slabs[h]], BF(0)),
-                        keys[pl.ds(at, size), slabs[h]],
-                    )
-                    + bias_scr[:, :size]
-                    for h in range(HEADS)
-                ]
-                expos = [jnp.exp(s - jnp.max(s, axis=1, keepdims=True)).astype(BF) for s in scores]
-                outs = []
-                for h in range(HEADS):
-                    ones = jnp.where(half == h % 2, values[pl.ds(at, size), slabs[h]], BF(1))
-                    mixed = dot(expos[h], ones)
-                    outs.append(mixed / pltpu.roll(mixed, HD, 1))
-                for h in range(0, HEADS, 2):
-                    out_ref.buffer[pl.ds(row, tile), slabs[h]] = jnp.where(
-                        half == 0, outs[h], outs[h + 1]
-                    ).astype(BF)
+                here = pl.ds(row - tiles[0] * tile, tile)
+
+                def heads(first):
+                    slabs = [pl.ds(first + k * 2 * HD, 2 * HD) for k in range(together)]
+                    both = [(slab, h) for slab in slabs for h in range(2)]
+                    scores = [
+                        dot_t(jnp.where(half == h, q_scr[:, slab], BF(0)), keys[pl.ds(at, size), slab])
+                        + bias_scr[:, :size]
+                        for slab, h in both
+                    ]
+                    expos = [jnp.exp(s - jnp.max(s, axis=1, keepdims=True)).astype(BF) for s in scores]
+                    outs = []
+                    for (slab, h), expo in zip(both, expos):
+                        mixed = dot(expo, jnp.where(half == h, values[pl.ds(at, size), slab], BF(1)))
+                        outs.append(mixed / pltpu.roll(mixed, HD, 1))
+                    for k, slab in enumerate(slabs):
+                        out = jnp.where(half == 0, outs[2 * k], outs[2 * k + 1])
+                        out_ref.buffer[here, slab] = out.astype(BF)
+
+                together = SLABS_AT_ONCE.get(size, 1 if size > 512 else HEADS // 2)
+                if together == HEADS // 2:
+                    heads(0)
+                else:
+
+                    @pl.loop(0, HEADS // 2 // together)
+                    def _(j):
+                        heads(pl.multiple_of(j * (together * 2 * HD), together * 2 * HD))
 
             before = jnp.where(fits, 1, before)
 
 
-def attention(x, wq, bq, keys, values, seg, pick, query, vectors, after, tile=256):
+def window_sizes(count):
+    return [size for size in (384, 512, 768) if size < count] + [count]
+
+
+def first_attention_kernel(
+    tile, tiles, x_ref, key_ref, wv_ref, bv_ref, wq_ref, bq_ref, seg_ref, pick_ref, query_ref, *refs
+):
+    out_ref, value_ref, probs_ref, vector_ref, q_scr, bias_scr = refs[-6:]
+    value_ref[...] = (dot(x_ref[...], wv_ref[...]) + bv_ref[...]).astype(BF)
+    value_ref.flush()
+    scores = dot_t(spread_heads(query_ref[...]) * BF(HD**-0.5), key_ref[...])
+    probs_ref[...] = softmax_of(scores, pick_ref[...].astype(F32) > 0.5, seg_ref)
+    probs_ref.flush()
+    for i, ref in enumerate(refs[:-6]):
+        vector_ref[i : i + 1, : ref.shape[1]] = ref[...]
+    vector_ref.flush()
+    sizes = window_sizes(x_ref.shape[0])
+    attention_kernel(
+        tile, tiles, sizes, x_ref, wq_ref, bq_ref, key_ref, value_ref, seg_ref, out_ref, q_scr, bias_scr
+    )
+
+
+def first_attention(x, keys, wv, bv, wq, bq, seg, pick, query, vectors, after, share, tile=256):
     t, d = x.shape
-    sizes = [s for s in (384, 512, 768) if s < t] + [t]
     return call(
-        functools.partial(attention_kernel, tile, sizes),
+        functools.partial(first_attention_kernel, tile, (0, share // tile)),
         [
+            ((share, d), BF, False),
             ((t, d), BF, False),
+            ((HEADS * query.shape[0], t), F32, False),
             ((8, vectors[-1].shape[1]), F32, False),
-            ((HEADS * query.shape[0], t), F32, False),
         ],
-        (x, wq, bq, keys, values, seg, pick, query) + vectors,
-        flops=8 * 10**9,
-        far=range(8 + len(vectors)),
+        (x, keys, wv, bv, wq, bq, seg, pick, query) + vectors,
+        flops=6 * 10**9,
+        far=range(9 + len(vectors)),
+        scratch=[pltpu.VMEM((tile, d), BF), pltpu.VMEM((tile, t), F32)],
+        limit=24,
+        after=after,
+        name="first_attention",
+    )
+
+
+def rest_attention(x, wq, bq, keys, values, seg, after, share, tile=256):
+    t, d = x.shape
+    return call(
+        functools.partial(attention_kernel, tile, (share // tile, t // tile), window_sizes(t)),
+        [((t - share, d), BF, False)],
+        (x, wq, bq, keys, values, seg),
+        flops=4 * 10**9,
+        far=range(6),
         scratch=[pltpu.VMEM((tile, d), BF), pltpu.VMEM((tile, t), F32)],
         limit=20,
         after=after,
-        name="attention",
+        name="rest_attention",
     )
 
 
 def ffn_kernel(
-    tile, x_ref, c_ref, wo_ref, vector_ref, wi_ref, wu_ref, out_ref,
+    tile, x_ref, first_ref, rest_ref, wo_ref, vector_ref, wi_ref, wu_ref, out_ref,
 ):
     bo_ref, g1_ref, s1_ref, bu_ref, g2_ref, s2_ref, bi_ref = vectors_of(vector_ref, x_ref.shape[1])
     chunk = wi_ref.size
     for t in range(0, x_ref.shape[0], tile):
         part = slice(t, t + tile)
-        attended = x_ref[part, :].astype(F32) + (dot(c_ref[part, :], wo_ref[...]) + bo_ref[...])
+        share = first_ref.shape[0]
+        near = first_ref[part, :] if t < share else rest_ref[t - share : t - share + tile, :]
+        attended = x_ref[part, :].astype(F32) + (dot(near, wo_ref[...]) + bo_ref[...])
         first = norm_stats(attended)[0] * g1_ref[...] + s1_ref[...]
         first_low = first.astype(BF)
         second = first + bu_ref[...]
@@ -699,11 +724,11 @@
     return call(
         functools.partial(ffn_kernel, tile),
         [(x.shape, BF, False)],
-        (x, context) + weights,
+        (x,) + context + weights,
         flops=6 * 10**9,
-        far=range(6),
+        far=range(7),
         limit=20,
-        split={4: (1, PARTS), 5: (0, PARTS)},
+        split={5: (1, PARTS), 6: (0, PARTS)},
         after=after,
         name="feed_forward",
     )
@@ -713,7 +738,7 @@
     rows, pass_count, core, mine, theirs, told, cluster, wo, bo, g1, s1, wi, bi, wu, bu, g2, s2
 ):
     width = wo.shape[0]
-    both = join_halves(core, mine, theirs)
+    both = join_halves(core, mine, theirs)[np.argsort(rows.landed())]
     attended = both[:, width:].astype(F32) + (dot(both[:, :width], wo) + bo)
     first_hat, first_inv = norm_stats(attended)
     first = first_hat * g1 + s1
@@ -723,9 +748,7 @@
     second = first + (dot(active_low, wu) + bu)
     second_hat, second_inv = norm_stats(second)
     final = (second_hat * g2 + s2).astype(BF)
-    order_q = np.argsort(rows.query, kind="stable")[-rows.batch_n * rows.n_query :]
-    order_p = np.argsort(rows.passage, kind="stable")[-pass_count:]
-    query_vec, pass_vec = final[order_q], final[order_p]
+    query_vec, pass_vec = final[: rows.queries], final[rows.queries : rows.queries + pass_count]
     scale = width ** (-0.5)
     score = dot_t(query_vec, pass_vec) * scale
     is_pair = iota(score.shape, 1) == told[:, pass_count:].astype(jnp.int32)
@@ -736,9 +759,8 @@
     loss = jnp.sum(resid * resid) / jnp.maximum(jnp.sum(counted.astype(F32)), 1.0)
     grad_score = jnp.where(is_pair, jnp.sum(resid, axis=1, keepdims=True), 0.0) - resid
     grad_low = (grad_score * scale).astype(BF)
-    grad_final = jnp.zeros((rows.count, width), F32)
-    grad_final = grad_final.at[order_q].set(dot(grad_low, pass_vec))
-    grad_final = grad_final.at[order_p].set(t_dot(grad_low, query_vec))
+    none = jnp.zeros((rows.count - rows.queries - pass_count, width), F32)
+    grad_final = jnp.concatenate([dot(grad_low, pass_vec), t_dot(grad_low, query_vec), none], axis=0)
     grad_second = norm_back(grad_final, second_hat, second_inv, g2)
     second_low = grad_second.astype(BF)
     grad_pre = dot_t(second_low, wu) * slope
@@ -813,8 +835,9 @@
     width, ff = weights[2].shape
     count = rows.count
     keys, values, cls_query, probs = kept
-    at = np.stack([rows.code, rows.query, rows.passage])
-    ins = (mine, theirs) + weights + (at, values, probs, hidden, keys, cls_query, cluster)
+    landed = rows.landed()
+    ins = (mine, theirs) + weights
+    ins += (rows.code[None, :], landed[None, :], values, probs, hidden, keys, cls_query, cluster[None, :])
     outs = [
         ((width, width), F32, True), ((width, width), BF, True), ((rows.n_query, width), BF, True),
         ((rows.n_query, width), BF, False), ((rows.n_query, width), F32, False), (probs.shape, BF, False),
@@ -827,13 +850,9 @@
         outs,
         ins,
         flops=12 * count * width * ff,
-        scratch=[
-            pltpu.VMEM((count, ff), F32),
-            pltpu.VMEM((rows.batch_n * rows.n_query, rows.columns), F32),
-        ],
-        far=range(6, len(ins)),
-        smem=(len(ins) - 1,),
-        late=range(7, len(ins) - 1),
+        scratch=[pltpu.VMEM((count, ff), F32)],
+        far=(7, 6) + tuple(range(8, len(ins))),
+        late=range(8, len(ins) - 1),
         limit=32,
         after=after,
         name="cls_middle",
@@ -882,28 +901,24 @@
         out_weight, vec(out_bias), vec(first_gain), vec(first_shift), inner_weight, vec(inner_bias),
         outer_weight, vec(outer_bias), vec(second_gain), vec(second_shift),
     )
-    small_case = rows.count <= 512 and 3 * rows.columns <= width and n_query % 32 == 0
-
-    token = ((count_tok, width), BF, False)
-    extra = n_query // 4 if small_case else 8
-    own, cls_query, pick, keys, values, terms, _ = call(
+    small_case = rows.count <= 512 and rows.columns == 128 and count_tok % 512 == 0
+
+    own, cls_query, pick, told, keys, _ = call(
         functools.partial(cls_forward_kernel, rows, small_case),
         [
             ((n_query, 2 * width), BF, True),
             ((n_query, width), BF, False),
             ((n_query, count_tok), BF, False),
-            token,
-            token,
-            ((extra, 2 * width), BF, True),
+            ((rows.half, rows.columns), BF, True),
+            ((count_tok, width), BF, False),
         ],
         (
             hidden, segments, query_cls, passage_cls, query_weight, vec(query_bias), key_weight,
             value_weight, vec(value_bias), teacher, pair_passage,
         ),
-        flops=4 * count_tok * width * width,
-        far=(6, 0, 9, 7, 1, 4, 5, 8),
+        flops=2 * count_tok * width * width,
+        far=(6, 0, 4, 1, 5, 9, 7, 8),
         smem=(2, 3, 10),
-        split={0: (0, PARTS)},
         limit=24,
         name="cls_forward",
     )
@@ -912,8 +927,8 @@
     if small_case:
         sent, half_done = call(
             functools.partial(half_kernel, rows),
-            [((batch_n, rows.half + extra, 2 * width), BF, True)],
-            near + (terms,),
+            [((batch_n, rows.half, 2 * width + rows.columns), BF, True)],
+            near + (told,),
             name="half_rows",
         )
     else:
@@ -926,8 +941,10 @@
         sent = jnp.broadcast_to(half[None], (batch_n,) + half.shape)
     mine = lax.all_to_all(sent, "batch", split_axis=0, concat_axis=0)
     vectors = (weights[1], weights[2], weights[3], weights[7], weights[8], weights[9], weights[5])
-    context, vectors, probs, attention_done = attention(
-        hidden, query_weight, vec(query_bias), keys, values, segments, pick, cls_query, vectors, (half_done,)
+    share = count_tok // 2
+    first_context, values, probs, vectors, attention_done = first_attention(
+        hidden, keys, value_weight, vec(value_bias), query_weight, vec(query_bias), segments, pick,
+        cls_query, vectors, (half_done,), share,
     )
     matrices = (out_weight, vectors, inner_weight, outer_weight)
     if small_case:
@@ -936,11 +953,13 @@
 
     if small_case:
         kept = (keys, values, cls_query, probs)
+        flat = (batch_n * rows.half, mine.shape[2])
         (
             keep, give, query_low, own_context, own_attended, grad_scores, loss, small, grad_inner_bias,
             both, first_low, active_low, pre_low, second_low, attended_low, _,
         ) = middle(
-            rows, pass_count, mine, theirs, kept, tuple(fetch(matrices, mine)), passage_cluster, hidden, ()
+            rows, pass_count, mine.reshape(flat), theirs.reshape(flat), kept, tuple(fetch(matrices, mine)),
+            passage_cluster, hidden, (),
         )
     else:
         told = jnp.concatenate([teacher, pair_passage[:, None].astype(F32)], axis=1)
@@ -976,14 +995,14 @@
     )
     peers, size = parts.shape[:2]
     if small_case and size % 16 == 0:
-        saved = (active_low, second_low, first_low, pre_low, both, attended_low, rows.slots[None, :])
+        saved = (active_low, second_low, first_low, pre_low, both, attended_low, rows.slots()[None, :])
         grad_outer_weight, grad_inner_weight, grad_out_weight, all_tokens, weight_done = call(
             weight_grads_kernel,
             [
                 (outer_weight.shape, F32, False),
                 (inner_weight.shape, F32, False),
                 (out_weight.shape, F32, False),
-                ((rows.slots.shape[0], width), BF, False),
+                ((4 * rows.batch_n * rows.slot, width), BF, False),
             ],
             saved,
             flops=2 * rows.count * width * (4 * width + width),
@@ -1001,7 +1020,10 @@
             name="add_parts",
         )
         whole = exchange(sent, batch_n)
-        rows_out, ffn_done = ffn(hidden, context, matrices, (add_done,))
+        rest_context, _ = rest_attention(
+            hidden, query_weight, vec(query_bias), keys, values, segments, (add_done,), share
+        )
+        rows_out, ffn_done = ffn(hidden, (first_context, rest_context), matrices, (add_done,))
         whole = behind(whole, ffn_done)
         other = lax.ppermute(whole, "side", CORE_SWAP)
         grad_key_weight, grad_value_weight, grad_query_weight, grad_query_bias, _ = call(
@@ -1013,7 +1035,10 @@
             name="last_grads",
         )
     else:
-        rows_out, _ = ffn(hidden, context, matrices, (sum_done,))
+        rest_context, _ = rest_attention(
+            hidden, query_weight, vec(query_bias), keys, values, segments, (sum_done,), share
+        )
+        rows_out, _ = ffn(hidden, (first_context, rest_context), matrices, (sum_done,))
         part = jnp.sum(parts.astype(F32), axis=0).astype(BF)
         whole = exchange(jnp.broadcast_to(part[None], parts.shape), batch_n).reshape(width, width)
         grad_outer_weight = t_dot(active_low, second_low)
@@ -1029,7 +1054,7 @@
         half = jnp.broadcast_to(half[None], (batch_n,) + half.shape)
         low_mine = lax.all_to_all(half, "batch", split_axis=0, concat_axis=0).reshape(flat)
         low_theirs = lax.ppermute(low_mine, "side", CORE_SWAP)
-        all_low = join_halves(side % 2, low_mine, low_theirs)
+        all_low = join_halves(side % 2, low_mine, low_theirs)[np.argsort(rows.landed())]
         grad_query_weight = t_dot(both[:, width:], all_low)
         grad_query_bias = jnp.sum(all_low.astype(F32), axis=0)
         other = lax.ppermute(whole, "side", CORE_SWAP)

time: 105 us -> 101 us (0.962)
  waiting for transfers between devices: 18.7 us -> 12 us
  Pallas kernels: 61.1 us -> 65.3 us
  starting transfers between devices: 23.1 us -> 21.3 us
    all_to_all x2, waiting for transfers between devices: 11.2 us -> 1.78 us  [exchange(): lax.all_to_all(sent, ('side', 'batch'), split_axis=0, concat_axis=0, axis...]
    pallas_call x10 -> x11, Pallas kernels: 58.6 us -> 62.9 us  [call(): pl.pallas_call(wrapped, out_shape=shapes, in_specs=spaces, out_specs=out_...]
    all_to_all x1, waiting for transfers between devices: 0.83 us -> 3.52 us  [body(): mine = lax.all_to_all(sent, 'batch', split_axis=0, concat_axis=0)]
    all_to_all x2, starting transfers between devices: 10.6 us -> 8.88 us  [exchange(): lax.all_to_all(sent, ('side', 'batch'), split_axis=0, concat_axis=0, axis...]
  transfers between devices with their start and end apart: 12 -> 12, of which waited for: 7 -> 7; matrix products, arithmetic and copies ran while one was open for 1% -> 1% of each run, Pallas kernels for 37% -> 43%
where the time goes in v2:
time: 101 us; the launch traced here: 100 us
  Pallas kernels  65.3 us (65%)
  starting transfers between devices  21.3 us (21%)
  waiting for transfers between devices  12 us (12%)
    pallas_call x11, Pallas kernels, call(): pl.pallas_call(wrapped, out_shape=shapes, in_specs=spaces, out_specs=out_...  62.9 us
    all_to_all x2, starting transfers between devices, exchange(): lax.all_to_all(sent, ('side', 'batch'), split_axis=0, concat_axis=0, axis...  8.88 us
    all_to_all x1, starting transfers between devices, body(): mine = lax.all_to_all(sent, 'batch', split_axis=0, concat_axis=0)  6.31 us
    ppermute x2, starting transfers between devices, near_rows(): far = lax.ppermute(own, 'side', CHIP_SWAP)  4.96 us
    all_to_all x1, waiting for transfers between devices, body(): mine = lax.all_to_all(sent, 'batch', split_axis=0, concat_axis=0)  3.52 us
    pallas_call x1, Pallas kernels, fetch(): pl.pallas_call(kernel, out_shape=[pltpu.VMEM(x.shape, x.dtype) for x in a...  2.45 us
    ppermute x2, waiting for transfers between devices, near_rows(): far = lax.ppermute(own, 'side', CHIP_SWAP)  2.24 us
  transfers between devices with their start and end apart: 12, of which 7 were waited for; matrix products, arithmetic and copies ran while one was open for 1% of the time, Pallas kernels for 43%

profile of v2, /device:TPU:0, one launch (start us, length us, event | category | flops | bytes accessed | tf_op | source)
XLA Modules:
  0.0 100.3 jit_solution(4565940185670001078)
XLA Ops:
  0.7 4.7 %cls_forward.1 = (bf16[32,1024]{1,0:T(8,128)(2,1)S(1)}, bf16[32,512]{1,0:T(8,128)(2,1)}, bf16[32,1024]{1,0:T(8,128)(2,1)}, bf16[24,128]{1,0:T(8,128)(2,1)S(1)}, ...) custom-call(bf16[1024,512]{1,0:T(8,128)(2,1)} %bitcast.28, s32[1,1,1024]{2,1,0:T(1,128)} %refs_5_.2, s32[1,32]{1,0:T(1,128)} %refs_2_.3, ...), custom_call_target="tpu_custom_call" | custom-call | flops 536870912 | bytes 3863828 | tf_op jit(solution)/shard_map/cls_forward/pallas_call | solution.py:193
  5.4 3.0 %collective-permute-start.1 = (bf16[32,1024]{1,0:T(8,128)(2,1)S(1)}, bf16[32,1024]{1,0:T(8,128)(2,1)S(1)}, u32[]{:S(2)}, u32[]{:S(2)}) collective-permute-start(bf16[32,1024]{1,0:T(8,128)(2,1)S(1)} %get-tuple-element.67.refs_0_), channel_id=1, source_target_pairs={{0,16},{16,0},{8,24},{24,8},{1,17},{17,1},{9,25},{25,9},{2,18},{18... | collective-permute-start | bytes 196616 | tf_op jit(solution)/shard_map/ppermute | solution.py:300
  8.4 2.2 %collective-permute-done.1.refs_2_ = bf16[32,1024]{1,0:T(8,128)(2,1)S(1)} collective-permute-done((bf16[32,1024]{1,0:T(8,128)(2,1)S(1)}, bf16[32,1024]{1,0:T(8,128)(2,1)S(1)}, u32[]{:S(2)}, u32[]{:S(2)}) %collective-permute-start.1) | collective-permute-done | bytes 65568 | tf_op jit(solution)/shard_map/ppermute | solution.py:300
  10.7 1.2 %collective-permute-done.2.refs_3_ = bf16[32,1024]{1,0:T(8,128)(2,1)S(1)} collective-permute-done((bf16[32,1024]{1,0:T(8,128)(2,1)S(1)}, bf16[32,1024]{1,0:T(8,128)(2,1)S(1)}, u32[]{:S(2)}, u32[]{:S(2)}) %collective-permute-start.2) | collective-permute-done | bytes 65568 | tf_op jit(solution)/shard_map/ppermute | solution.py:303
  11.9 0.9 half_rows.1
  12.9 6.3 %all-to-all-start = ((bf16[8,24,1152]{2,1,0:T(8,128)(2,1)}), bf16[8,24,1152]{2,1,0:T(8,128)(2,1)S(1)}, u32[]{:S(2)}, u32[]{:S(2)}) async-start(bf16[8,24,1152]{2,1,0:T(8,128)(2,1)} %get-tuple-element.69), calls=%async_computation | async-start | bytes 884736 | tf_op jit(solution)/shard_map/all_to_all | solution.py:942
  19.2 9.5 %first_attention.1 = (bf16[512,512]{1,0:T(8,128)(2,1)}, bf16[1024,512]{1,0:T(8,128)(2,1)}, f32[256,1024]{1,0:T(8,128)}, f32[8,2048]{1,0:T(8,128)}, f32[8,128]{1,0:T(8,128)}) custom-call(bf16[1024,512]{1,0:T(8,128)(2,1)} %bitcast.29, bf16[1024,512]{1,0:T(8,128)(2,1)} %get-tuple-element.70.refs_1_.refs_11_.refs_3_, bf16[512,512]{1,0:T(8,128)(2,1)} %refs_9_.3, ...), custom_call_target="tpu_custom_call" | custom-call | flops 6000000000 | bytes 5959680 | tf_op jit(solution)/shard_map/first_attention/pallas_call | solution.py:193
  28.7 3.5 %all-to-all-done.refs_0_ = bf16[8,24,1152]{2,1,0:T(8,128)(2,1)S(1)} async-done(((bf16[8,24,1152]{2,1,0:T(8,128)(2,1)}), bf16[8,24,1152]{2,1,0:T(8,128)(2,1)S(1)}, u32[]{:S(2)}, u32[]{:S(2)}) %all-to-all-start) | async-done | bytes 442400 | tf_op jit(solution)/shard_map/all_to_all | solution.py:942
  32.2 2.5 %fetch.1 = (bf16[512,512]{1,0:T(8,128)(2,1)S(1)}, f32[8,2048]{1,0:T(8,128)S(1)}, bf16[512,2048]{1,0:T(8,128)(2,1)S(1)}, bf16[2048,512]{1,0:T(8,128)(2,1)S(1)}) custom-call(bf16[512,512]{1,0:T(8,128)(2,1)} %refs_3_.5, f32[8,2048]{1,0:T(8,128)} %get-tuple-element.75.refs_1_.refs_4_, bf16[512,2048]{1,0:T(8,128)(2,1)} %refs_5_.3, bf16[2048,512]{1,0:T(8,128)(2,1)} %refs_6_.7, ...), custom_call_target="tpu_custom_call" | custom-call | tf_op jit(solution)/shard_map/fetch/pallas_call | solution.py:823
  34.7 11.4 %cls_middle.1 = (f32[512,512]{1,0:T(8,128)S(1)}, bf16[512,512]{1,0:T(8,128)(2,1)S(1)}, bf16[32,512]{1,0:T(8,128)(2,1)S(1)}, bf16[32,512]{1,0:T(8,128)(2,1)}, f32...) custom-call(bf16[192,1152]{1,0:T(8,128)(2,1)S(1)} %bitcast.26, ...), custom_call_target="tpu_custom_call" | custom-call | flops 4831838208 | bytes 17264100 | tf_op jit(solution)/shard_map/cls_middle/pallas_call | solution.py:193
  46.7 1.5 %collective-permute-done.4.refs_1_ = bf16[512,512]{1,0:T(8,128)(2,1)S(1)} collective-permute-done((bf16[512,512]{1,0:T(8,128)(2,1)S(1)}, bf16[512,512]{1,0:T(8,128)(2,1)S(1)}, u32[]{:S(2)}, u32[]{:S(2)}) %collective-permute-start.4) | collective-permute-done | bytes 524320 | tf_op jit(solution)/shard_map/ppermute | solution.py:541
  48.2 0.9 chip_sum.1
  49.1 4.7 %all-to-all-start.1 = ((bf16[16,32,512]{2,1,0:T(8,128)(2,1)}), bf16[16,32,512]{2,1,0:T(8,128)(2,1)S(1)}, u32[]{:S(2)}, u32[]{:S(2)}) async-start(bf16[16,32,512]{2,1,0:T(8,128)(2,1)} %bitcast.14), calls=%async_computation.1 | async-start | bytes 1048576 | tf_op jit(solution)/shard_map/all_to_all | solution.py:535
  53.8 1.9 %collective-permute-start.6 = (bf16[32,512]{1,0:T(8,128)(2,1)S(1)}, bf16[32,512]{1,0:T(8,128)(2,1)S(1)}, u32[]{:S(2)}, u32[]{:S(2)}) collective-permute-start(bf16[32,512]{1,0:T(8,128)(2,1)S(1)} %get-tuple-element.87.refs_5_.refs_1_), channel_id=1, source_target_pairs={{0,16},{16,0},{8,24},{24,8},{1,17},{17,1},{9,25},{25,9},{2,18},{18... | collective-permute-start | bytes 98312 | tf_op jit(solution)/shard_map/ppermute | solution.py:300
  55.7 6.3 %weight_grads.1 = (f32[2048,512]{1,0:T(8,128)}, f32[512,2048]{1,0:T(8,128)}, f32[512,512]{1,0:T(8,128)}, bf16[512,512]{1,0:T(8,128)(2,1)}, f32[8,128]{1,0:T(8,128)}) custom-call(bf16[384,2048]{1,0:T(8,128)(2,1)} %get-tuple-element.88.refs_0_, bf16[384,512]{1,0:T(8,128)(2,1)} %get-tuple-element.89.refs_1_, bf16[384,512]{1,0:T(8,128)(2,1)} %get-tuple-element.90.refs_2_, ...), custom_call_target="tpu_custom_call" | custom-call | flops 1006632960 | bytes 15075328 | tf_op jit(solution)/shard_map/weight_grads/pallas_call | solution.py:193
  62.7 5.2 %input_grad.1 = (bf16[1024,512]{1,0:T(8,128)(2,1)}, f32[8,128]{1,0:T(8,128)}) custom-call(bf16[32,1024]{1,0:T(8,128)(2,1)} %get-tuple-element.71.refs_7_.refs_0_, bf16[256,1024]{1,0:T(8,128)(2,1)} %get-tuple-element.96.refs_1_, f32[256,1024]{1,0:T(8,128)} %get-tuple-element.81.refs_9_.refs_2_, bf16[32,512]{1,0:T(8,128)(2,1)} %get-tuple-element.97.refs_3_, ...), custom_call_target="tpu_custom_call" | custom-call | flops 1610612736 | bytes 4423680 | tf_op jit(solution)/shard_map/input_grad/pallas_call | solution.py:193
  67.9 1.4 %all-to-all-done.1.refs_0_ = bf16[16,32,512]{2,1,0:T(8,128)(2,1)S(1)} async-done(((bf16[16,32,512]{2,1,0:T(8,128)(2,1)}), bf16[16,32,512]{2,1,0:T(8,128)(2,1)S(1)}, u32[]{:S(2)}, u32[]{:S(2)}) %all-to-all-start.1) | async-done | bytes 524320 | tf_op jit(solution)/shard_map/all_to_all | solution.py:535
  69.3 1.0 %add_parts.1 = (bf16[16,48,512]{2,1,0:T(8,128)(2,1)}, f32[8,128]{1,0:T(8,128)}) custom-call(bf16[16,32,512]{2,1,0:T(8,128)(2,1)S(1)} %all-to-all-done.1.refs_0_, bf16[32,512]{1,0:T(8,128)(2,1)S(1)} %get-tuple-element.87.refs_5_.refs_1_, bf16[32,512]{1,0:T(8,128)(2,1)S(1)} %collective-permute-done.5.refs_2_, bf16[32,512]{1,0:T(8,128)(2,1)S(1)} %hand_on.4.refs_3_, ...), custom_call_target="tpu_custom_call" | custom-call | bytes 1441792 | tf_op jit(solution)/shard_map/add_parts/pallas_call | solution.py:193
  70.3 4.2 %all-to-all-start.2 = ((bf16[16,48,512]{2,1,0:T(8,128)(2,1)}), bf16[16,48,512]{2,1,0:T(8,128)(2,1)S(1)}, u32[]{:S(2)}, u32[]{:S(2)}) async-start(bf16[16,48,512]{2,1,0:T(8,128)(2,1)} %get-tuple-element.104), calls=%async_computation.2 | async-start | bytes 1572864 | tf_op jit(solution)/shard_map/all_to_all | solution.py:535
  74.5 9.2 %rest_attention.1 = (bf16[512,512]{1,0:T(8,128)(2,1)}, f32[8,128]{1,0:T(8,128)}) custom-call(bf16[1024,512]{1,0:T(8,128)(2,1)} %bitcast.31, bf16[512,512]{1,0:T(8,128)(2,1)} %refs_1_.3, f32[1,512]{1,0:T(1,128)} %bitcast.44, bf16[1024,512]{1,0:T(8,128)(2,1)} %get-tuple-element.70.refs_1_.refs_11_.refs_3_, ...), custom_call_target="tpu_custom_call" | custom-call | flops 4000000000 | bytes 4200448 | tf_op jit(solution)/shard_map/rest_attention/pallas_call | solution.py:193
  83.7 10.9 %feed_forward.1 = (bf16[1024,512]{1,0:T(8,128)(2,1)}, f32[8,128]{1,0:T(8,128)}) custom-call(bf16[1024,512]{1,0:T(8,128)(2,1)} %bitcast.32, bf16[512,512]{1,0:T(8,128)(2,1)} %get-tuple-element.83.refs_1_, bf16[512,512]{1,0:T(8,128)(2,1)} %get-tuple-element.101.refs_2_, bf16[512,512]{1,0:T(8,128)(2,1)} %refs_3_.5, ...), custom_call_target="tpu_custom_call" | custom-call | flops 6000000000 | bytes 7929856 | tf_op jit(solution)/shard_map/feed_forward/pallas_call | solution.py:193
  95.1 0.6 fusion
  95.7 1.7 %collective-permute-done.8.refs_1_ = bf16[16,48,512]{2,1,0:T(8,128)(2,1)S(1)} collective-permute-done((bf16[16,48,512]{2,1,0:T(8,128)(2,1)S(1)}, bf16[16,48,512]{2,1,0:T(8,128)(2,1)S(1)}, u32[]{:S(2)}, u32[]{:S(2)}) %collective-permute-start.8) | collective-permute-done | bytes 786464 | tf_op jit(solution)/shard_map/ppermute | solution.py:1028
  97.3 2.7 %last_grads.1 = (f32[512,512]{1,0:T(8,128)}, f32[512,512]{1,0:T(8,128)}, f32[512,512]{1,0:T(8,128)}, f32[1,512]{1,0:T(1,128)}, f32[8,128]{1,0:T(8,128)}) custom-call(bf16[16,48,512]{2,1,0:T(8,128)(2,1)S(1)} %hand_on.5.refs_0_, bf16[16,48,512]{2,1,0:T(8,128)(2,1)S(1)} %collective-permute-done.8.refs_1_, bf16[512,512]{1,0:T(8,128)(2,1)} %get-tuple-element.106.refs_2_), custom_call_target="tpu_custom_call" | custom-call | bytes 5244928 | tf_op jit(solution)/shard_map/last_grads/pallas_call | solution.py:193
  (18 shorter events, 1.6 us)
Async XLA Ops:
  5.4 5.3 %collective-permute-start.1 = (bf16[32,1024]{1,0:T(8,128)(2,1)S(1)}, bf16[32,1024]{1,0:T(8,128)(2,1)S(1)}, u32[]{:S(2)}, u32[]{:S(2)}) collective-permute-start(bf16[32,1024]{1,0:T(8,128)(2,1)S(1)} %get-tuple-element.67.refs_0_), channel_id=1, source_target_pairs={{0,16},{16,0},{8,24},{24,8},{1,17},{17,1},{9,25},{25,9},{2,18},{18... | collective-permute-start | bytes 196616 | tf_op jit(solution)/shard_map/ppermute | solution.py:300
  8.4 2.3 %collective-permute-start = (bf16[32,1024]{1,0:T(8,128)(2,1)S(1)}, bf16[32,1024]{1,0:T(8,128)(2,1)S(1)}, u32[]{:S(2)}, u32[]{:S(2)}) collective-permute-start(bf16[32,1024]{1,0:T(8,128)(2,1)S(1)} %get-tuple-element.67.refs_0_), channel_id=1, source_target_pairs={{0,8},{8,0},{16,24},{24,16},{1,9},{9,1},{17,25},{25,17},{2,10},{10... | collective-permute-start | bytes 196616 | tf_op jit(solution)/shard_map/ppermute | solution.py:299
  10.7 1.3 %collective-permute-start.2 = (bf16[32,1024]{1,0:T(8,128)(2,1)S(1)}, bf16[32,1024]{1,0:T(8,128)(2,1)S(1)}, u32[]{:S(2)}, u32[]{:S(2)}) collective-permute-start(bf16[32,1024]{1,0:T(8,128)(2,1)S(1)} %collective-permute-done.1.refs_2_), channel_id=1, source_target_pairs={{0,8},{8,0},{16,24},{24,16},{1,9},{9,1},{17,25},{25,17},{2,10},{10... | collective-permute-start | bytes 196616 | tf_op jit(solution)/shard_map/ppermute | solution.py:303
  12.9 19.4 %all-to-all-start = ((bf16[8,24,1152]{2,1,0:T(8,128)(2,1)}), bf16[8,24,1152]{2,1,0:T(8,128)(2,1)S(1)}, u32[]{:S(2)}, u32[]{:S(2)}) async-start(bf16[8,24,1152]{2,1,0:T(8,128)(2,1)} %get-tuple-element.69), calls=%async_computation | async-start | bytes 884736 | tf_op jit(solution)/shard_map/all_to_all | solution.py:942
  32.2 2.5 %collective-permute-start.3 = (bf16[8,24,1152]{2,1,0:T(8,128)(2,1)S(1)}, bf16[8,24,1152]{2,1,0:T(8,128)(2,1)S(1)}, u32[]{:S(2)}, u32[]{:S(2)}) collective-permute-start(bf16[8,24,1152]{2,1,0:T(8,128)(2,1)S(1)} %hand_on.3.refs_4_), channel_id=1, source_target_pairs={{0,8},{8,0},{16,24},{24,16},{1,9},{9,1},{17,25},{25,17},{2,10},{10... | collective-permute-start | bytes 1327112 | tf_op jit(solution)/shard_map/ppermute | solution.py:952
  46.1 2.1 %collective-permute-start.4 = (bf16[512,512]{1,0:T(8,128)(2,1)S(1)}, bf16[512,512]{1,0:T(8,128)(2,1)S(1)}, u32[]{:S(2)}, u32[]{:S(2)}) collective-permute-start(bf16[512,512]{1,0:T(8,128)(2,1)S(1)} %get-tuple-element.85), channel_id=1, source_target_pairs={{0,8},{8,0},{16,24},{24,16},{1,9},{9,1},{17,25},{25,17},{2,10},{10... | collective-permute-start | bytes 1572872 | tf_op jit(solution)/shard_map/ppermute | solution.py:541
  49.1 20.2 %all-to-all-start.1 = ((bf16[16,32,512]{2,1,0:T(8,128)(2,1)}), bf16[16,32,512]{2,1,0:T(8,128)(2,1)S(1)}, u32[]{:S(2)}, u32[]{:S(2)}) async-start(bf16[16,32,512]{2,1,0:T(8,128)(2,1)} %bitcast.14), calls=%async_computation.1 | async-start | bytes 1048576 | tf_op jit(solution)/shard_map/all_to_all | solution.py:535
  53.8 8.2 %collective-permute-start.6 = (bf16[32,512]{1,0:T(8,128)(2,1)S(1)}, bf16[32,512]{1,0:T(8,128)(2,1)S(1)}, u32[]{:S(2)}, u32[]{:S(2)}) collective-permute-start(bf16[32,512]{1,0:T(8,128)(2,1)S(1)} %get-tuple-element.87.refs_5_.refs_1_), channel_id=1, source_target_pairs={{0,16},{16,0},{8,24},{24,8},{1,17},{17,1},{9,25},{25,9},{2,18},{18... | collective-permute-start | bytes 98312 | tf_op jit(solution)/shard_map/ppermute | solution.py:300
  55.7 12.1 %collective-permute-start.5 = (bf16[32,512]{1,0:T(8,128)(2,1)S(1)}, bf16[32,512]{1,0:T(8,128)(2,1)S(1)}, u32[]{:S(2)}, u32[]{:S(2)}) collective-permute-start(bf16[32,512]{1,0:T(8,128)(2,1)S(1)} %get-tuple-element.87.refs_5_.refs_1_), channel_id=1, source_target_pairs={{0,8},{8,0},{16,24},{24,16},{1,9},{9,1},{17,25},{25,17},{2,10},{10... | collective-permute-start | bytes 98312 | tf_op jit(solution)/shard_map/ppermute | solution.py:299
  62.1 5.8 %collective-permute-start.7 = (bf16[32,512]{1,0:T(8,128)(2,1)S(1)}, bf16[32,512]{1,0:T(8,128)(2,1)S(1)}, u32[]{:S(2)}, u32[]{:S(2)}) collective-permute-start(bf16[32,512]{1,0:T(8,128)(2,1)S(1)} %hand_on.4.refs_3_), channel_id=1, source_target_pairs={{0,8},{8,0},{16,24},{24,16},{1,9},{9,1},{17,25},{25,17},{2,10},{10... | collective-permute-start | bytes 98312 | tf_op jit(solution)/shard_map/ppermute | solution.py:303
  70.3 24.7 %all-to-all-start.2 = ((bf16[16,48,512]{2,1,0:T(8,128)(2,1)}), bf16[16,48,512]{2,1,0:T(8,128)(2,1)S(1)}, u32[]{:S(2)}, u32[]{:S(2)}) async-start(bf16[16,48,512]{2,1,0:T(8,128)(2,1)} %get-tuple-element.104), calls=%async_computation.2 | async-start | bytes 1572864 | tf_op jit(solution)/shard_map/all_to_all | solution.py:535
  83.7 11.3 %copy-start = (f32[8,512]{1,0:T(8,128)S(1)}, f32[8,512]{1,0:T(8,128)}, u32[]{:S(2)}) copy-start(f32[8,512]{1,0:T(8,128)} %get-tuple-element.111) | copy-start | bytes 49156
  95.1 2.3 %collective-permute-start.8 = (bf16[16,48,512]{2,1,0:T(8,128)(2,1)S(1)}, bf16[16,48,512]{2,1,0:T(8,128)(2,1)S(1)}, u32[]{:S(2)}, u32[]{:S(2)}) collective-permute-start(bf16[16,48,512]{2,1,0:T(8,128)(2,1)S(1)} %hand_on.5.refs_0_), channel_id=1, source_target_pairs={{0,8},{8,0},{16,24},{24,16},{1,9},{9,1},{17,25},{25,17},{2,10},{10... | collective-permute-start | bytes 2359304 | tf_op jit(solution)/shard_map/ppermute | solution.py:1028

commit v3 on v2

--- a/solution.py
+++ b/solution.py
@@ -217,6 +217,14 @@
     )(value, *tokens)
 
 
+def exchange_order(batch_n, turn=0):
+    order = []
+    for x in range(2):
+        run = [b for b in range(batch_n) if b % 2 == x][::-1]
+        order += run[turn:] + run[:turn]
+    return order
+
+
 class Rows:
     def __init__(self, batch_n, n_query, n_pass, pass_count):
         block = n_query + 3 * n_pass
@@ -237,12 +245,13 @@
         self.code = np.empty(self.count, np.int32)
         self.code[order.reshape(-1)] = np.arange(self.count)
 
-    def landed(self):
-        halves = self.order.reshape(self.batch_n, 2, self.half).transpose(1, 0, 2)
+    def landed(self, batches):
+        halves = self.order.reshape(self.batch_n, 2, self.half).transpose(1, 0, 2)[:, batches]
         return halves.reshape(-1).astype(np.int32)
 
     def slots(self):
         quarters = self.order.reshape(self.batch_n, 2, 2, self.quarter).transpose(1, 2, 0, 3)
+        quarters = quarters[:, :, exchange_order(self.batch_n)]
         none = np.full((2, 2, self.batch_n, self.slot - self.quarter), -1)
         return np.concatenate([quarters, none], axis=3).reshape(-1).astype(np.int32)
 
@@ -474,6 +483,16 @@
     low_ref[...] = (fold_heads(dot(grad_scores, key_ref[...])) * HD**-0.5).astype(BF)
 
 
+def grads_kernel(*refs):
+    weights, inputs, outs = refs[:7], refs[7:17], refs[17:]
+    weights[0].ref(), weights[1].ref()
+    for ref in weights[2:] + inputs:
+        if isinstance(ref, Fetched):
+            ref.start()
+    weight_grads_kernel(*weights, *outs[:4])
+    input_grad_kernel(*inputs, outs[4])
+
+
 def input_grad_kernel(
     pick_ref, scores_ref, probs_ref, context_ref, query_ref, low_ref, gown_ref,
     wq_ref, wk_ref, wv_ref, out_ref,
@@ -528,7 +547,8 @@
 
 
 def core_groups(batch_n):
-    return [[(y * 2 + c) * batch_n + b for y in range(2) for b in range(batch_n)] for c in range(2)]
+    order = exchange_order(batch_n)
+    return [[(y * 2 + c) * batch_n + b for y in range(2) for b in order] for c in range(2)]
 
 
 def exchange(sent, batch_n):
@@ -629,7 +649,7 @@
                         outs.append(mixed / pltpu.roll(mixed, HD, 1))
                     for k, slab in enumerate(slabs):
                         out = jnp.where(half == 0, outs[2 * k], outs[2 * k + 1])
-                        out_ref.buffer[here, slab] = out.astype(BF)
+                        ref_of(out_ref)[here, slab] = out.astype(BF)
 
                 together = SLABS_AT_ONCE.get(size, 1 if size > 512 else HEADS // 2)
                 if together == HEADS // 2:
@@ -682,21 +702,6 @@
         limit=24,
         after=after,
         name="first_attention",
-    )
-
-
-def rest_attention(x, wq, bq, keys, values, seg, after, share, tile=256):
-    t, d = x.shape
-    return call(
-        functools.partial(attention_kernel, tile, (share // tile, t // tile), window_sizes(t)),
-        [((t - share, d), BF, False)],
-        (x, wq, bq, keys, values, seg),
-        flops=4 * 10**9,
-        far=range(6),
-        scratch=[pltpu.VMEM((tile, d), BF), pltpu.VMEM((tile, t), F32)],
-        limit=20,
-        after=after,
-        name="rest_attention",
     )
 
 
@@ -720,17 +725,37 @@
         out_ref.flush(t, tile)
 
 
-def ffn(x, context, weights, after, tile=512):
+def dense_kernel(
+    tile, tiles, x_ref, wq_ref, bq_ref, key_ref, value_ref, seg_ref, first_ref, wo_ref, vector_ref, wi_ref,
+    wu_ref, out_ref, rest_ref, q_scr, bias_scr,
+):
+    for ref in (x_ref, wq_ref, bq_ref, key_ref, value_ref, seg_ref):
+        ref.ref()
+    for ref in (first_ref, wo_ref, vector_ref, wi_ref, wu_ref):
+        ref.start()
+    count = x_ref.shape[0]
+    attention_kernel(
+        tile, tiles, window_sizes(count), x_ref, wq_ref, bq_ref, key_ref, value_ref, seg_ref, rest_ref,
+        q_scr, bias_scr,
+    )
+    ffn_kernel(512, x_ref, first_ref, rest_ref, wo_ref, vector_ref, wi_ref, wu_ref, out_ref)
+
+
+def dense_rest(x, wq, bq, keys, values, seg, context, weights, after, tile=256):
+    t, d = x.shape
+    share = context.shape[0]
     return call(
-        functools.partial(ffn_kernel, tile),
+        functools.partial(dense_kernel, tile, (share // tile, t // tile)),
         [(x.shape, BF, False)],
-        (x,) + context + weights,
-        flops=6 * 10**9,
-        far=range(7),
-        limit=20,
-        split={5: (1, PARTS), 6: (0, PARTS)},
+        (x, wq, bq, keys, values, seg, context) + weights,
+        flops=8 * 10**9,
+        far=(0, 1, 2, 5, 3, 4, 6, 7, 8, 9, 10),
+        late=range(6, 11),
+        split={9: (1, PARTS), 10: (0, PARTS)},
+        scratch=[pltpu.VMEM((t - share, d), BF), pltpu.VMEM((tile, d), BF), pltpu.VMEM((tile, t), F32)],
+        limit=40,
         after=after,
-        name="feed_forward",
+        name="dense_rest",
     )
 
 
@@ -738,7 +763,7 @@
     rows, pass_count, core, mine, theirs, told, cluster, wo, bo, g1, s1, wi, bi, wu, bu, g2, s2
 ):
     width = wo.shape[0]
-    both = join_halves(core, mine, theirs)[np.argsort(rows.landed())]
+    both = join_halves(core, mine, theirs)[np.argsort(rows.landed(np.arange(rows.batch_n)))]
     attended = both[:, width:].astype(F32) + (dot(both[:, :width], wo) + bo)
     first_hat, first_inv = norm_stats(attended)
     first = first_hat * g1 + s1
@@ -835,7 +860,7 @@
     width, ff = weights[2].shape
     count = rows.count
     keys, values, cls_query, probs = kept
-    landed = rows.landed()
+    landed = rows.landed(exchange_order(rows.batch_n, 1))
     ins = (mine, theirs) + weights
     ins += (rows.code[None, :], landed[None, :], values, probs, hidden, keys, cls_query, cluster[None, :])
     outs = [
@@ -939,7 +964,10 @@
             name="half_rows",
         )
         sent = jnp.broadcast_to(half[None], (batch_n,) + half.shape)
-    mine = lax.all_to_all(sent, "batch", split_axis=0, concat_axis=0)
+    batches = exchange_order(batch_n, 1)
+    mine = lax.all_to_all(
+        sent, "batch", split_axis=0, concat_axis=0, axis_index_groups=[batches] if small_case else None
+    )
     vectors = (weights[1], weights[2], weights[3], weights[7], weights[8], weights[9], weights[5])
     share = count_tok // 2
     first_context, values, probs, vectors, attention_done = first_attention(
@@ -980,51 +1008,44 @@
         )
 
     parts, sum_done = scatter_sum(keep, give, batch_n)
-    input_grad, input_done = call(
-        input_grad_kernel,
-        [(hidden.shape, BF, False)],
-        (
-            pick, grad_scores, probs, own_context, cls_query, query_low, own_attended, query_weight,
-            key_weight, value_weight,
-        ),
-        flops=6 * count_tok * width * width,
-        far=(1, 4, 2, 3, 0, 6, 8, 9, 7),
-        limit=20,
-        after=(sum_done,),
-        name="input_grad",
-    )
     peers, size = parts.shape[:2]
+    for_input = (
+        pick, grad_scores, probs, own_context, cls_query, query_low, own_attended, query_weight, key_weight,
+        value_weight,
+    )
     if small_case and size % 16 == 0:
         saved = (active_low, second_low, first_low, pre_low, both, attended_low, rows.slots()[None, :])
-        grad_outer_weight, grad_inner_weight, grad_out_weight, all_tokens, weight_done = call(
-            weight_grads_kernel,
+        grad_outer_weight, grad_inner_weight, grad_out_weight, all_tokens, input_grad, weight_done = call(
+            grads_kernel,
             [
                 (outer_weight.shape, F32, False),
                 (inner_weight.shape, F32, False),
                 (out_weight.shape, F32, False),
                 ((4 * rows.batch_n * rows.slot, width), BF, False),
+                (hidden.shape, BF, False),
             ],
-            saved,
-            flops=2 * rows.count * width * (4 * width + width),
-            far=range(7),
-            limit=32,
+            saved + for_input,
+            flops=2 * rows.count * width * (4 * width + width) + 6 * count_tok * width * width,
+            far=tuple(i for i in range(17) if i != 12),
+            late=range(2, 17),
+            limit=40,
             after=(sum_done,),
-            name="weight_grads",
+            name="grads",
         )
         low = near_rows(query_low, weight_done)
         sent, add_done = call(
             functools.partial(add_parts_kernel, rows),
             [((peers, size + rows.slot, width), BF, True)],
             (parts,) + low,
-            after=(input_done, weight_done),
+            after=(weight_done,),
             name="add_parts",
         )
         whole = exchange(sent, batch_n)
-        rest_context, _ = rest_attention(
-            hidden, query_weight, vec(query_bias), keys, values, segments, (add_done,), share
+        rows_out, dense_done = dense_rest(
+            hidden, query_weight, vec(query_bias), keys, values, segments, first_context, matrices,
+            (add_done,),
         )
-        rows_out, ffn_done = ffn(hidden, (first_context, rest_context), matrices, (add_done,))
-        whole = behind(whole, ffn_done)
+        whole = behind(whole, dense_done)
         other = lax.ppermute(whole, "side", CORE_SWAP)
         grad_key_weight, grad_value_weight, grad_query_weight, grad_query_bias, _ = call(
             functools.partial(last_kernel, size),
@@ -1035,10 +1056,19 @@
             name="last_grads",
         )
     else:
-        rest_context, _ = rest_attention(
-            hidden, query_weight, vec(query_bias), keys, values, segments, (sum_done,), share
+        input_grad, _ = call(
+            input_grad_kernel,
+            [(hidden.shape, BF, False)],
+            for_input,
+            far=(1, 4, 2, 3, 0, 6, 8, 9, 7),
+            limit=20,
+            after=(sum_done,),
+            name="input_grad",
         )
-        rows_out, _ = ffn(hidden, (first_context, rest_context), matrices, (sum_done,))
+        rows_out, _ = dense_rest(
+            hidden, query_weight, vec(query_bias), keys, values, segments, first_context, matrices,
+            (sum_done,),
+        )
         part = jnp.sum(parts.astype(F32), axis=0).astype(BF)
         whole = exchange(jnp.broadcast_to(part[None], parts.shape), batch_n).reshape(width, width)
         grad_outer_weight = t_dot(active_low, second_low)
@@ -1054,7 +1084,7 @@
         half = jnp.broadcast_to(half[None], (batch_n,) + half.shape)
         low_mine = lax.all_to_all(half, "batch", split_axis=0, concat_axis=0).reshape(flat)
         low_theirs = lax.ppermute(low_mine, "side", CORE_SWAP)
-        all_low = join_halves(side % 2, low_mine, low_theirs)[np.argsort(rows.landed())]
+        all_low = join_halves(side % 2, low_mine, low_theirs)[np.argsort(rows.landed(np.arange(rows.batch_n)))]
         grad_query_weight = t_dot(both[:, width:], all_low)
         grad_query_bias = jnp.sum(all_low.astype(F32), axis=0)
         other = lax.ppermute(whole, "side", CORE_SWAP)

time: 101 us -> 98.8 us (0.978)
  starting transfers between devices: 21.3 us -> 26 us
  waiting for transfers between devices: 12 us -> 8.04 us
  Pallas kernels: 65.3 us -> 62.7 us
    all_to_all x2, starting transfers between devices: 8.88 us -> 13.4 us  [exchange(): lax.all_to_all(sent, ('side', 'batch'), split_axis=0, concat_axis=0, axis...]
    all_to_all x1, waiting for transfers between devices: 3.52 us -> 0.01 us  [body(): lax.all_to_all(sent, 'batch', split_axis=0, concat_axis=0, axis_index_gro...]
    pallas_call x11 -> x9, Pallas kernels: 62.9 us -> 60.2 us  [call(): pl.pallas_call(wrapped, out_shape=shapes, in_specs=spaces, out_specs=out_...]
    all_to_all x2, waiting for transfers between devices: 1.78 us -> 0.49 us  [exchange(): lax.all_to_all(sent, ('side', 'batch'), split_axis=0, concat_axis=0, axis...]
  transfers between devices with their start and end apart: 12 -> 12, of which waited for: 7 -> 6; matrix products, arithmetic and copies ran while one was open for 1% -> 1% of each run, Pallas kernels for 43% -> 42%
where the time goes in v3:
time: 98.8 us; the launch traced here: 98.3 us
  Pallas kernels  62.7 us (63%)
  starting transfers between devices  26 us (26%)
  waiting for transfers between devices  8.04 us (8%)
    pallas_call x9, Pallas kernels, call(): pl.pallas_call(wrapped, out_shape=shapes, in_specs=spaces, out_specs=out_...  60.2 us
    all_to_all x2, starting transfers between devices, exchange(): lax.all_to_all(sent, ('side', 'batch'), split_axis=0, concat_axis=0, axis...  13.4 us
    all_to_all x1, starting transfers between devices, body(): lax.all_to_all(sent, 'batch', split_axis=0, concat_axis=0, axis_index_gro...  6.87 us
    ppermute x2, starting transfers between devices, near_rows(): far = lax.ppermute(own, 'side', CHIP_SWAP)  4.5 us
    pallas_call x1, Pallas kernels, fetch(): pl.pallas_call(kernel, out_shape=[pltpu.VMEM(x.shape, x.dtype) for x in a...  2.46 us
    ppermute x2, waiting for transfers between devices, near_rows(): far = lax.ppermute(own, 'side', CHIP_SWAP)  2.24 us
    ppermute x2, waiting for transfers between devices, near_rows(): return (own, other, far, lax.ppermute(far, 'side', CORE_SWAP))  2.11 us
  transfers between devices with their start and end apart: 12, of which 6 were waited for; matrix products, arithmetic and copies ran while one was open for 1% of the time, Pallas kernels for 42%

profile of v3, /device:TPU:0, one launch (start us, length us, event | category | flops | bytes accessed | tf_op | source)
XLA Modules:
  0.0 98.3 jit_solution(9042886952115910770)
XLA Ops:
  0.7 4.7 %cls_forward.1 = (bf16[32,1024]{1,0:T(8,128)(2,1)S(1)}, bf16[32,512]{1,0:T(8,128)(2,1)}, bf16[32,1024]{1,0:T(8,128)(2,1)}, bf16[24,128]{1,0:T(8,128)(2,1)S(1)}, ...) custom-call(bf16[1024,512]{1,0:T(8,128)(2,1)} %bitcast.28, s32[1,1,1024]{2,1,0:T(1,128)} %refs_5_.1, s32[1,32]{1,0:T(1,128)} %refs_2_.3, ...), custom_call_target="tpu_custom_call" | custom-call | flops 536870912 | bytes 3863828 | tf_op jit(solution)/shard_map/cls_forward/pallas_call | solution.py:193
  5.4 3.0 %collective-permute-start.1 = (bf16[32,1024]{1,0:T(8,128)(2,1)S(1)}, bf16[32,1024]{1,0:T(8,128)(2,1)S(1)}, u32[]{:S(2)}, u32[]{:S(2)}) collective-permute-start(bf16[32,1024]{1,0:T(8,128)(2,1)S(1)} %get-tuple-element.65.refs_0_), channel_id=1, source_target_pairs={{0,16},{16,0},{8,24},{24,8},{1,17},{17,1},{9,25},{25,9},{2,18},{18... | collective-permute-start | bytes 196616 | tf_op jit(solution)/shard_map/ppermute | solution.py:309
  8.4 2.2 %collective-permute-done.1.refs_2_ = bf16[32,1024]{1,0:T(8,128)(2,1)S(1)} collective-permute-done((bf16[32,1024]{1,0:T(8,128)(2,1)S(1)}, bf16[32,1024]{1,0:T(8,128)(2,1)S(1)}, u32[]{:S(2)}, u32[]{:S(2)}) %collective-permute-start.1) | collective-permute-done | bytes 65568 | tf_op jit(solution)/shard_map/ppermute | solution.py:309
  10.7 1.2 %collective-permute-done.2.refs_3_ = bf16[32,1024]{1,0:T(8,128)(2,1)S(1)} collective-permute-done((bf16[32,1024]{1,0:T(8,128)(2,1)S(1)}, bf16[32,1024]{1,0:T(8,128)(2,1)S(1)}, u32[]{:S(2)}, u32[]{:S(2)}) %collective-permute-start.2) | collective-permute-done | bytes 65568 | tf_op jit(solution)/shard_map/ppermute | solution.py:312
  11.9 0.9 half_rows.1
  12.9 6.9 %all-to-all-start = ((bf16[8,24,1152]{2,1,0:T(8,128)(2,1)}), bf16[8,24,1152]{2,1,0:T(8,128)(2,1)S(1)}, u32[]{:S(2)}, u32[]{:S(2)}) async-start(bf16[8,24,1152]{2,1,0:T(8,128)(2,1)} %get-tuple-element.67), calls=%async_computation | async-start | bytes 884736 | tf_op jit(solution)/shard_map/all_to_all | solution.py:968
  19.8 9.5 %first_attention.1 = (bf16[512,512]{1,0:T(8,128)(2,1)}, bf16[1024,512]{1,0:T(8,128)(2,1)}, f32[256,1024]{1,0:T(8,128)}, f32[8,2048]{1,0:T(8,128)}, f32[8,128]{1,0:T(8,128)}) custom-call(bf16[1024,512]{1,0:T(8,128)(2,1)} %bitcast.29, bf16[1024,512]{1,0:T(8,128)(2,1)} %get-tuple-element.68.refs_1_.refs_11_.refs_3_, bf16[512,512]{1,0:T(8,128)(2,1)} %refs_16_.1, ...), custom_call_target="tpu_custom_call" | custom-call | flops 6000000000 | bytes 5959680 | tf_op jit(solution)/shard_map/first_attention/pallas_call | solution.py:193
  29.4 2.5 %fetch.1 = (bf16[512,512]{1,0:T(8,128)(2,1)S(1)}, f32[8,2048]{1,0:T(8,128)S(1)}, bf16[512,2048]{1,0:T(8,128)(2,1)S(1)}, bf16[2048,512]{1,0:T(8,128)(2,1)S(1)}) custom-call(bf16[512,512]{1,0:T(8,128)(2,1)} %refs_7_.4, f32[8,2048]{1,0:T(8,128)} %get-tuple-element.73.refs_1_.refs_8_, bf16[512,2048]{1,0:T(8,128)(2,1)} %refs_9_.3, bf16[2048,512]{1,0:T(8,128)(2,1)} %refs_10_.3, ...), custom_call_target="tpu_custom_call" | custom-call | tf_op jit(solution)/shard_map/fetch/pallas_call | solution.py:848
  31.8 11.4 %cls_middle.1 = (f32[512,512]{1,0:T(8,128)S(1)}, bf16[512,512]{1,0:T(8,128)(2,1)S(1)}, bf16[32,512]{1,0:T(8,128)(2,1)S(1)}, bf16[32,512]{1,0:T(8,128)(2,1)}, f32...) custom-call(bf16[192,1152]{1,0:T(8,128)(2,1)S(1)} %bitcast.26, ...), custom_call_target="tpu_custom_call" | custom-call | flops 4831838208 | bytes 17264100 | tf_op jit(solution)/shard_map/cls_middle/pallas_call | solution.py:193
  43.2 0.6 collective-permute-start.4
  43.8 1.5 %collective-permute-done.4.refs_1_ = bf16[512,512]{1,0:T(8,128)(2,1)S(1)} collective-permute-done((bf16[512,512]{1,0:T(8,128)(2,1)S(1)}, bf16[512,512]{1,0:T(8,128)(2,1)S(1)}, u32[]{:S(2)}, u32[]{:S(2)}) %collective-permute-start.4) | collective-permute-done | bytes 524320 | tf_op jit(solution)/shard_map/ppermute | solution.py:561
  45.3 0.9 chip_sum.1
  46.2 7.4 %all-to-all-start.1 = ((bf16[16,32,512]{2,1,0:T(8,128)(2,1)}), bf16[16,32,512]{2,1,0:T(8,128)(2,1)S(1)}, u32[]{:S(2)}, u32[]{:S(2)}) async-start(bf16[16,32,512]{2,1,0:T(8,128)(2,1)} %bitcast.14), calls=%async_computation.1 | async-start | bytes 1048576 | tf_op jit(solution)/shard_map/all_to_all | solution.py:555
  53.6 1.5 %collective-permute-start.6 = (bf16[32,512]{1,0:T(8,128)(2,1)S(1)}, bf16[32,512]{1,0:T(8,128)(2,1)S(1)}, u32[]{:S(2)}, u32[]{:S(2)}) collective-permute-start(bf16[32,512]{1,0:T(8,128)(2,1)S(1)} %get-tuple-element.85.refs_12_.refs_1_), channel_id=1, source_target_pairs={{0,16},{16,0},{8,24},{24,8},{1,17},{17,1},{9,25},{25,9},{2,18},{18... | collective-permute-start | bytes 98312 | tf_op jit(solution)/shard_map/ppermute | solution.py:309
  55.1 11.4 %grads.1 = (f32[2048,512]{1,0:T(8,128)}, f32[512,2048]{1,0:T(8,128)}, f32[512,512]{1,0:T(8,128)}, bf16[512,512]{1,0:T(8,128)(2,1)}, bf16[1024,512]{1,0:T(8,128)(2,1)}, /*index=5*/f32[8,128]{1,0:T(8,128)}) custom-call(bf16[384,2048]{1,0:T(8,128)(2,1)} %get-tuple-element.86.refs_0_, bf16[384,512]{1,0:T(8,128)(2,1)} %get-tuple-element.87.refs_1_, ...), custom_call_target="tpu_custom_call" | custom-call | flops 2617245696 | bytes 19499008 | tf_op jit(solution)/shard_map/grads/pallas_call | solution.py:193
  66.5 0.6 collective-permute-start.7
  67.1 0.9 collective-permute-done.7.refs_4_
  68.0 1.0 %add_parts.1 = (bf16[16,48,512]{2,1,0:T(8,128)(2,1)}, f32[8,128]{1,0:T(8,128)}) custom-call(bf16[16,32,512]{2,1,0:T(8,128)(2,1)S(1)} %all-to-all-done.1.refs_0_, bf16[32,512]{1,0:T(8,128)(2,1)S(1)} %get-tuple-element.85.refs_12_.refs_1_, bf16[32,512]{1,0:T(8,128)(2,1)S(1)} %collective-permute-done.5.refs_2_, bf16[32,512]{1,0:T(8,128)(2,1)S(1)} %hand_on.4.refs_3_, ...), custom_call_target="tpu_custom_call" | custom-call | bytes 1441792 | tf_op jit(solution)/shard_map/add_parts/pallas_call | solution.py:193
  69.0 6.0 %all-to-all-start.2 = ((bf16[16,48,512]{2,1,0:T(8,128)(2,1)}), bf16[16,48,512]{2,1,0:T(8,128)(2,1)S(1)}, u32[]{:S(2)}, u32[]{:S(2)}) async-start(bf16[16,48,512]{2,1,0:T(8,128)(2,1)} %get-tuple-element.100), calls=%async_computation.2 | async-start | bytes 1572864 | tf_op jit(solution)/shard_map/all_to_all | solution.py:555
  75.1 17.5 %dense_rest.1 = (bf16[1024,512]{1,0:T(8,128)(2,1)}, f32[8,128]{1,0:T(8,128)}) custom-call(bf16[1024,512]{1,0:T(8,128)(2,1)} %bitcast.31, bf16[512,512]{1,0:T(8,128)(2,1)} %refs_1_.3, f32[1,512]{1,0:T(1,128)} %bitcast.43, bf16[1024,512]{1,0:T(8,128)(2,1)} %get-tuple-element.68.refs_1_.refs_11_.refs_3_, bf16[1024,512]{1,0:T(8,128)(2,1)} %get-tuple-element.78.refs_8_.refs_4_, ...), custom_call_target="tpu_custom_call" | custom-call | flops 8000000000 | bytes 10033152 | tf_op jit(solution)/shard_map/dense_rest/pallas_call | solution.py:193
  92.6 0.5 all-to-all-done.2.refs_0_
  93.1 0.6 fusion
  93.7 1.6 %collective-permute-done.8.refs_1_ = bf16[16,48,512]{2,1,0:T(8,128)(2,1)S(1)} collective-permute-done((bf16[16,48,512]{2,1,0:T(8,128)(2,1)S(1)}, bf16[16,48,512]{2,1,0:T(8,128)(2,1)S(1)}, u32[]{:S(2)}, u32[]{:S(2)}) %collective-permute-start.8) | collective-permute-done | bytes 786464 | tf_op jit(solution)/shard_map/ppermute | solution.py:1049
  95.4 2.7 %last_grads.1 = (f32[512,512]{1,0:T(8,128)}, f32[512,512]{1,0:T(8,128)}, f32[512,512]{1,0:T(8,128)}, f32[1,512]{1,0:T(1,128)}, f32[8,128]{1,0:T(8,128)}) custom-call(bf16[16,48,512]{2,1,0:T(8,128)(2,1)S(1)} %hand_on.5.refs_0_, bf16[16,48,512]{2,1,0:T(8,128)(2,1)S(1)} %collective-permute-done.8.refs_1_, bf16[512,512]{1,0:T(8,128)(2,1)} %get-tuple-element.102.refs_2_), custom_call_target="tpu_custom_call" | custom-call | bytes 5244928 | tf_op jit(solution)/shard_map/last_grads/pallas_call | solution.py:193
  (16 shorter events, 0.1 us)
Async XLA Ops:
  5.4 5.3 %collective-permute-start.1 = (bf16[32,1024]{1,0:T(8,128)(2,1)S(1)}, bf16[32,1024]{1,0:T(8,128)(2,1)S(1)}, u32[]{:S(2)}, u32[]{:S(2)}) collective-permute-start(bf16[32,1024]{1,0:T(8,128)(2,1)S(1)} %get-tuple-element.65.refs_0_), channel_id=1, source_target_pairs={{0,16},{16,0},{8,24},{24,8},{1,17},{17,1},{9,25},{25,9},{2,18},{18... | collective-permute-start | bytes 196616 | tf_op jit(solution)/shard_map/ppermute | solution.py:309
  8.4 2.3 %collective-permute-start = (bf16[32,1024]{1,0:T(8,128)(2,1)S(1)}, bf16[32,1024]{1,0:T(8,128)(2,1)S(1)}, u32[]{:S(2)}, u32[]{:S(2)}) collective-permute-start(bf16[32,1024]{1,0:T(8,128)(2,1)S(1)} %get-tuple-element.65.refs_0_), channel_id=1, source_target_pairs={{0,8},{8,0},{16,24},{24,16},{1,9},{9,1},{17,25},{25,17},{2,10},{10... | collective-permute-start | bytes 196616 | tf_op jit(solution)/shard_map/ppermute | solution.py:308
  10.7 1.3 %collective-permute-start.2 = (bf16[32,1024]{1,0:T(8,128)(2,1)S(1)}, bf16[32,1024]{1,0:T(8,128)(2,1)S(1)}, u32[]{:S(2)}, u32[]{:S(2)}) collective-permute-start(bf16[32,1024]{1,0:T(8,128)(2,1)S(1)} %collective-permute-done.1.refs_2_), channel_id=1, source_target_pairs={{0,8},{8,0},{16,24},{24,16},{1,9},{9,1},{17,25},{25,17},{2,10},{10... | collective-permute-start | bytes 196616 | tf_op jit(solution)/shard_map/ppermute | solution.py:312
  12.9 16.4 %all-to-all-start = ((bf16[8,24,1152]{2,1,0:T(8,128)(2,1)}), bf16[8,24,1152]{2,1,0:T(8,128)(2,1)S(1)}, u32[]{:S(2)}, u32[]{:S(2)}) async-start(bf16[8,24,1152]{2,1,0:T(8,128)(2,1)} %get-tuple-element.67), calls=%async_computation | async-start | bytes 884736 | tf_op jit(solution)/shard_map/all_to_all | solution.py:968
  29.3 2.5 %collective-permute-start.3 = (bf16[8,24,1152]{2,1,0:T(8,128)(2,1)S(1)}, bf16[8,24,1152]{2,1,0:T(8,128)(2,1)S(1)}, u32[]{:S(2)}, u32[]{:S(2)}) collective-permute-start(bf16[8,24,1152]{2,1,0:T(8,128)(2,1)S(1)} %hand_on.3.refs_4_), channel_id=1, source_target_pairs={{0,8},{8,0},{16,24},{24,16},{1,9},{9,1},{17,25},{25,17},{2,10},{10... | collective-permute-start | bytes 1327112 | tf_op jit(solution)/shard_map/ppermute | solution.py:980
  43.2 2.1 %collective-permute-start.4 = (bf16[512,512]{1,0:T(8,128)(2,1)S(1)}, bf16[512,512]{1,0:T(8,128)(2,1)S(1)}, u32[]{:S(2)}, u32[]{:S(2)}) collective-permute-start(bf16[512,512]{1,0:T(8,128)(2,1)S(1)} %get-tuple-element.83), channel_id=1, source_target_pairs={{0,8},{8,0},{16,24},{24,16},{1,9},{9,1},{17,25},{25,17},{2,10},{10... | collective-permute-start | bytes 1572872 | tf_op jit(solution)/shard_map/ppermute | solution.py:561
  46.2 21.8 %all-to-all-start.1 = ((bf16[16,32,512]{2,1,0:T(8,128)(2,1)}), bf16[16,32,512]{2,1,0:T(8,128)(2,1)S(1)}, u32[]{:S(2)}, u32[]{:S(2)}) async-start(bf16[16,32,512]{2,1,0:T(8,128)(2,1)} %bitcast.14), calls=%async_computation.1 | async-start | bytes 1048576 | tf_op jit(solution)/shard_map/all_to_all | solution.py:555
  53.6 12.9 %collective-permute-start.6 = (bf16[32,512]{1,0:T(8,128)(2,1)S(1)}, bf16[32,512]{1,0:T(8,128)(2,1)S(1)}, u32[]{:S(2)}, u32[]{:S(2)}) collective-permute-start(bf16[32,512]{1,0:T(8,128)(2,1)S(1)} %get-tuple-element.85.refs_12_.refs_1_), channel_id=1, source_target_pairs={{0,16},{16,0},{8,24},{24,8},{1,17},{17,1},{9,25},{25,9},{2,18},{18... | collective-permute-start | bytes 98312 | tf_op jit(solution)/shard_map/ppermute | solution.py:309
  55.0 12.1 %collective-permute-start.5 = (bf16[32,512]{1,0:T(8,128)(2,1)S(1)}, bf16[32,512]{1,0:T(8,128)(2,1)S(1)}, u32[]{:S(2)}, u32[]{:S(2)}) collective-permute-start(bf16[32,512]{1,0:T(8,128)(2,1)S(1)} %get-tuple-element.85.refs_12_.refs_1_), channel_id=1, source_target_pairs={{0,8},{8,0},{16,24},{24,16},{1,9},{9,1},{17,25},{25,17},{2,10},{10... | collective-permute-start | bytes 98312 | tf_op jit(solution)/shard_map/ppermute | solution.py:308
  66.5 1.5 %collective-permute-start.7 = (bf16[32,512]{1,0:T(8,128)(2,1)S(1)}, bf16[32,512]{1,0:T(8,128)(2,1)S(1)}, u32[]{:S(2)}, u32[]{:S(2)}) collective-permute-start(bf16[32,512]{1,0:T(8,128)(2,1)S(1)} %hand_on.4.refs_3_), channel_id=1, source_target_pairs={{0,8},{8,0},{16,24},{24,16},{1,9},{9,1},{17,25},{25,17},{2,10},{10... | collective-permute-start | bytes 98312 | tf_op jit(solution)/shard_map/ppermute | solution.py:312
  69.0 24.0 %all-to-all-start.2 = ((bf16[16,48,512]{2,1,0:T(8,128)(2,1)}), bf16[16,48,512]{2,1,0:T(8,128)(2,1)S(1)}, u32[]{:S(2)}, u32[]{:S(2)}) async-start(bf16[16,48,512]{2,1,0:T(8,128)(2,1)} %get-tuple-element.100), calls=%async_computation.2 | async-start | bytes 1572864 | tf_op jit(solution)/shard_map/all_to_all | solution.py:555
  75.0 18.1 %copy-start = (f32[8,512]{1,0:T(8,128)S(1)}, f32[8,512]{1,0:T(8,128)}, u32[]{:S(2)}) copy-start(f32[8,512]{1,0:T(8,128)} %get-tuple-element.107) | copy-start | bytes 49156
  93.1 2.3 %collective-permute-start.8 = (bf16[16,48,512]{2,1,0:T(8,128)(2,1)S(1)}, bf16[16,48,512]{2,1,0:T(8,128)(2,1)S(1)}, u32[]{:S(2)}, u32[]{:S(2)}) collective-permute-start(bf16[16,48,512]{2,1,0:T(8,128)(2,1)S(1)} %hand_on.5.refs_0_), channel_id=1, source_target_pairs={{0,8},{8,0},{16,24},{24,16},{1,9},{9,1},{17,25},{25,17},{2,10},{10... | collective-permute-start | bytes 2359304 | tf_op jit(solution)/shard_map/ppermute | solution.py:1049

commit v4 on v3

--- a/solution.py
+++ b/solution.py
@@ -217,11 +217,11 @@
     )(value, *tokens)
 
 
-def exchange_order(batch_n, turn=0):
+def exchange_order(batch_n):
     order = []
     for x in range(2):
         run = [b for b in range(batch_n) if b % 2 == x][::-1]
-        order += run[turn:] + run[:turn]
+        order += run[1:] + run[:1]
     return order
 
 
@@ -860,7 +860,7 @@
     width, ff = weights[2].shape
     count = rows.count
     keys, values, cls_query, probs = kept
-    landed = rows.landed(exchange_order(rows.batch_n, 1))
+    landed = rows.landed(exchange_order(rows.batch_n))
     ins = (mine, theirs) + weights
     ins += (rows.code[None, :], landed[None, :], values, probs, hidden, keys, cls_query, cluster[None, :])
     outs = [
@@ -964,7 +964,7 @@
             name="half_rows",
         )
         sent = jnp.broadcast_to(half[None], (batch_n,) + half.shape)
-    batches = exchange_order(batch_n, 1)
+    batches = exchange_order(batch_n)
     mine = lax.all_to_all(
         sent, "batch", split_axis=0, concat_axis=0, axis_index_groups=[batches] if small_case else None
     )

time: 98.8 us -> 97.7 us (0.989)
  starting transfers between devices: 26 us -> 24.5 us
    all_to_all x2, starting transfers between devices: 13.4 us -> 11.9 us  [exchange(): lax.all_to_all(sent, ('side', 'batch'), split_axis=0, concat_axis=0, axis...]
where the time goes in v4:
time: 97.7 us; the launch traced here: 97.2 us
  Pallas kernels  62.7 us (64%)
  starting transfers between devices  24.5 us (25%)
  waiting for transfers between devices  8.41 us (9%)
    pallas_call x9, Pallas kernels, call(): pl.pallas_call(wrapped, out_shape=shapes, in_specs=spaces, out_specs=out_...  60.2 us
    all_to_all x2, starting transfers between devices, exchange(): lax.all_to_all(sent, ('side', 'batch'), split_axis=0, concat_axis=0, axis...  11.9 us
    all_to_all x1, starting transfers between devices, body(): lax.all_to_all(sent, 'batch', split_axis=0, concat_axis=0, axis_index_gro...  6.87 us
    ppermute x2, starting transfers between devices, near_rows(): far = lax.ppermute(own, 'side', CHIP_SWAP)  4.5 us
    pallas_call x1, Pallas kernels, fetch(): pl.pallas_call(kernel, out_shape=[pltpu.VMEM(x.shape, x.dtype) for x in a...  2.45 us
    ppermute x2, waiting for transfers between devices, near_rows(): far = lax.ppermute(own, 'side', CHIP_SWAP)  2.24 us
    ppermute x2, waiting for transfers between devices, near_rows(): return (own, other, far, lax.ppermute(far, 'side', CORE_SWAP))  2.11 us
  transfers between devices with their start and end apart: 12, of which 6 were waited for; matrix products, arithmetic and copies ran while one was open for 1% of the time, Pallas kernels for 42%

profile of v4, /device:TPU:0, one launch (start us, length us, event | category | flops | bytes accessed | tf_op | source)
XLA Modules:
  0.0 97.2 jit_solution(7682982180030738533)
XLA Ops:
  0.7 4.7 %cls_forward.1 = (bf16[32,1024]{1,0:T(8,128)(2,1)S(1)}, bf16[32,512]{1,0:T(8,128)(2,1)}, bf16[32,1024]{1,0:T(8,128)(2,1)}, bf16[24,128]{1,0:T(8,128)(2,1)S(1)}, ...) custom-call(bf16[1024,512]{1,0:T(8,128)(2,1)} %bitcast.28, s32[1,1,1024]{2,1,0:T(1,128)} %refs_5_.1, s32[1,32]{1,0:T(1,128)} %refs_2_.3, ...), custom_call_target="tpu_custom_call" | custom-call | flops 536870912 | bytes 3863828 | tf_op jit(solution)/shard_map/cls_forward/pallas_call | solution.py:193
  5.4 3.0 %collective-permute-start.1 = (bf16[32,1024]{1,0:T(8,128)(2,1)S(1)}, bf16[32,1024]{1,0:T(8,128)(2,1)S(1)}, u32[]{:S(2)}, u32[]{:S(2)}) collective-permute-start(bf16[32,1024]{1,0:T(8,128)(2,1)S(1)} %get-tuple-element.65.refs_0_), channel_id=1, source_target_pairs={{0,16},{16,0},{8,24},{24,8},{1,17},{17,1},{9,25},{25,9},{2,18},{18... | collective-permute-start | bytes 196616 | tf_op jit(solution)/shard_map/ppermute | solution.py:309
  8.4 2.2 %collective-permute-done.1.refs_2_ = bf16[32,1024]{1,0:T(8,128)(2,1)S(1)} collective-permute-done((bf16[32,1024]{1,0:T(8,128)(2,1)S(1)}, bf16[32,1024]{1,0:T(8,128)(2,1)S(1)}, u32[]{:S(2)}, u32[]{:S(2)}) %collective-permute-start.1) | collective-permute-done | bytes 65568 | tf_op jit(solution)/shard_map/ppermute | solution.py:309
  10.7 1.2 %collective-permute-done.2.refs_3_ = bf16[32,1024]{1,0:T(8,128)(2,1)S(1)} collective-permute-done((bf16[32,1024]{1,0:T(8,128)(2,1)S(1)}, bf16[32,1024]{1,0:T(8,128)(2,1)S(1)}, u32[]{:S(2)}, u32[]{:S(2)}) %collective-permute-start.2) | collective-permute-done | bytes 65568 | tf_op jit(solution)/shard_map/ppermute | solution.py:312
  11.9 0.9 half_rows.1
  12.9 6.9 %all-to-all-start = ((bf16[8,24,1152]{2,1,0:T(8,128)(2,1)}), bf16[8,24,1152]{2,1,0:T(8,128)(2,1)S(1)}, u32[]{:S(2)}, u32[]{:S(2)}) async-start(bf16[8,24,1152]{2,1,0:T(8,128)(2,1)} %get-tuple-element.67), calls=%async_computation | async-start | bytes 884736 | tf_op jit(solution)/shard_map/all_to_all | solution.py:968
  19.8 9.5 %first_attention.1 = (bf16[512,512]{1,0:T(8,128)(2,1)}, bf16[1024,512]{1,0:T(8,128)(2,1)}, f32[256,1024]{1,0:T(8,128)}, f32[8,2048]{1,0:T(8,128)}, f32[8,128]{1,0:T(8,128)}) custom-call(bf16[1024,512]{1,0:T(8,128)(2,1)} %bitcast.29, bf16[1024,512]{1,0:T(8,128)(2,1)} %get-tuple-element.68.refs_1_.refs_11_.refs_3_, bf16[512,512]{1,0:T(8,128)(2,1)} %refs_16_.1, ...), custom_call_target="tpu_custom_call" | custom-call | flops 6000000000 | bytes 5959680 | tf_op jit(solution)/shard_map/first_attention/pallas_call | solution.py:193
  29.3 0.6 collective-permute-start.3
  29.9 2.5 %fetch.1 = (bf16[512,512]{1,0:T(8,128)(2,1)S(1)}, f32[8,2048]{1,0:T(8,128)S(1)}, bf16[512,2048]{1,0:T(8,128)(2,1)S(1)}, bf16[2048,512]{1,0:T(8,128)(2,1)S(1)}) custom-call(bf16[512,512]{1,0:T(8,128)(2,1)} %refs_7_.4, f32[8,2048]{1,0:T(8,128)} %get-tuple-element.73.refs_1_.refs_8_, bf16[512,2048]{1,0:T(8,128)(2,1)} %refs_9_.3, bf16[2048,512]{1,0:T(8,128)(2,1)} %refs_10_.3, ...), custom_call_target="tpu_custom_call" | custom-call | tf_op jit(solution)/shard_map/fetch/pallas_call | solution.py:848
  32.4 11.4 %cls_middle.1 = (f32[512,512]{1,0:T(8,128)S(1)}, bf16[512,512]{1,0:T(8,128)(2,1)S(1)}, bf16[32,512]{1,0:T(8,128)(2,1)S(1)}, bf16[32,512]{1,0:T(8,128)(2,1)}, f32...) custom-call(bf16[192,1152]{1,0:T(8,128)(2,1)S(1)} %bitcast.26, ...), custom_call_target="tpu_custom_call" | custom-call | flops 4831838208 | bytes 17264100 | tf_op jit(solution)/shard_map/cls_middle/pallas_call | solution.py:193
  43.8 1.9 %collective-permute-done.4.refs_1_ = bf16[512,512]{1,0:T(8,128)(2,1)S(1)} collective-permute-done((bf16[512,512]{1,0:T(8,128)(2,1)S(1)}, bf16[512,512]{1,0:T(8,128)(2,1)S(1)}, u32[]{:S(2)}, u32[]{:S(2)}) %collective-permute-start.4) | collective-permute-done | bytes 524320 | tf_op jit(solution)/shard_map/ppermute | solution.py:561
  45.7 0.9 chip_sum.1
  46.6 6.8 %all-to-all-start.1 = ((bf16[16,32,512]{2,1,0:T(8,128)(2,1)}), bf16[16,32,512]{2,1,0:T(8,128)(2,1)S(1)}, u32[]{:S(2)}, u32[]{:S(2)}) async-start(bf16[16,32,512]{2,1,0:T(8,128)(2,1)} %bitcast.14), calls=%async_computation.1 | async-start | bytes 1048576 | tf_op jit(solution)/shard_map/all_to_all | solution.py:555
  53.4 1.5 %collective-permute-start.6 = (bf16[32,512]{1,0:T(8,128)(2,1)S(1)}, bf16[32,512]{1,0:T(8,128)(2,1)S(1)}, u32[]{:S(2)}, u32[]{:S(2)}) collective-permute-start(bf16[32,512]{1,0:T(8,128)(2,1)S(1)} %get-tuple-element.85.refs_12_.refs_1_), channel_id=1, source_target_pairs={{0,16},{16,0},{8,24},{24,8},{1,17},{17,1},{9,25},{25,9},{2,18},{18... | collective-permute-start | bytes 98312 | tf_op jit(solution)/shard_map/ppermute | solution.py:309
  54.8 11.5 %grads.1 = (f32[2048,512]{1,0:T(8,128)}, f32[512,2048]{1,0:T(8,128)}, f32[512,512]{1,0:T(8,128)}, bf16[512,512]{1,0:T(8,128)(2,1)}, bf16[1024,512]{1,0:T(8,128)(2,1)}, /*index=5*/f32[8,128]{1,0:T(8,128)}) custom-call(bf16[384,2048]{1,0:T(8,128)(2,1)} %get-tuple-element.86.refs_0_, bf16[384,512]{1,0:T(8,128)(2,1)} %get-tuple-element.87.refs_1_, ...), custom_call_target="tpu_custom_call" | custom-call | flops 2617245696 | bytes 19499008 | tf_op jit(solution)/shard_map/grads/pallas_call | solution.py:193
  66.3 0.6 collective-permute-start.7
  66.9 0.9 collective-permute-done.7.refs_4_
  67.8 1.0 %add_parts.1 = (bf16[16,48,512]{2,1,0:T(8,128)(2,1)}, f32[8,128]{1,0:T(8,128)}) custom-call(bf16[16,32,512]{2,1,0:T(8,128)(2,1)S(1)} %all-to-all-done.1.refs_0_, bf16[32,512]{1,0:T(8,128)(2,1)S(1)} %get-tuple-element.85.refs_12_.refs_1_, bf16[32,512]{1,0:T(8,128)(2,1)S(1)} %collective-permute-done.5.refs_2_, bf16[32,512]{1,0:T(8,128)(2,1)S(1)} %hand_on.4.refs_3_, ...), custom_call_target="tpu_custom_call" | custom-call | bytes 1441792 | tf_op jit(solution)/shard_map/add_parts/pallas_call | solution.py:193
  68.8 5.1 %all-to-all-start.2 = ((bf16[16,48,512]{2,1,0:T(8,128)(2,1)}), bf16[16,48,512]{2,1,0:T(8,128)(2,1)S(1)}, u32[]{:S(2)}, u32[]{:S(2)}) async-start(bf16[16,48,512]{2,1,0:T(8,128)(2,1)} %get-tuple-element.100), calls=%async_computation.2 | async-start | bytes 1572864 | tf_op jit(solution)/shard_map/all_to_all | solution.py:555
  73.9 17.5 %dense_rest.1 = (bf16[1024,512]{1,0:T(8,128)(2,1)}, f32[8,128]{1,0:T(8,128)}) custom-call(bf16[1024,512]{1,0:T(8,128)(2,1)} %bitcast.31, bf16[512,512]{1,0:T(8,128)(2,1)} %refs_1_.3, f32[1,512]{1,0:T(1,128)} %bitcast.43, bf16[1024,512]{1,0:T(8,128)(2,1)} %get-tuple-element.68.refs_1_.refs_11_.refs_3_, bf16[1024,512]{1,0:T(8,128)(2,1)} %get-tuple-element.78.refs_8_.refs_4_, ...), custom_call_target="tpu_custom_call" | custom-call | flops 8000000000 | bytes 10033152 | tf_op jit(solution)/shard_map/dense_rest/pallas_call | solution.py:193
  91.5 0.5 all-to-all-done.2.refs_0_
  92.0 0.6 fusion
  92.6 1.7 %collective-permute-done.8.refs_1_ = bf16[16,48,512]{2,1,0:T(8,128)(2,1)S(1)} collective-permute-done((bf16[16,48,512]{2,1,0:T(8,128)(2,1)S(1)}, bf16[16,48,512]{2,1,0:T(8,128)(2,1)S(1)}, u32[]{:S(2)}, u32[]{:S(2)}) %collective-permute-start.8) | collective-permute-done | bytes 786464 | tf_op jit(solution)/shard_map/ppermute | solution.py:1049
  94.2 2.7 %last_grads.1 = (f32[512,512]{1,0:T(8,128)}, f32[512,512]{1,0:T(8,128)}, f32[512,512]{1,0:T(8,128)}, f32[1,512]{1,0:T(1,128)}, f32[8,128]{1,0:T(8,128)}) custom-call(bf16[16,48,512]{2,1,0:T(8,128)(2,1)S(1)} %hand_on.5.refs_0_, bf16[16,48,512]{2,1,0:T(8,128)(2,1)S(1)} %collective-permute-done.8.refs_1_, bf16[512,512]{1,0:T(8,128)(2,1)} %get-tuple-element.102.refs_2_), custom_call_target="tpu_custom_call" | custom-call | bytes 5244928 | tf_op jit(solution)/shard_map/last_grads/pallas_call | solution.py:193
  (16 shorter events, 0.1 us)
Async XLA Ops:
  5.4 5.3 %collective-permute-start.1 = (bf16[32,1024]{1,0:T(8,128)(2,1)S(1)}, bf16[32,1024]{1,0:T(8,128)(2,1)S(1)}, u32[]{:S(2)}, u32[]{:S(2)}) collective-permute-start(bf16[32,1024]{1,0:T(8,128)(2,1)S(1)} %get-tuple-element.65.refs_0_), channel_id=1, source_target_pairs={{0,16},{16,0},{8,24},{24,8},{1,17},{17,1},{9,25},{25,9},{2,18},{18... | collective-permute-start | bytes 196616 | tf_op jit(solution)/shard_map/ppermute | solution.py:309
  8.4 2.3 %collective-permute-start = (bf16[32,1024]{1,0:T(8,128)(2,1)S(1)}, bf16[32,1024]{1,0:T(8,128)(2,1)S(1)}, u32[]{:S(2)}, u32[]{:S(2)}) collective-permute-start(bf16[32,1024]{1,0:T(8,128)(2,1)S(1)} %get-tuple-element.65.refs_0_), channel_id=1, source_target_pairs={{0,8},{8,0},{16,24},{24,16},{1,9},{9,1},{17,25},{25,17},{2,10},{10... | collective-permute-start | bytes 196616 | tf_op jit(solution)/shard_map/ppermute | solution.py:308
  10.7 1.3 %collective-permute-start.2 = (bf16[32,1024]{1,0:T(8,128)(2,1)S(1)}, bf16[32,1024]{1,0:T(8,128)(2,1)S(1)}, u32[]{:S(2)}, u32[]{:S(2)}) collective-permute-start(bf16[32,1024]{1,0:T(8,128)(2,1)S(1)} %collective-permute-done.1.refs_2_), channel_id=1, source_target_pairs={{0,8},{8,0},{16,24},{24,16},{1,9},{9,1},{17,25},{25,17},{2,10},{10... | collective-permute-start | bytes 196616 | tf_op jit(solution)/shard_map/ppermute | solution.py:312
  12.9 16.4 %all-to-all-start = ((bf16[8,24,1152]{2,1,0:T(8,128)(2,1)}), bf16[8,24,1152]{2,1,0:T(8,128)(2,1)S(1)}, u32[]{:S(2)}, u32[]{:S(2)}) async-start(bf16[8,24,1152]{2,1,0:T(8,128)(2,1)} %get-tuple-element.67), calls=%async_computation | async-start | bytes 884736 | tf_op jit(solution)/shard_map/all_to_all | solution.py:968
  29.3 3.1 %collective-permute-start.3 = (bf16[8,24,1152]{2,1,0:T(8,128)(2,1)S(1)}, bf16[8,24,1152]{2,1,0:T(8,128)(2,1)S(1)}, u32[]{:S(2)}, u32[]{:S(2)}) collective-permute-start(bf16[8,24,1152]{2,1,0:T(8,128)(2,1)S(1)} %hand_on.3.refs_4_), channel_id=1, source_target_pairs={{0,8},{8,0},{16,24},{24,16},{1,9},{9,1},{17,25},{25,17},{2,10},{10... | collective-permute-start | bytes 1327112 | tf_op jit(solution)/shard_map/ppermute | solution.py:980
  43.7 2.0 %collective-permute-start.4 = (bf16[512,512]{1,0:T(8,128)(2,1)S(1)}, bf16[512,512]{1,0:T(8,128)(2,1)S(1)}, u32[]{:S(2)}, u32[]{:S(2)}) collective-permute-start(bf16[512,512]{1,0:T(8,128)(2,1)S(1)} %get-tuple-element.83), channel_id=1, source_target_pairs={{0,8},{8,0},{16,24},{24,16},{1,9},{9,1},{17,25},{25,17},{2,10},{10... | collective-permute-start | bytes 1572872 | tf_op jit(solution)/shard_map/ppermute | solution.py:561
  46.6 21.2 %all-to-all-start.1 = ((bf16[16,32,512]{2,1,0:T(8,128)(2,1)}), bf16[16,32,512]{2,1,0:T(8,128)(2,1)S(1)}, u32[]{:S(2)}, u32[]{:S(2)}) async-start(bf16[16,32,512]{2,1,0:T(8,128)(2,1)} %bitcast.14), calls=%async_computation.1 | async-start | bytes 1048576 | tf_op jit(solution)/shard_map/all_to_all | solution.py:555
  53.4 12.9 %collective-permute-start.6 = (bf16[32,512]{1,0:T(8,128)(2,1)S(1)}, bf16[32,512]{1,0:T(8,128)(2,1)S(1)}, u32[]{:S(2)}, u32[]{:S(2)}) collective-permute-start(bf16[32,512]{1,0:T(8,128)(2,1)S(1)} %get-tuple-element.85.refs_12_.refs_1_), channel_id=1, source_target_pairs={{0,16},{16,0},{8,24},{24,8},{1,17},{17,1},{9,25},{25,9},{2,18},{18... | collective-permute-start | bytes 98312 | tf_op jit(solution)/shard_map/ppermute | solution.py:309
  54.8 12.1 %collective-permute-start.5 = (bf16[32,512]{1,0:T(8,128)(2,1)S(1)}, bf16[32,512]{1,0:T(8,128)(2,1)S(1)}, u32[]{:S(2)}, u32[]{:S(2)}) collective-permute-start(bf16[32,512]{1,0:T(8,128)(2,1)S(1)} %get-tuple-element.85.refs_12_.refs_1_), channel_id=1, source_target_pairs={{0,8},{8,0},{16,24},{24,16},{1,9},{9,1},{17,25},{25,17},{2,10},{10... | collective-permute-start | bytes 98312 | tf_op jit(solution)/shard_map/ppermute | solution.py:308
  66.3 1.4 %collective-permute-start.7 = (bf16[32,512]{1,0:T(8,128)(2,1)S(1)}, bf16[32,512]{1,0:T(8,128)(2,1)S(1)}, u32[]{:S(2)}, u32[]{:S(2)}) collective-permute-start(bf16[32,512]{1,0:T(8,128)(2,1)S(1)} %hand_on.4.refs_3_), channel_id=1, source_target_pairs={{0,8},{8,0},{16,24},{24,16},{1,9},{9,1},{17,25},{25,17},{2,10},{10... | collective-permute-start | bytes 98312 | tf_op jit(solution)/shard_map/ppermute | solution.py:312
  68.8 23.1 %all-to-all-start.2 = ((bf16[16,48,512]{2,1,0:T(8,128)(2,1)}), bf16[16,48,512]{2,1,0:T(8,128)(2,1)S(1)}, u32[]{:S(2)}, u32[]{:S(2)}) async-start(bf16[16,48,512]{2,1,0:T(8,128)(2,1)} %get-tuple-element.100), calls=%async_computation.2 | async-start | bytes 1572864 | tf_op jit(solution)/shard_map/all_to_all | solution.py:555
  73.9 18.0 %copy-start = (f32[8,512]{1,0:T(8,128)S(1)}, f32[8,512]{1,0:T(8,128)}, u32[]{:S(2)}) copy-start(f32[8,512]{1,0:T(8,128)} %get-tuple-element.107) | copy-start | bytes 49156
  92.0 2.3 %collective-permute-start.8 = (bf16[16,48,512]{2,1,0:T(8,128)(2,1)S(1)}, bf16[16,48,512]{2,1,0:T(8,128)(2,1)S(1)}, u32[]{:S(2)}, u32[]{:S(2)}) collective-permute-start(bf16[16,48,512]{2,1,0:T(8,128)(2,1)S(1)} %hand_on.5.refs_0_), channel_id=1, source_target_pairs={{0,8},{8,0},{16,24},{24,16},{1,9},{9,1},{17,25},{25,17},{2,10},{10... | collective-permute-start | bytes 2359304 | tf_op jit(solution)/shard_map/ppermute | solution.py:1049

commit v5 on v4

--- a/solution.py
+++ b/solution.py
@@ -485,12 +485,13 @@
 
 def grads_kernel(*refs):
     weights, inputs, outs = refs[:7], refs[7:17], refs[17:]
-    weights[0].ref(), weights[1].ref()
-    for ref in weights[2:] + inputs:
+    for ref in inputs + weights:
         if isinstance(ref, Fetched):
             ref.start()
-    weight_grads_kernel(*weights, *outs[:4])
+    part_rows(outs[0], weights[0], weights[1][...])
     input_grad_kernel(*inputs, outs[4])
+    outs[4].flush()
+    weight_grads_kernel(*weights[2:], *outs[1:4])
 
 
 def input_grad_kernel(
@@ -571,10 +572,8 @@
 
 
 def weight_grads_kernel(
-    active_ref, second_ref, first_ref, pre_ref, both_ref, attended_ref, slots_ref,
-    outer_ref, inner_ref, out_ref, x_ref,
+    first_ref, pre_ref, both_ref, attended_ref, slots_ref, inner_ref, out_ref, x_ref
 ):
-    part_rows(outer_ref, active_ref, second_ref[...])
     part_rows(inner_ref, first_ref, pre_ref[...])
     part_rows(out_ref, both_ref, attended_ref[...])
     width = out_ref.shape[0]

time: 97.7 us -> 96.5 us (0.988)
  Pallas kernels: 62.7 us -> 60.8 us
  starting transfers between devices: 24.5 us -> 26.2 us
    pallas_call x9, Pallas kernels: 60.2 us -> 58.3 us  [call(): pl.pallas_call(wrapped, out_shape=shapes, in_specs=spaces, out_specs=out_...]
    all_to_all x2, starting transfers between devices: 11.9 us -> 13.5 us  [exchange(): lax.all_to_all(sent, ('side', 'batch'), split_axis=0, concat_axis=0, axis...]
  transfers between devices with their start and end apart: 12 -> 12, of which waited for: 6 -> 5; matrix products, arithmetic and copies ran while one was open for 1% -> 1% of each run, Pallas kernels for 42% -> 41%
where the time goes in v5:
time: 96.5 us; the launch traced here: 96.1 us
  Pallas kernels  60.8 us (63%)
  starting transfers between devices  26.2 us (27%)
  waiting for transfers between devices  7.56 us (8%)
  between operations  0.98 us (1%)
    pallas_call x9, Pallas kernels, call(): pl.pallas_call(wrapped, out_shape=shapes, in_specs=spaces, out_specs=out_...  58.3 us
    all_to_all x2, starting transfers between devices, exchange(): lax.all_to_all(sent, ('side', 'batch'), split_axis=0, concat_axis=0, axis...  13.5 us
    all_to_all x1, starting transfers between devices, body(): lax.all_to_all(sent, 'batch', split_axis=0, concat_axis=0, axis_index_gro...  6.87 us
    ppermute x2, starting transfers between devices, near_rows(): far = lax.ppermute(own, 'side', CHIP_SWAP)  4.5 us
    pallas_call x1, Pallas kernels, fetch(): pl.pallas_call(kernel, out_shape=[pltpu.VMEM(x.shape, x.dtype) for x in a...  2.46 us
    ppermute x2, waiting for transfers between devices, near_rows(): far = lax.ppermute(own, 'side', CHIP_SWAP)  2.24 us
    ppermute x2, waiting for transfers between devices, near_rows(): return (own, other, far, lax.ppermute(far, 'side', CORE_SWAP))  2.11 us
  transfers between devices with their start and end apart: 12, of which 5 were waited for; matrix products, arithmetic and copies ran while one was open for 1% of the time, Pallas kernels for 41%

profile of v5, /device:TPU:0, one launch (start us, length us, event | category | flops | bytes accessed | tf_op | source)
XLA Modules:
  0.0 96.1 jit_solution(11394626753564757081)
XLA Ops:
  0.7 4.7 %cls_forward.1 = (bf16[32,1024]{1,0:T(8,128)(2,1)S(1)}, bf16[32,512]{1,0:T(8,128)(2,1)}, bf16[32,1024]{1,0:T(8,128)(2,1)}, bf16[24,128]{1,0:T(8,128)(2,1)S(1)}, ...) custom-call(bf16[1024,512]{1,0:T(8,128)(2,1)} %bitcast.28, s32[1,1,1024]{2,1,0:T(1,128)} %refs_5_.1, s32[1,32]{1,0:T(1,128)} %refs_2_.3, ...), custom_call_target="tpu_custom_call" | custom-call | flops 536870912 | bytes 3863828 | tf_op jit(solution)/shard_map/cls_forward/pallas_call | solution.py:193
  5.4 3.0 %collective-permute-start.1 = (bf16[32,1024]{1,0:T(8,128)(2,1)S(1)}, bf16[32,1024]{1,0:T(8,128)(2,1)S(1)}, u32[]{:S(2)}, u32[]{:S(2)}) collective-permute-start(bf16[32,1024]{1,0:T(8,128)(2,1)S(1)} %get-tuple-element.65.refs_0_), channel_id=1, source_target_pairs={{0,16},{16,0},{8,24},{24,8},{1,17},{17,1},{9,25},{25,9},{2,18},{18... | collective-permute-start | bytes 196616 | tf_op jit(solution)/shard_map/ppermute | solution.py:309
  8.4 2.2 %collective-permute-done.1.refs_2_ = bf16[32,1024]{1,0:T(8,128)(2,1)S(1)} collective-permute-done((bf16[32,1024]{1,0:T(8,128)(2,1)S(1)}, bf16[32,1024]{1,0:T(8,128)(2,1)S(1)}, u32[]{:S(2)}, u32[]{:S(2)}) %collective-permute-start.1) | collective-permute-done | bytes 65568 | tf_op jit(solution)/shard_map/ppermute | solution.py:309
  10.7 1.2 %collective-permute-done.2.refs_3_ = bf16[32,1024]{1,0:T(8,128)(2,1)S(1)} collective-permute-done((bf16[32,1024]{1,0:T(8,128)(2,1)S(1)}, bf16[32,1024]{1,0:T(8,128)(2,1)S(1)}, u32[]{:S(2)}, u32[]{:S(2)}) %collective-permute-start.2) | collective-permute-done | bytes 65568 | tf_op jit(solution)/shard_map/ppermute | solution.py:312
  11.9 0.9 half_rows.1
  12.9 6.9 %all-to-all-start = ((bf16[8,24,1152]{2,1,0:T(8,128)(2,1)}), bf16[8,24,1152]{2,1,0:T(8,128)(2,1)S(1)}, u32[]{:S(2)}, u32[]{:S(2)}) async-start(bf16[8,24,1152]{2,1,0:T(8,128)(2,1)} %get-tuple-element.67), calls=%async_computation | async-start | bytes 884736 | tf_op jit(solution)/shard_map/all_to_all | solution.py:967
  19.8 9.5 %first_attention.1 = (bf16[512,512]{1,0:T(8,128)(2,1)}, bf16[1024,512]{1,0:T(8,128)(2,1)}, f32[256,1024]{1,0:T(8,128)}, f32[8,2048]{1,0:T(8,128)}, f32[8,128]{1,0:T(8,128)}) custom-call(bf16[1024,512]{1,0:T(8,128)(2,1)} %bitcast.29, bf16[1024,512]{1,0:T(8,128)(2,1)} %get-tuple-element.68.refs_1_.refs_11_.refs_3_, bf16[512,512]{1,0:T(8,128)(2,1)} %refs_16_.1, ...), custom_call_target="tpu_custom_call" | custom-call | flops 6000000000 | bytes 5959680 | tf_op jit(solution)/shard_map/first_attention/pallas_call | solution.py:193
  29.3 0.1 collective-permute-start.3
  29.4 2.5 %fetch.1 = (bf16[512,512]{1,0:T(8,128)(2,1)S(1)}, f32[8,2048]{1,0:T(8,128)S(1)}, bf16[512,2048]{1,0:T(8,128)(2,1)S(1)}, bf16[2048,512]{1,0:T(8,128)(2,1)S(1)}) custom-call(bf16[512,512]{1,0:T(8,128)(2,1)} %refs_7_.4, f32[8,2048]{1,0:T(8,128)} %get-tuple-element.73.refs_1_.refs_8_, bf16[512,2048]{1,0:T(8,128)(2,1)} %refs_9_.3, bf16[2048,512]{1,0:T(8,128)(2,1)} %refs_10_.3, ...), custom_call_target="tpu_custom_call" | custom-call | tf_op jit(solution)/shard_map/fetch/pallas_call | solution.py:847
  31.8 11.4 %cls_middle.1 = (f32[512,512]{1,0:T(8,128)S(1)}, bf16[512,512]{1,0:T(8,128)(2,1)S(1)}, bf16[32,512]{1,0:T(8,128)(2,1)S(1)}, bf16[32,512]{1,0:T(8,128)(2,1)}, f32...) custom-call(bf16[192,1152]{1,0:T(8,128)(2,1)S(1)} %bitcast.26, ...), custom_call_target="tpu_custom_call" | custom-call | flops 4831838208 | bytes 17264100 | tf_op jit(solution)/shard_map/cls_middle/pallas_call | solution.py:193
  43.2 0.6 collective-permute-start.4
  43.8 1.5 %collective-permute-done.4.refs_1_ = bf16[512,512]{1,0:T(8,128)(2,1)S(1)} collective-permute-done((bf16[512,512]{1,0:T(8,128)(2,1)S(1)}, bf16[512,512]{1,0:T(8,128)(2,1)S(1)}, u32[]{:S(2)}, u32[]{:S(2)}) %collective-permute-start.4) | collective-permute-done | bytes 524320 | tf_op jit(solution)/shard_map/ppermute | solution.py:562
  45.3 0.9 chip_sum.1
  46.2 7.3 %all-to-all-start.1 = ((bf16[16,32,512]{2,1,0:T(8,128)(2,1)}), bf16[16,32,512]{2,1,0:T(8,128)(2,1)S(1)}, u32[]{:S(2)}, u32[]{:S(2)}) async-start(bf16[16,32,512]{2,1,0:T(8,128)(2,1)} %bitcast.14), calls=%async_computation.1 | async-start | bytes 1048576 | tf_op jit(solution)/shard_map/all_to_all | solution.py:556
  53.5 1.5 %collective-permute-start.6 = (bf16[32,512]{1,0:T(8,128)(2,1)S(1)}, bf16[32,512]{1,0:T(8,128)(2,1)S(1)}, u32[]{:S(2)}, u32[]{:S(2)}) collective-permute-start(bf16[32,512]{1,0:T(8,128)(2,1)S(1)} %get-tuple-element.85.refs_12_.refs_1_), channel_id=1, source_target_pairs={{0,16},{16,0},{8,24},{24,8},{1,17},{17,1},{9,25},{25,9},{2,18},{18... | collective-permute-start | bytes 98312 | tf_op jit(solution)/shard_map/ppermute | solution.py:309
  55.0 9.6 %grads.1 = (f32[2048,512]{1,0:T(8,128)}, f32[512,2048]{1,0:T(8,128)}, f32[512,512]{1,0:T(8,128)}, bf16[512,512]{1,0:T(8,128)(2,1)}, bf16[1024,512]{1,0:T(8,128)(2,1)}, /*index=5*/f32[8,128]{1,0:T(8,128)}) custom-call(bf16[384,2048]{1,0:T(8,128)(2,1)} %get-tuple-element.86.refs_0_, bf16[384,512]{1,0:T(8,128)(2,1)} %get-tuple-element.87.refs_1_, ...), custom_call_target="tpu_custom_call" | custom-call | flops 2617245696 | bytes 19499008 | tf_op jit(solution)/shard_map/grads/pallas_call | solution.py:193
  64.6 0.6 collective-permute-start.7
  65.1 0.9 collective-permute-done.7.refs_4_
  66.0 1.0 %add_parts.1 = (bf16[16,48,512]{2,1,0:T(8,128)(2,1)}, f32[8,128]{1,0:T(8,128)}) custom-call(bf16[16,32,512]{2,1,0:T(8,128)(2,1)S(1)} %all-to-all-done.1.refs_0_, bf16[32,512]{1,0:T(8,128)(2,1)S(1)} %get-tuple-element.85.refs_12_.refs_1_, bf16[32,512]{1,0:T(8,128)(2,1)S(1)} %collective-permute-done.5.refs_2_, bf16[32,512]{1,0:T(8,128)(2,1)S(1)} %hand_on.4.refs_3_, ...), custom_call_target="tpu_custom_call" | custom-call | bytes 1441792 | tf_op jit(solution)/shard_map/add_parts/pallas_call | solution.py:193
  67.0 6.2 %all-to-all-start.2 = ((bf16[16,48,512]{2,1,0:T(8,128)(2,1)}), bf16[16,48,512]{2,1,0:T(8,128)(2,1)S(1)}, u32[]{:S(2)}, u32[]{:S(2)}) async-start(bf16[16,48,512]{2,1,0:T(8,128)(2,1)} %get-tuple-element.100), calls=%async_computation.2 | async-start | bytes 1572864 | tf_op jit(solution)/shard_map/all_to_all | solution.py:556
  73.2 17.5 %dense_rest.1 = (bf16[1024,512]{1,0:T(8,128)(2,1)}, f32[8,128]{1,0:T(8,128)}) custom-call(bf16[1024,512]{1,0:T(8,128)(2,1)} %bitcast.31, bf16[512,512]{1,0:T(8,128)(2,1)} %refs_1_.3, f32[1,512]{1,0:T(1,128)} %bitcast.43, bf16[1024,512]{1,0:T(8,128)(2,1)} %get-tuple-element.68.refs_1_.refs_11_.refs_3_, bf16[1024,512]{1,0:T(8,128)(2,1)} %get-tuple-element.78.refs_8_.refs_4_, ...), custom_call_target="tpu_custom_call" | custom-call | flops 8000000000 | bytes 10033152 | tf_op jit(solution)/shard_map/dense_rest/pallas_call | solution.py:193
  90.9 0.6 fusion
  91.5 1.7 %collective-permute-done.8.refs_1_ = bf16[16,48,512]{2,1,0:T(8,128)(2,1)S(1)} collective-permute-done((bf16[16,48,512]{2,1,0:T(8,128)(2,1)S(1)}, bf16[16,48,512]{2,1,0:T(8,128)(2,1)S(1)}, u32[]{:S(2)}, u32[]{:S(2)}) %collective-permute-start.8) | collective-permute-done | bytes 786464 | tf_op jit(solution)/shard_map/ppermute | solution.py:1048
  93.2 2.7 %last_grads.1 = (f32[512,512]{1,0:T(8,128)}, f32[512,512]{1,0:T(8,128)}, f32[512,512]{1,0:T(8,128)}, f32[1,512]{1,0:T(1,128)}, f32[8,128]{1,0:T(8,128)}) custom-call(bf16[16,48,512]{2,1,0:T(8,128)(2,1)S(1)} %hand_on.5.refs_0_, bf16[16,48,512]{2,1,0:T(8,128)(2,1)S(1)} %collective-permute-done.8.refs_1_, bf16[512,512]{1,0:T(8,128)(2,1)} %get-tuple-element.102.refs_2_), custom_call_target="tpu_custom_call" | custom-call | bytes 5244928 | tf_op jit(solution)/shard_map/last_grads/pallas_call | solution.py:193
  (16 shorter events, 0.1 us)
Async XLA Ops:
  5.4 5.3 %collective-permute-start.1 = (bf16[32,1024]{1,0:T(8,128)(2,1)S(1)}, bf16[32,1024]{1,0:T(8,128)(2,1)S(1)}, u32[]{:S(2)}, u32[]{:S(2)}) collective-permute-start(bf16[32,1024]{1,0:T(8,128)(2,1)S(1)} %get-tuple-element.65.refs_0_), channel_id=1, source_target_pairs={{0,16},{16,0},{8,24},{24,8},{1,17},{17,1},{9,25},{25,9},{2,18},{18... | collective-permute-start | bytes 196616 | tf_op jit(solution)/shard_map/ppermute | solution.py:309
  8.4 2.3 %collective-permute-start = (bf16[32,1024]{1,0:T(8,128)(2,1)S(1)}, bf16[32,1024]{1,0:T(8,128)(2,1)S(1)}, u32[]{:S(2)}, u32[]{:S(2)}) collective-permute-start(bf16[32,1024]{1,0:T(8,128)(2,1)S(1)} %get-tuple-element.65.refs_0_), channel_id=1, source_target_pairs={{0,8},{8,0},{16,24},{24,16},{1,9},{9,1},{17,25},{25,17},{2,10},{10... | collective-permute-start | bytes 196616 | tf_op jit(solution)/shard_map/ppermute | solution.py:308
  10.7 1.3 %collective-permute-start.2 = (bf16[32,1024]{1,0:T(8,128)(2,1)S(1)}, bf16[32,1024]{1,0:T(8,128)(2,1)S(1)}, u32[]{:S(2)}, u32[]{:S(2)}) collective-permute-start(bf16[32,1024]{1,0:T(8,128)(2,1)S(1)} %collective-permute-done.1.refs_2_), channel_id=1, source_target_pairs={{0,8},{8,0},{16,24},{24,16},{1,9},{9,1},{17,25},{25,17},{2,10},{10... | collective-permute-start | bytes 196616 | tf_op jit(solution)/shard_map/ppermute | solution.py:312
  12.9 16.4 %all-to-all-start = ((bf16[8,24,1152]{2,1,0:T(8,128)(2,1)}), bf16[8,24,1152]{2,1,0:T(8,128)(2,1)S(1)}, u32[]{:S(2)}, u32[]{:S(2)}) async-start(bf16[8,24,1152]{2,1,0:T(8,128)(2,1)} %get-tuple-element.67), calls=%async_computation | async-start | bytes 884736 | tf_op jit(solution)/shard_map/all_to_all | solution.py:967
  29.3 2.5 %collective-permute-start.3 = (bf16[8,24,1152]{2,1,0:T(8,128)(2,1)S(1)}, bf16[8,24,1152]{2,1,0:T(8,128)(2,1)S(1)}, u32[]{:S(2)}, u32[]{:S(2)}) collective-permute-start(bf16[8,24,1152]{2,1,0:T(8,128)(2,1)S(1)} %hand_on.3.refs_4_), channel_id=1, source_target_pairs={{0,8},{8,0},{16,24},{24,16},{1,9},{9,1},{17,25},{25,17},{2,10},{10... | collective-permute-start | bytes 1327112 | tf_op jit(solution)/shard_map/ppermute | solution.py:979
  43.2 2.1 %collective-permute-start.4 = (bf16[512,512]{1,0:T(8,128)(2,1)S(1)}, bf16[512,512]{1,0:T(8,128)(2,1)S(1)}, u32[]{:S(2)}, u32[]{:S(2)}) collective-permute-start(bf16[512,512]{1,0:T(8,128)(2,1)S(1)} %get-tuple-element.83), channel_id=1, source_target_pairs={{0,8},{8,0},{16,24},{24,16},{1,9},{9,1},{17,25},{25,17},{2,10},{10... | collective-permute-start | bytes 1572872 | tf_op jit(solution)/shard_map/ppermute | solution.py:562
  46.2 19.8 %all-to-all-start.1 = ((bf16[16,32,512]{2,1,0:T(8,128)(2,1)}), bf16[16,32,512]{2,1,0:T(8,128)(2,1)S(1)}, u32[]{:S(2)}, u32[]{:S(2)}) async-start(bf16[16,32,512]{2,1,0:T(8,128)(2,1)} %bitcast.14), calls=%async_computation.1 | async-start | bytes 1048576 | tf_op jit(solution)/shard_map/all_to_all | solution.py:556
  53.5 11.0 %collective-permute-start.6 = (bf16[32,512]{1,0:T(8,128)(2,1)S(1)}, bf16[32,512]{1,0:T(8,128)(2,1)S(1)}, u32[]{:S(2)}, u32[]{:S(2)}) collective-permute-start(bf16[32,512]{1,0:T(8,128)(2,1)S(1)} %get-tuple-element.85.refs_12_.refs_1_), channel_id=1, source_target_pairs={{0,16},{16,0},{8,24},{24,8},{1,17},{17,1},{9,25},{25,9},{2,18},{18... | collective-permute-start | bytes 98312 | tf_op jit(solution)/shard_map/ppermute | solution.py:309
  55.0 10.1 %collective-permute-start.5 = (bf16[32,512]{1,0:T(8,128)(2,1)S(1)}, bf16[32,512]{1,0:T(8,128)(2,1)S(1)}, u32[]{:S(2)}, u32[]{:S(2)}) collective-permute-start(bf16[32,512]{1,0:T(8,128)(2,1)S(1)} %get-tuple-element.85.refs_12_.refs_1_), channel_id=1, source_target_pairs={{0,8},{8,0},{16,24},{24,16},{1,9},{9,1},{17,25},{25,17},{2,10},{10... | collective-permute-start | bytes 98312 | tf_op jit(solution)/shard_map/ppermute | solution.py:308
  64.6 1.4 %collective-permute-start.7 = (bf16[32,512]{1,0:T(8,128)(2,1)S(1)}, bf16[32,512]{1,0:T(8,128)(2,1)S(1)}, u32[]{:S(2)}, u32[]{:S(2)}) collective-permute-start(bf16[32,512]{1,0:T(8,128)(2,1)S(1)} %hand_on.4.refs_3_), channel_id=1, source_target_pairs={{0,8},{8,0},{16,24},{24,16},{1,9},{9,1},{17,25},{25,17},{2,10},{10... | collective-permute-start | bytes 98312 | tf_op jit(solution)/shard_map/ppermute | solution.py:312
  67.0 23.7 %all-to-all-start.2 = ((bf16[16,48,512]{2,1,0:T(8,128)(2,1)}), bf16[16,48,512]{2,1,0:T(8,128)(2,1)S(1)}, u32[]{:S(2)}, u32[]{:S(2)}) async-start(bf16[16,48,512]{2,1,0:T(8,128)(2,1)} %get-tuple-element.100), calls=%async_computation.2 | async-start | bytes 1572864 | tf_op jit(solution)/shard_map/all_to_all | solution.py:556
  73.2 17.6 %copy-start = (f32[8,512]{1,0:T(8,128)S(1)}, f32[8,512]{1,0:T(8,128)}, u32[]{:S(2)}) copy-start(f32[8,512]{1,0:T(8,128)} %get-tuple-element.107) | copy-start | bytes 49156
  90.8 2.4 %collective-permute-start.8 = (bf16[16,48,512]{2,1,0:T(8,128)(2,1)S(1)}, bf16[16,48,512]{2,1,0:T(8,128)(2,1)S(1)}, u32[]{:S(2)}, u32[]{:S(2)}) collective-permute-start(bf16[16,48,512]{2,1,0:T(8,128)(2,1)S(1)} %hand_on.5.refs_0_), channel_id=1, source_target_pairs={{0,8},{8,0},{16,24},{24,16},{1,9},{9,1},{17,25},{25,17},{2,10},{10... | collective-permute-start | bytes 2359304 | tf_op jit(solution)/shard_map/ppermute | solution.py:1048
